TPU v7x, 32 devices: a whole 2x2x4 slice. The times are simulated.
32 devices in a mesh: gx: 4 (over z), gy: 4 (over x, core), gz: 2 (over y).
Axes of the slice: x: 2, y: 2, z: 4, core: 2. Of those that a mesh axis runs over, the one named last changes fastest.
Arguments:
- elevation: float32 [256, 8192], P('gx', ('gy', 'gz')), may hold values from -1 to 1
- surface_potential: float32 [256, 8192], P('gx', ('gy', 'gz')), may hold values from -2 to 2
- seabed: int32 [256, 8192], P('gx', 'gy'), may hold values from 384 to 1023
- interior_potential: float32 [16, 256, 8192], P('gz', 'gx', 'gy'), may hold values from -1.5 to 1.5
Outputs:
- new_elevation: float32 [256, 8192], P('gx', ('gy', 'gz'))
- new_potential: float32 [256, 8192], P('gx', ('gy', 'gz'))
- laplace_apply: float32 [16, 256, 8192], P('gz', 'gx', 'gy')
All inputs are finite; a program needn't handle non-finite values.
Results may differ from a plain program's by a relative error of at most 0.0003.
Values sent between devices are 32-bit elements; how exact they have to be, the bound alone decides.
No kernel may reach another device: no remote copies, remote signals or barrier semaphores. Data moves between devices by JAX's collectives and lax.ppermute only.
A program may use at most 64 MiB of HBM per device.

v0:
```python
import functools

import jax
import jax.numpy as jnp
from jax import lax
from jax.experimental import pallas as pl
from jax.experimental.pallas import tpu as pltpu
from jax.sharding import PartitionSpec as P

time_step = 0.05
depth_unit = 0.015625
LANES = 128
SUBS = 8


def shift_lanes(left, cur, right, step):
    lane = lax.broadcasted_iota(jnp.int32, cur.shape, 1)
    if step < 0:
        return pltpu.roll(jnp.where(lane >= LANES + step, left, cur), -step, 1)
    return pltpu.roll(jnp.where(lane < step, right, cur), LANES - step, 1)


def square(tile, at_end):
    rest = jnp.zeros((LANES - tile.shape[0], LANES), tile.dtype)
    return jnp.concatenate([rest, tile] if at_end else [tile, rest], 0)


def first_pack(group, e, p, v, seam, outer, layer, edges, sems):
    rows, width = e.shape
    low = group[0] == 0
    source = jnp.where(low, v.shape[0] - 1, 0)
    whole = pltpu.make_async_copy(v.at[source], layer, sems.at[4])
    copies = []
    for index, (field, start) in enumerate(((e, 0), (p, 0), (e, width - LANES), (p, width - LANES))):
        into = edges.at[index // 2, (index % 2) * rows : (index % 2 + 1) * rows, :]
        copies.append(pltpu.make_async_copy(field.at[:, start : start + LANES], into, sems.at[index]))
    for copy in copies:
        copy.start()
    whole.start()
    for copy in copies:
        copy.wait()
    left = edges[0].T[:SUBS]
    right = edges[1].T[LANES - SUBS :]
    seam[...] = jnp.where(low, right, left)
    outer[...] = jnp.where(low, left, right)
    whole.wait()


def lazy_pack(v_top, v_bottom, v_left, v_right, s_top, s_bottom, s_left, s_right, up, down, to_right, to_left):
    layers, _, width = v_top.shape
    piece = width // SUBS
    for k in range(layers):
        up[k : k + 1, :width] = v_bottom[k, SUBS - 1 : SUBS, :]
        down[k : k + 1, :width] = v_top[k, 0:1, :]
    for q in range(SUBS):
        part = slice(q * piece, (q + 1) * piece)
        up[q : q + 1, width:] = s_bottom[SUBS - 1 : SUBS, part].astype(jnp.float32) * depth_unit
        down[q : q + 1, width:] = s_top[0:1, part].astype(jnp.float32) * depth_unit
    to_right[...] = jnp.zeros_like(to_right)
    to_left[...] = jnp.zeros_like(to_left)
    for j in range(layers // 2):
        both = jnp.concatenate([v_right[2 * j], v_right[2 * j + 1]], 0).T
        to_right[j : j + 1, :] = both[LANES - 1 :]
        both = jnp.concatenate([v_left[2 * j], v_left[2 * j + 1]], 0).T
        to_left[j : j + 1, :] = both[:1]
    j = layers // 2
    both = jnp.concatenate([s_right[...], s_right[...]], 0).astype(jnp.float32) * depth_unit
    to_right[j : j + 1, :] = both.T[LANES - 1 :]
    both = jnp.concatenate([s_left[...], s_left[...]], 0).astype(jnp.float32) * depth_unit
    to_left[j : j + 1, :] = both.T[:1]


def side_blocks(low, seam, outer):
    left = square(jnp.where(low, outer, seam), True).T
    right = square(jnp.where(low, seam, outer), False).T
    return left, right


def row_pack(group, e_top, e_bottom, p_top, p_bottom, seam, outer, up, down):
    left, right = side_blocks(group[0] == 0, seam[...], outer[...])
    rows = LANES // 2
    width = e_top.shape[1]
    for row, tops, bottoms in ((0, e_top, e_bottom), (SUBS, p_top, p_bottom)):
        base = 0 if row == 0 else rows
        up[row : row + SUBS, :LANES] = left[base + rows - SUBS : base + rows]
        up[row : row + SUBS, LANES : LANES + width] = bottoms[...]
        up[row : row + SUBS, LANES + width :] = right[base + rows - SUBS : base + rows]
        down[row : row + SUBS, :LANES] = left[base : base + SUBS]
        down[row : row + SUBS, LANES : LANES + width] = tops[...]
        down[row : row + SUBS, LANES + width :] = right[base : base + SUBS]


def neighbourhood(ref, lane_tile, row):
    last = ref.shape[0] - 1
    at = lambda column, step: ref[column, pl.ds(row + step, SUBS), :]
    cur = at(lane_tile, 0)
    left, right = at(max(lane_tile - 1, 0), 0), at(min(lane_tile + 1, last), 0)
    rows = [at(lane_tile, step) for step in (-2, -1, 1, 2)]
    lanes = [shift_lanes(left, cur, right, step) for step in (-2, -1, 1, 2)]
    return cur, rows, lanes


def slope(values):
    return (2.0 / 3.0) * (values[2] - values[1]) - (1.0 / 12.0) * (values[3] - values[0])


def tile_rates(e_near, p_near):
    e, e_rows, e_lanes = e_near
    p, p_rows, p_lanes = p_near
    p_x, p_y = slope(p_rows), slope(p_lanes)
    near = (p_rows[1] + p_rows[2]) + (p_lanes[1] + p_lanes[2])
    far = (p_rows[0] + p_rows[3]) + (p_lanes[0] + p_lanes[3])
    bend = (4.0 / 3.0) * near - (1.0 / 12.0) * far - 5.0 * p
    rate_e = bend - (slope(e_rows) * p_x + slope(e_lanes) * p_y)
    rate_p = 0.5 * (p_x * p_x + p_y * p_y) + e
    return e, p, time_step * rate_e, -time_step * rate_p


def surface(
    group, e, p, seam, outer, north, south,
    new_e, new_p, height, wide_e, wide_p, e0, p0, e1, p1,
):
    rows, width = e.shape
    low = group[0] == 0
    left, right = side_blocks(low, seam[...], outer[...])
    tiles = width // LANES + 2
    inner = slice(SUBS, SUBS + rows)
    for old, source, base in ((e0, e, 0), (p0, p, LANES // 2)):
        half = SUBS if base else 0
        for t in range(tiles):
            part = slice(t * LANES, (t + 1) * LANES)
            old[t, :SUBS, :] = north[half : half + SUBS, part]
            old[t, SUBS + rows : 2 * SUBS + rows, :] = south[half : half + SUBS, part]
            if 0 < t < tiles - 1:
                old[t, inner, :] = source[:, (t - 1) * LANES : t * LANES]
        old[0, inner, :] = left[base : base + rows]
        old[tiles - 1, inner, :] = right[base : base + rows]
    blocks = rows // SUBS + 1

    def first(block, carry):
        row = block * SUBS + SUBS - 3
        for t in range(tiles):
            old_e, old_p, step_e, step_p = tile_rates(neighbourhood(e0, t, row), neighbourhood(p0, t, row))
            e1[t, pl.ds(row, SUBS), :] = old_e + step_e
            p1[t, pl.ds(row, SUBS), :] = old_p + step_p
        return carry

    lax.fori_loop(0, blocks, first, 0)

    def second(block, carry):
        row = block * SUBS + SUBS - 1
        for t in range(tiles):
            one_e, one_p, step_e, step_p = tile_rates(neighbourhood(e1, t, row), neighbourhood(p1, t, row))
            old_e = e0[t, pl.ds(row, SUBS), :]
            old_p = p0[t, pl.ds(row, SUBS), :]
            wide_e[t, pl.ds(row, SUBS), :] = 0.5 * ((old_e + one_e) + step_e)
            wide_p[t, pl.ds(row, SUBS), :] = 0.5 * ((old_p + one_p) + step_p)
        return carry

    lax.fori_loop(0, blocks, second, 0)
    for t in range(1, tiles - 1):
        part = slice((t - 1) * LANES, t * LANES)
        tile_e = wide_e[t, inner, :]
        new_e[:, part] = tile_e
        height[:rows, part] = tile_e
        new_p[:, part] = wide_p[t, inner, :]
        for row, wide in ((0, wide_e), (2, wide_p)):
            height[rows + row : rows + row + 1, part] = wide[t, SUBS - 1 : SUBS, :]
            height[rows + row + 1 : rows + row + 2, part] = wide[t, SUBS + rows : SUBS + rows + 1, :]
        height[rows + 4 :, part] = jnp.zeros((4, LANES), jnp.float32)
    left = jnp.concatenate([wide_e[0, inner, :], wide_p[0, inner, :]], 0).T[LANES - 1 :]
    right = jnp.concatenate([wide_e[tiles - 1, inner, :], wide_p[tiles - 1, inner, :]], 0).T[:1]
    height[rows + 4 : rows + 5, :LANES] = jnp.where(low, left, right)


def rim_pack(group, far_north, far_south, x_left, x_right, rims):
    low = group[0] == 0
    layers = far_north.shape[0]
    width = rims.shape[1]
    pairs = layers // 2
    rims[...] = jnp.zeros_like(rims)
    for row, side in ((0, far_north), (2, far_south)):
        for half in range(2):
            part = slice(half * width, (half + 1) * width)
            rims[row + half : row + half + 1, :] = jnp.where(low, side[layers - 1 : layers, part], side[0:1, part])
    for lane, side in ((0, x_left), (LANES, x_right)):
        top_pair = pltpu.roll(side[...], LANES // 2, 1)[pairs - 1 : pairs]
        rims[4:5, lane : lane + LANES] = jnp.where(low, top_pair, side[0:1, :])


def prepare(v, sea, far_north, far_south, x_left, x_right, volume, depth, sems):
    layers, rows, tile = v.shape
    tiles = tile // LANES
    inner = slice(SUBS, SUBS + rows)
    copies = []
    for t in range(tiles):
        copies.append(
            pltpu.make_async_copy(
                v.at[:, :, t * LANES : (t + 1) * LANES], volume.at[:, t + 1, inner, :], sems.at[t]
            )
        )
        copies[-1].start()
    left = square(x_left[...], False).T
    right = square(x_right[...], False).T
    half, pairs = LANES // 2, layers // 2
    for k in range(layers):
        base = (k % 2) * half
        volume[k, 0, inner, :] = pltpu.roll(left, LANES - 1 - k // 2, 1)[base : base + rows]
        volume[k, tiles + 1, inner, :] = pltpu.roll(right, (LANES - k // 2) % LANES, 1)[base : base + rows]
        for t in range(tiles):
            part = slice(t * LANES, (t + 1) * LANES)
            volume[k, t + 1, SUBS - 1 : SUBS, :] = far_north[k : k + 1, part]
            volume[k, t + 1, SUBS + rows : SUBS + rows + 1, :] = far_south[k : k + 1, part]
    depth[0, inner, :] = pltpu.roll(left, LANES - 1 - pairs, 1)[:rows]
    depth[tiles + 1, inner, :] = pltpu.roll(right, LANES - pairs, 1)[:rows]
    piece = tile // SUBS // LANES
    for t in range(tiles):
        part = slice(t * LANES, (t + 1) * LANES)
        depth[t + 1, inner, :] = sea[:, part].astype(jnp.float32) * depth_unit
        q, start = t // piece, tile + (t % piece) * LANES
        depth[t + 1, SUBS - 1 : SUBS, :] = far_north[q : q + 1, start : start + LANES]
        depth[t + 1, SUBS + rows : SUBS + rows + 1, :] = far_south[q : q + 1, start : start + LANES]
    for copy in copies:
        copy.wait()


def laplace(
    total_layers, group_ref, volume, depth, far_layer, rims, wide_e, wide_p, height,
    out, part, coefficients, column, ghost,
):
    block = pl.program_id(0)
    group = group_ref[0]
    low = group == 0
    layers = volume.shape[0]
    rows, tile = far_layer.shape
    width = tile // 2
    tiles, halves = tile // LANES, width // LANES
    inner = slice(SUBS, SUBS + rows)

    @pl.when(block == 0)
    def _():
        far_left = pltpu.roll(square(rims[:, :LANES], False).T, LANES - 5, 1)[:rows]
        far_right = pltpu.roll(square(rims[:, LANES : 2 * LANES], False).T, LANES - 4, 1)[:rows]
        ghost[0, inner, :] = far_left
        ghost[tiles + 1, inner, :] = far_right
        for t in range(tiles):
            ghost[t + 1, inner, :] = far_layer[:, t * LANES : (t + 1) * LANES]
            half, spot = t // halves, slice((t % halves) * LANES, (t % halves + 1) * LANES)
            ghost[t + 1, SUBS - 1 : SUBS, :] = rims[half : half + 1, spot]
            ghost[t + 1, SUBS + rows : SUBS + rows + 1, :] = rims[2 + half : 3 + half, spot]
        own = group * halves + 1
        other = (1 - group) * halves + 1
        for t in range(halves):
            spot = slice(t * LANES, (t + 1) * LANES)
            column[own + t, : rows + 2 * SUBS, :] = wide_e[t + 1, : rows + 2 * SUBS, :] + depth[own + t]
            column[other + t, inner, :] = height[:rows, spot] + depth[other + t, inner, :]
            for row, at in ((SUBS - 1, rows), (SUBS + rows, rows + 1)):
                column[other + t, row : row + 1, :] = height[at : at + 1, spot] + depth[other + t, row : row + 1, :]
        own_side = group * (tiles + 1)
        other_side = (1 - group) * (tiles + 1)
        edge = jnp.where(low, wide_e[0, inner, :], wide_e[halves + 1, inner, :])
        column[own_side, inner, :] = edge + depth[own_side, inner, :]
        edge = square(height[rows:, :LANES], False).T[:rows]
        edge = jnp.where(low, pltpu.roll(edge, LANES - 4, 1), pltpu.roll(edge, LANES - 5, 1))
        column[other_side, inner, :] = edge + depth[other_side, inner, :]

    spacing = 1.0 / total_layers
    sigma = (group * layers).astype(jnp.float32) * spacing + 0.5 * spacing
    sign = (1 - 2 * group).astype(jnp.float32)
    gain = (2 * group).astype(jnp.float32)
    here = pl.multiple_of((block + 1) * SUBS, SUBS)

    def near(ref, t):
        at = lambda column, step: ref[column, pl.ds(here + step, SUBS), :]
        cur = at(t, 0)
        left, right = at(t - 1, 0), at(t + 1, 0)
        return cur, at(t, -1), at(t, 1), shift_lanes(left, cur, right, -1), shift_lanes(left, cur, right, 1)

    def differences(ref, t):
        p, up, down, left, right = near(ref, t)
        return p, down - up, right - left

    def chunk(t, mine):
        c, c_up, c_down, c_left, c_right = near(column, t)
        _, d_x, d_y = differences(depth, t)
        inverse = 1.0 / c
        scale = (0.25 / spacing) * inverse
        bx, by = scale * (c_down - c_up), scale * (c_right - c_left)
        ux, uy = scale * d_x - sigma * bx, scale * d_y - sigma * by
        bx, by = spacing * bx, spacing * by
        scaled = inverse * (1.0 / spacing)
        weight = 4.0 * (ux * ux + uy * uy) + scaled * scaled
        bend = 4.0 * (bx * bx + by * by)
        step = bend - 8.0 * (ux * bx + uy * by)
        bend = bend + bend

        def level(k):
            p, up, down, left, right = near(volume.at[k], t)
            return p, down - up, right - left, ((down + up) + (right + left)) - 4.0 * p

        far = differences(ghost, t)
        this = level(0)
        lower = [jnp.where(low, a, b) for a, b in zip(this, far)]
        rise_below = this[0] - lower[0]
        spot = pl.ds(pl.multiple_of((t - 1) * LANES, LANES), LANES)
        for k in range(layers):
            if k < layers - 1:
                upper = level(k + 1)
            else:
                upper = [jnp.where(low, a, -b) for a, b in zip(far, this)]
                if mine is not None:
                    upper = [a + gain * b for a, b in zip(upper, differences(wide_p, mine))]
            rise = upper[0] - this[0]
            value = this[3] + ux * (upper[1] - lower[1]) + uy * (upper[2] - lower[2])
            value = value + weight * (rise - rise_below)
            out[k, :, spot] = value
            if k < layers - 1:
                ux, uy = ux - bx, uy - by
                weight, step = weight + step, step + bend
            elif mine is None:
                local = pl.ds(pl.multiple_of((t - 1 - (1 - group) * halves) * LANES, LANES), LANES)
                part[:, local] = value
                coefficients[0, :, local] = ux
                coefficients[1, :, local] = uy
                coefficients[2, :, local] = weight
            lower, this, rise_below = this, upper, rise

    def own_pair(index, carry):
        for inside in range(2):
            mine = index * 2 + inside + 1
            chunk(group * halves + mine, mine)
        return carry

    def other_pair(index, carry):
        for inside in range(2):
            chunk((1 - group) * halves + index * 2 + inside + 1, None)
        return carry

    lax.fori_loop(0, halves // 2, own_pair, 0)
    lax.fori_loop(0, halves // 2, other_pair, 0)


def top(group_ref, before, part, coefficients, height, wide_p, other_p, out, potential):
    del before
    low = group_ref[0] == 0
    rows, width = other_p.shape
    halves = width // LANES
    inner = slice(SUBS, SUBS + rows)
    edge = square(height[rows:, :LANES], False).T[LANES // 2 : LANES // 2 + rows]
    potential[0, inner, :] = pltpu.roll(edge, LANES - 5, 1)
    potential[halves + 1, inner, :] = wide_p[1, inner, :]
    for t in range(halves):
        spot = slice(t * LANES, (t + 1) * LANES)
        potential[t + 1, inner, :] = other_p[:, spot]
        potential[t + 1, SUBS - 1 : SUBS, :] = height[rows + 2 : rows + 3, spot]
        potential[t + 1, SUBS + rows : SUBS + rows + 1, :] = height[rows + 3 : rows + 4, spot]

    def body(block, carry):
        here = pl.multiple_of((block + 1) * SUBS, SUBS)
        to = pl.ds(pl.multiple_of(block * SUBS, SUBS), SUBS)
        for t in range(1, halves + 1):
            at = lambda column, step: potential[column, pl.ds(here + step, SUBS), :]
            cur, left, right = at(t, 0), at(t - 1, 0), at(t + 1, 0)
            east = shift_lanes(left, cur, right, 1) - shift_lanes(left, cur, right, -1)
            spot = slice((t - 1) * LANES, t * LANES)
            value = coefficients[0, to, spot] * (at(t, 1) - at(t, -1)) + coefficients[1, to, spot] * east
            value = value + coefficients[2, to, spot] * cur
            partial = part[to, spot]
            out[0, to, spot] = jnp.where(low, partial, partial + 2.0 * value)
        return carry

    lax.fori_loop(0, rows // SUBS, body, 0)


def ring(axis, step):
    count = lax.axis_size(axis)
    return [(i, (i + step) % count) for i in range(count)]


def shards(elevation, surface_potential, seabed, interior_potential):
    rows, width = elevation.shape
    layers, _, tile = interior_potential.shape
    assert 2 * rows == LANES and tile == 2 * width and layers == SUBS
    assert lax.axis_size("gz") == 2
    total_layers = layers * lax.axis_size("gz")
    f32 = jnp.float32
    shape = lambda *dims: jax.ShapeDtypeStruct(dims, f32)
    whole = lambda *dims: pl.BlockSpec(dims, lambda *_: (0,) * len(dims))
    group = lax.axis_index("gz").astype(jnp.int32).reshape((1,))
    scalar = pl.BlockSpec(memory_space=pltpu.SMEM)
    last_row, last_tile = rows // SUBS - 1, tile // LANES - 1

    def block(dims, *index):
        return pl.BlockSpec(dims, lambda *_: index)

    params = pltpu.CompilerParams(vmem_limit_bytes=24 * 1024 * 1024)
    vmem = pl.BlockSpec(memory_space=pltpu.VMEM)
    hbm = pl.BlockSpec(memory_space=pltpu.HBM)
    seam, outer, layer = pl.pallas_call(
        first_pack,
        out_shape=(shape(SUBS, LANES), shape(SUBS, LANES), shape(rows, tile)),
        in_specs=[scalar, hbm, hbm, hbm],
        out_specs=[vmem] * 3,
        scratch_shapes=[pltpu.VMEM((2, LANES, LANES), f32), pltpu.SemaphoreType.DMA((5,))],
        compiler_params=params,
        name="first_pack",
    )(group, *(pltpu.with_memory_space_constraint(x, pltpu.HBM) for x in (elevation, surface_potential, interior_potential)))

    flat = ("gy", "gz")
    count = lax.axis_size("gy")
    partner = [(2 * i + g, 2 * i + 1 - g) for i in range(count) for g in range(2)]
    across = [(2 * i + 1, (2 * i + 2) % (2 * count)) for i in range(count)]
    across = across + [(b, a) for a, b in across]
    seam = lax.ppermute(seam, flat, partner)
    far_layer = lax.ppermute(layer, flat, partner)
    outer = lax.ppermute(outer, flat, across)

    up, down, to_right, to_left = pl.pallas_call(
        lazy_pack,
        out_shape=(shape(SUBS, tile + tile // SUBS),) * 2 + (shape(SUBS, LANES),) * 2,
        grid=(1,),
        in_specs=[
            block((layers, SUBS, tile), 0, 0, 0),
            block((layers, SUBS, tile), 0, last_row, 0),
            block((layers, rows, LANES), 0, 0, 0),
            block((layers, rows, LANES), 0, 0, last_tile),
            block((SUBS, tile), 0, 0),
            block((SUBS, tile), last_row, 0),
            block((rows, LANES), 0, 0),
            block((rows, LANES), 0, last_tile),
        ],
        out_specs=[whole(SUBS, tile + tile // SUBS)] * 2 + [whole(SUBS, LANES)] * 2,
        compiler_params=params,
        name="lazy_pack",
    )(*(interior_potential,) * 4, *(seabed,) * 4)

    wide = width + 2 * LANES
    row_up, row_down = pl.pallas_call(
        row_pack,
        out_shape=(shape(2 * SUBS, wide),) * 2,
        grid=(1,),
        in_specs=[
            scalar,
            block((SUBS, width), 0, 0),
            block((SUBS, width), last_row, 0),
            block((SUBS, width), 0, 0),
            block((SUBS, width), last_row, 0),
            whole(SUBS, LANES),
            whole(SUBS, LANES),
        ],
        out_specs=[whole(2 * SUBS, wide)] * 2,
        compiler_params=params,
        name="row_pack",
    )(group, elevation, elevation, surface_potential, surface_potential, seam, outer)
    north = lax.ppermute(row_up, "gx", ring("gx", 1))
    south = lax.ppermute(row_down, "gx", ring("gx", -1))

    deep = rows + 3 * SUBS
    padded = (width // LANES + 2, deep, LANES)
    new_e, new_p, height, wide_e, wide_p = pl.pallas_call(
        surface,
        out_shape=(shape(rows, width),) * 2 + (shape(rows + SUBS, width),) + (shape(*padded),) * 2,
        in_specs=[scalar] + [vmem] * 6,
        out_specs=[vmem] * 5,
        scratch_shapes=[pltpu.VMEM(padded, f32)] * 4,
        compiler_params=params,
        name="surface",
    )(group, elevation, surface_potential, seam, outer, north, south)
    far_height = lax.ppermute(height, flat, partner)
    far_north = lax.ppermute(up, "gx", ring("gx", 1))
    far_south = lax.ppermute(down, "gx", ring("gx", -1))
    x_left = lax.ppermute(to_right, "gy", ring("gy", 1))
    x_right = lax.ppermute(to_left, "gy", ring("gy", -1))
    rims = pl.pallas_call(
        rim_pack,
        out_shape=shape(SUBS, width),
        in_specs=[scalar] + [vmem] * 4,
        out_specs=vmem,
        compiler_params=params,
        name="rim_pack",
    )(group, far_north, far_south, x_left, x_right)
    far_rims = lax.ppermute(rims, flat, partner)
    other_p = lax.ppermute(new_p, flat, partner)

    blocks = rows // SUBS
    tiles = tile // LANES
    tall = rows + 2 * SUBS
    volume, depth = pl.pallas_call(
        prepare,
        out_shape=(shape(layers, tiles + 2, tall, LANES), shape(tiles + 2, tall, LANES)),
        in_specs=[hbm] + [vmem] * 5,
        out_specs=[vmem] * 2,
        scratch_shapes=[pltpu.SemaphoreType.DMA((tiles,))],
        compiler_params=params,
        name="prepare",
    )(pltpu.with_memory_space_constraint(interior_potential, pltpu.HBM), seabed, far_north, far_south, x_left, x_right)
    partial, part, coefficients = pl.pallas_call(
        functools.partial(laplace, total_layers),
        out_shape=(shape(layers, rows, tile), shape(rows, width), shape(3, rows, width)),
        grid=(blocks,),
        in_specs=[scalar] + [vmem] * 7,
        out_specs=[
            pl.BlockSpec((layers, SUBS, tile), lambda i: (0, i, 0)),
            pl.BlockSpec((SUBS, width), lambda i: (i, 0)),
            pl.BlockSpec((3, SUBS, width), lambda i: (0, i, 0)),
        ],
        scratch_shapes=[pltpu.VMEM((tiles + 2, tall, LANES), f32)] * 2,
        compiler_params=params,
        name="laplace",
    )(group, volume, depth, far_layer, far_rims, wide_e, wide_p, far_height)
    result = pl.pallas_call(
        top,
        out_shape=shape(layers, rows, tile),
        grid_spec=pltpu.PrefetchScalarGridSpec(
            num_scalar_prefetch=1,
            grid=(1,),
            in_specs=[hbm] + [vmem] * 5,
            out_specs=pl.BlockSpec((1, rows, width), lambda i, g: (layers - 1, 0, 1 - g[0])),
            scratch_shapes=[pltpu.VMEM((width // LANES + 2, tall, LANES), f32)],
        ),
        input_output_aliases={1: 0},
        compiler_params=params,
        name="top",
    )(group, partial, part, coefficients, far_height, wide_p, other_p)
    return new_e, new_p, result


def solution(mesh):
    return jax.shard_map(
        shards,
        mesh=mesh,
        in_specs=(P("gx", ("gy", "gz")), P("gx", ("gy", "gz")), P("gx", "gy"), P("gz", "gx", "gy")),
        out_specs=(P("gx", ("gy", "gz")), P("gx", ("gy", "gz")), P("gz", "gx", "gy")),
        check_vma=False,
    )
```

profile of v0, /device:TPU:0, one launch (start us, length us, event | category | flops | bytes accessed | tf_op | source)
XLA Modules:
  0.0 56.5 jit_solution(11590076356668583475)
XLA Ops:
  0.7 1.3 %first_pack.1 = (f32[8,128]{1,0:T(8,128)S(1)}, f32[8,128]{1,0:T(8,128)S(1)}, f32[64,2048]{1,0:T(8,128)S(1)}) custom-call(s32[1]{0:T(128)} %bitcast.group.group_ref, f32[64,1024]{1,0:T(8,128)} %e.3, f32[64,1024]{1,0:T(8,128)} %p.3, f32[8,64,2048]{2,1,0:T(8,128)} %v.3), custom_call_target="tpu_custom_call" | custom-call | tf_op jit(solution)/shard_map/first_pack/pallas_call | solution.py:399
  2.0 3.1 %collective-permute-start.8 = (f32[64,2048]{1,0:T(8,128)S(1)}, f32[64,2048]{1,0:T(8,128)S(1)}, u32[]{:S(2)}, u32[]{:S(2)}) collective-permute-start(f32[64,2048]{1,0:T(8,128)S(1)} %get-tuple-element.34), channel_id=1, source_target_pairs={{0,1},{1,0},{2,3},{3,2},{4,5},{5,4},{6,7},{7,6},{8,9},{9,8},{10,11... | collective-permute-start | bytes 1572872 | tf_op jit(solution)/shard_map/ppermute | solution.py:415
  5.0 0.1 collective-permute-start
  5.1 1.8 %collective-permute-start.1 = (f32[8,128]{1,0:T(8,128)S(1)}, f32[8,128]{1,0:T(8,128)S(1)}, u32[]{:S(2)}, u32[]{:S(2)}) collective-permute-start(f32[8,128]{1,0:T(8,128)S(1)} %get-tuple-element.23), channel_id=1, source_target_pairs={{1,2},{3,4},{5,6},{7,0},{2,1},{4,3},{6,5},{0,7},{9,10},{11,12},{13... | collective-permute-start | bytes 12296 | tf_op jit(solution)/shard_map/ppermute | solution.py:416
  6.9 10.2 %collective-permute-done.seam = f32[8,128]{1,0:T(8,128)S(1)} collective-permute-done((f32[8,128]{1,0:T(8,128)S(1)}, f32[8,128]{1,0:T(8,128)S(1)}, u32[]{:S(2)}, u32[]{:S(2)}) %collective-permute-start) | collective-permute-done | bytes 4128 | tf_op jit(solution)/shard_map/ppermute | solution.py:414
  17.1 0.1 row_pack.1
  17.2 1.8 %collective-permute-start.2 = (f32[16,1280]{1,0:T(8,128)S(1)}, f32[16,1280]{1,0:T(8,128)S(1)}, u32[]{:S(2)}, u32[]{:S(2)}) collective-permute-start(f32[16,1280]{1,0:T(8,128)S(1)} %get-tuple-element.24), channel_id=1, source_target_pairs={{0,8},{8,16},{16,24},{24,0},{1,9},{9,17},{17,25},{25,1},{2,10},{10... | collective-permute-start | bytes 245768 | tf_op jit(solution)/shard_map/ppermute | solution.py:455
  19.1 2.1 %collective-permute-start.3 = (f32[16,1280]{1,0:T(8,128)S(1)}, f32[16,1280]{1,0:T(8,128)S(1)}, u32[]{:S(2)}, u32[]{:S(2)}) collective-permute-start(f32[16,1280]{1,0:T(8,128)S(1)} %get-tuple-element.25), channel_id=1, source_target_pairs={{0,24},{8,0},{16,8},{24,16},{1,25},{9,1},{17,9},{25,17},{2,26},{10... | collective-permute-start | bytes 245768 | tf_op jit(solution)/shard_map/ppermute | solution.py:456
  21.2 2.9 %collective-permute-done.2.north = f32[16,1280]{1,0:T(8,128)S(1)} collective-permute-done((f32[16,1280]{1,0:T(8,128)S(1)}, f32[16,1280]{1,0:T(8,128)S(1)}, u32[]{:S(2)}, u32[]{:S(2)}) %collective-permute-start.2) | collective-permute-done | bytes 81952 | tf_op jit(solution)/shard_map/ppermute | solution.py:455
  24.1 0.9 %collective-permute-done.3.south = f32[16,1280]{1,0:T(8,128)S(1)} collective-permute-done((f32[16,1280]{1,0:T(8,128)S(1)}, f32[16,1280]{1,0:T(8,128)S(1)}, u32[]{:S(2)}, u32[]{:S(2)}) %collective-permute-start.3) | collective-permute-done | bytes 81952 | tf_op jit(solution)/shard_map/ppermute | solution.py:456
  25.0 3.9 %surface.1 = (f32[64,1024]{1,0:T(8,128)}, f32[64,1024]{1,0:T(8,128)}, f32[72,1024]{1,0:T(8,128)S(1)}, f32[10,88,128]{2,1,0:T(8,128)S(1)}, f32[10,88,128]{2,1,0:T(8,128)S(1)}) custom-call(s32[1]{0:T(128)} %bitcast.group.group_ref, f32[64,1024]{1,0:T(8,128)S(1)} %copy-done.2, f32[64,1024]{1,0:T(8,128)S(1)} %copy-done.3, ...), custom_call_target="tpu_custom_call" | custom-call | tf_op jit(solution)/shard_map/surface/pallas_call | solution.py:460
  28.9 1.0 %collective-permute-start.10 = (f32[72,1024]{1,0:T(8,128)S(1)}, f32[72,1024]{1,0:T(8,128)S(1)}, u32[]{:S(2)}, u32[]{:S(2)}) collective-permute-start(f32[72,1024]{1,0:T(8,128)S(1)} %get-tuple-element.37), channel_id=1, source_target_pairs={{0,1},{1,0},{2,3},{3,2},{4,5},{5,4},{6,7},{7,6},{8,9},{9,8},{10,11... | collective-permute-start | bytes 884744 | tf_op jit(solution)/shard_map/ppermute | solution.py:469
  29.9 1.1 %collective-permute-start.11 = (f32[64,1024]{1,0:T(8,128)}, f32[64,1024]{1,0:T(8,128)S(1)}, u32[]{:S(2)}, u32[]{:S(2)}) collective-permute-start(f32[64,1024]{1,0:T(8,128)} %get-tuple-element.20), channel_id=1, source_target_pairs={{0,1},{1,0},{2,3},{3,2},{4,5},{5,4},{6,7},{7,6},{8,9},{9,8},{10,11... | collective-permute-start | bytes 786440 | tf_op jit(solution)/shard_map/ppermute | solution.py:483
  30.9 0.2 lazy_pack.1
  31.2 1.7 %collective-permute-start.7 = (f32[8,128]{1,0:T(8,128)S(1)}, f32[8,128]{1,0:T(8,128)S(1)}, u32[]{:S(2)}, u32[]{:S(2)}) collective-permute-start(f32[8,128]{1,0:T(8,128)S(1)} %get-tuple-element.31), channel_id=1, source_target_pairs={{0,6},{2,0},{4,2},{6,4},{1,7},{3,1},{5,3},{7,5},{8,14},{10,8},{12,... | collective-permute-start | bytes 12296 | tf_op jit(solution)/shard_map/ppermute | solution.py:473
  33.0 1.3 %collective-permute-done.6.x_left = f32[8,128]{1,0:T(8,128)S(1)} collective-permute-done((f32[8,128]{1,0:T(8,128)S(1)}, f32[8,128]{1,0:T(8,128)S(1)}, u32[]{:S(2)}, u32[]{:S(2)}) %collective-permute-start.6) | collective-permute-done | bytes 4128 | tf_op jit(solution)/shard_map/ppermute | solution.py:472
  34.3 1.1 %collective-permute-start.4 = (f32[8,2304]{1,0:T(8,128)S(1)}, f32[8,2304]{1,0:T(8,128)S(1)}, u32[]{:S(2)}, u32[]{:S(2)}) collective-permute-start(f32[8,2304]{1,0:T(8,128)S(1)} %get-tuple-element.28), channel_id=1, source_target_pairs={{0,8},{8,16},{16,24},{24,0},{1,9},{9,17},{17,25},{25,1},{2,10},{10... | collective-permute-start | bytes 221192 | tf_op jit(solution)/shard_map/ppermute | solution.py:470
  35.4 2.7 %collective-permute-start.5 = (f32[8,2304]{1,0:T(8,128)S(1)}, f32[8,2304]{1,0:T(8,128)S(1)}, u32[]{:S(2)}, u32[]{:S(2)}) collective-permute-start(f32[8,2304]{1,0:T(8,128)S(1)} %get-tuple-element.29), channel_id=1, source_target_pairs={{0,24},{8,0},{16,8},{24,16},{1,25},{9,1},{17,9},{25,17},{2,26},{10... | collective-permute-start | bytes 221192 | tf_op jit(solution)/shard_map/ppermute | solution.py:471
  38.1 3.2 %collective-permute-done.4.far_north = f32[8,2304]{1,0:T(8,128)S(1)} collective-permute-done((f32[8,2304]{1,0:T(8,128)S(1)}, f32[8,2304]{1,0:T(8,128)S(1)}, u32[]{:S(2)}, u32[]{:S(2)}) %collective-permute-start.4) | collective-permute-done | bytes 73760 | tf_op jit(solution)/shard_map/ppermute | solution.py:470
  41.3 0.8 %collective-permute-start.9 = (f32[8,1024]{1,0:T(8,128)S(1)}, f32[8,1024]{1,0:T(8,128)S(1)}, u32[]{:S(2)}, u32[]{:S(2)}) collective-permute-start(f32[8,1024]{1,0:T(8,128)S(1)} %rim_pack.1), channel_id=1, source_target_pairs={{0,1},{1,0},{2,3},{3,2},{4,5},{5,4},{6,7},{7,6},{8,9},{9,8},{10,11... | collective-permute-start | bytes 98312 | tf_op jit(solution)/shard_map/ppermute | solution.py:482
  42.2 2.3 %prepare.1 = (f32[8,18,80,128]{3,2,1,0:T(8,128)S(1)}, f32[18,80,128]{2,1,0:T(8,128)S(1)}) custom-call(f32[8,64,2048]{2,1,0:T(8,128)} %v.3, s32[64,2048]{1,0:T(8,128)S(1)} %copy-done.1, f32[8,2304]{1,0:T(8,128)S(1)} %collective-permute-done.4.far_north, f32[8,2304]{1,0:T(8,128)S(1)} %collective-permute-done.5.far_south, ...), custom_call_target="tpu_custom_call" | custom-call | tf_op jit(solution)/shard_map/prepare/pallas_call | solution.py:488
  44.5 0.7 %collective-permute-done.9.rims = f32[8,1024]{1,0:T(8,128)S(1)} collective-permute-done((f32[8,1024]{1,0:T(8,128)S(1)}, f32[8,1024]{1,0:T(8,128)S(1)}, u32[]{:S(2)}, u32[]{:S(2)}) %collective-permute-start.9) | collective-permute-done | bytes 32800 | tf_op jit(solution)/shard_map/ppermute | solution.py:482
  45.3 9.6 %laplace.1 = (f32[8,64,2048]{2,1,0:T(8,128)}, f32[64,1024]{1,0:T(8,128)S(1)}, f32[3,64,1024]{2,1,0:T(8,128)S(1)}) custom-call(s32[1]{0:T(128)} %bitcast.group.group_ref, f32[8,18,80,128]{3,2,1,0:T(8,128)S(1)} %get-tuple-element.32.volume, f32[18,80,128]{2,1,0:T(8,128)S(1)} %get-tuple-element.33.depth, f32[64,2048]{1,0:T(8,128)S(1)} %collective-permute-done.8.far_layer, ...), custom_call_target="tpu_custom_call" | custom-call | tf_op jit(solution)/shard_map/laplace/pallas_call | solution.py:497
  54.8 1.6 %top.1 = f32[8,64,2048]{2,1,0:T(8,128)} custom-call(s32[1]{0:T(128)} %bitcast.group.group_ref, f32[8,64,2048]{2,1,0:T(8,128)} %get-tuple-element.38.before, f32[64,1024]{1,0:T(8,128)S(1)} %get-tuple-element.39.part, f32[3,64,1024]{2,1,0:T(8,128)S(1)} %get-tuple-element.40.coefficients, ...), custom_call_target="tpu_custom_call", output_to_operand_aliasing={{}: (1, {})} | custom-call | tf_op jit(solution)/shard_map/top/pallas_call | solution.py:511
  (16 shorter events, 0.2 us)
Async XLA Ops:
  0.6 16.5 %copy-start.2 = (f32[64,1024]{1,0:T(8,128)S(1)}, f32[64,1024]{1,0:T(8,128)}, u32[]{:S(2)}) copy-start(f32[64,1024]{1,0:T(8,128)} %e.3) | copy-start | bytes 786436
  0.6 16.5 %copy-start.3 = (f32[64,1024]{1,0:T(8,128)S(1)}, f32[64,1024]{1,0:T(8,128)}, u32[]{:S(2)}) copy-start(f32[64,1024]{1,0:T(8,128)} %p.3) | copy-start | bytes 786436
  0.7 30.3 %copy-start.1 = (s32[64,2048]{1,0:T(8,128)S(1)}, s32[64,2048]{1,0:T(8,128)}, u32[]{:S(2)}) copy-start(s32[64,2048]{1,0:T(8,128)} %sea.1) | copy-start | bytes 1572868
  0.7 30.3 %copy-start = (f32[8,64,2048]{2,1,0:T(8,128)S(1)}, f32[8,64,2048]{2,1,0:T(8,128)}, u32[]{:S(2)}) copy-start(f32[8,64,2048]{2,1,0:T(8,128)} %v.3) | copy-start | bytes 12582916
  2.0 43.3 %collective-permute-start.8 = (f32[64,2048]{1,0:T(8,128)S(1)}, f32[64,2048]{1,0:T(8,128)S(1)}, u32[]{:S(2)}, u32[]{:S(2)}) collective-permute-start(f32[64,2048]{1,0:T(8,128)S(1)} %get-tuple-element.34), channel_id=1, source_target_pairs={{0,1},{1,0},{2,3},{3,2},{4,5},{5,4},{6,7},{7,6},{8,9},{9,8},{10,11... | collective-permute-start | bytes 1572872 | tf_op jit(solution)/shard_map/ppermute | solution.py:415
  5.0 12.1 %collective-permute-start = (f32[8,128]{1,0:T(8,128)S(1)}, f32[8,128]{1,0:T(8,128)S(1)}, u32[]{:S(2)}, u32[]{:S(2)}) collective-permute-start(f32[8,128]{1,0:T(8,128)S(1)} %get-tuple-element.22), channel_id=1, source_target_pairs={{0,1},{1,0},{2,3},{3,2},{4,5},{5,4},{6,7},{7,6},{8,9},{9,8},{10,11... | collective-permute-start | bytes 12296 | tf_op jit(solution)/shard_map/ppermute | solution.py:414
  5.1 12.0 %collective-permute-start.1 = (f32[8,128]{1,0:T(8,128)S(1)}, f32[8,128]{1,0:T(8,128)S(1)}, u32[]{:S(2)}, u32[]{:S(2)}) collective-permute-start(f32[8,128]{1,0:T(8,128)S(1)} %get-tuple-element.23), channel_id=1, source_target_pairs={{1,2},{3,4},{5,6},{7,0},{2,1},{4,3},{6,5},{0,7},{9,10},{11,12},{13... | collective-permute-start | bytes 12296 | tf_op jit(solution)/shard_map/ppermute | solution.py:416
  17.2 6.9 %collective-permute-start.2 = (f32[16,1280]{1,0:T(8,128)S(1)}, f32[16,1280]{1,0:T(8,128)S(1)}, u32[]{:S(2)}, u32[]{:S(2)}) collective-permute-start(f32[16,1280]{1,0:T(8,128)S(1)} %get-tuple-element.24), channel_id=1, source_target_pairs={{0,8},{8,16},{16,24},{24,0},{1,9},{9,17},{17,25},{25,1},{2,10},{10... | collective-permute-start | bytes 245768 | tf_op jit(solution)/shard_map/ppermute | solution.py:455
  19.1 5.9 %collective-permute-start.3 = (f32[16,1280]{1,0:T(8,128)S(1)}, f32[16,1280]{1,0:T(8,128)S(1)}, u32[]{:S(2)}, u32[]{:S(2)}) collective-permute-start(f32[16,1280]{1,0:T(8,128)S(1)} %get-tuple-element.25), channel_id=1, source_target_pairs={{0,24},{8,0},{16,8},{24,16},{1,25},{9,1},{17,9},{25,17},{2,26},{10... | collective-permute-start | bytes 245768 | tf_op jit(solution)/shard_map/ppermute | solution.py:456
  28.9 16.4 %collective-permute-start.10 = (f32[72,1024]{1,0:T(8,128)S(1)}, f32[72,1024]{1,0:T(8,128)S(1)}, u32[]{:S(2)}, u32[]{:S(2)}) collective-permute-start(f32[72,1024]{1,0:T(8,128)S(1)} %get-tuple-element.37), channel_id=1, source_target_pairs={{0,1},{1,0},{2,3},{3,2},{4,5},{5,4},{6,7},{7,6},{8,9},{9,8},{10,11... | collective-permute-start | bytes 884744 | tf_op jit(solution)/shard_map/ppermute | solution.py:469
  29.9 25.0 %collective-permute-start.11 = (f32[64,1024]{1,0:T(8,128)}, f32[64,1024]{1,0:T(8,128)S(1)}, u32[]{:S(2)}, u32[]{:S(2)}) collective-permute-start(f32[64,1024]{1,0:T(8,128)} %get-tuple-element.20), channel_id=1, source_target_pairs={{0,1},{1,0},{2,3},{3,2},{4,5},{5,4},{6,7},{7,6},{8,9},{9,8},{10,11... | collective-permute-start | bytes 786440 | tf_op jit(solution)/shard_map/ppermute | solution.py:483
  31.2 3.1 %collective-permute-start.6 = (f32[8,128]{1,0:T(8,128)S(1)}, f32[8,128]{1,0:T(8,128)S(1)}, u32[]{:S(2)}, u32[]{:S(2)}) collective-permute-start(f32[8,128]{1,0:T(8,128)S(1)} %get-tuple-element.30), channel_id=1, source_target_pairs={{0,2},{2,4},{4,6},{6,0},{1,3},{3,5},{5,7},{7,1},{8,10},{10,12},{12... | collective-permute-start | bytes 12296 | tf_op jit(solution)/shard_map/ppermute | solution.py:472
  31.2 4.2 %collective-permute-start.7 = (f32[8,128]{1,0:T(8,128)S(1)}, f32[8,128]{1,0:T(8,128)S(1)}, u32[]{:S(2)}, u32[]{:S(2)}) collective-permute-start(f32[8,128]{1,0:T(8,128)S(1)} %get-tuple-element.31), channel_id=1, source_target_pairs={{0,6},{2,0},{4,2},{6,4},{1,7},{3,1},{5,3},{7,5},{8,14},{10,8},{12,... | collective-permute-start | bytes 12296 | tf_op jit(solution)/shard_map/ppermute | solution.py:473
  34.3 7.0 %collective-permute-start.4 = (f32[8,2304]{1,0:T(8,128)S(1)}, f32[8,2304]{1,0:T(8,128)S(1)}, u32[]{:S(2)}, u32[]{:S(2)}) collective-permute-start(f32[8,2304]{1,0:T(8,128)S(1)} %get-tuple-element.28), channel_id=1, source_target_pairs={{0,8},{8,16},{16,24},{24,0},{1,9},{9,17},{17,25},{25,1},{2,10},{10... | collective-permute-start | bytes 221192 | tf_op jit(solution)/shard_map/ppermute | solution.py:470
  35.4 5.9 %collective-permute-start.5 = (f32[8,2304]{1,0:T(8,128)S(1)}, f32[8,2304]{1,0:T(8,128)S(1)}, u32[]{:S(2)}, u32[]{:S(2)}) collective-permute-start(f32[8,2304]{1,0:T(8,128)S(1)} %get-tuple-element.29), channel_id=1, source_target_pairs={{0,24},{8,0},{16,8},{24,16},{1,25},{9,1},{17,9},{25,17},{2,26},{10... | collective-permute-start | bytes 221192 | tf_op jit(solution)/shard_map/ppermute | solution.py:471
  41.3 3.9 %collective-permute-start.9 = (f32[8,1024]{1,0:T(8,128)S(1)}, f32[8,1024]{1,0:T(8,128)S(1)}, u32[]{:S(2)}, u32[]{:S(2)}) collective-permute-start(f32[8,1024]{1,0:T(8,128)S(1)} %rim_pack.1), channel_id=1, source_target_pairs={{0,1},{1,0},{2,3},{3,2},{4,5},{5,4},{6,7},{7,6},{8,9},{9,8},{10,11... | collective-permute-start | bytes 98312 | tf_op jit(solution)/shard_map/ppermute | solution.py:482
where the time goes:
time: 56.6 us; the launch traced here: 56.5 us
  waiting for transfers between devices  19.3 us (34%)
  Pallas kernels  19.2 us (34%)
  starting transfers between devices  17.3 us (31%)
  between operations  0.72 us (1%)
    ppermute x1, waiting for transfers between devices, shards(): seam = lax.ppermute(seam, flat, partner)  10.2 us
    pallas_call x1, Pallas kernels, shards(): pl.pallas_call(functools.partial(laplace, total_layers), out_shape=(shape...  9.58 us
    pallas_call x1, Pallas kernels, shards(): pl.pallas_call(surface, out_shape=(shape(rows, width),) * 2 + (shape(rows...  3.91 us
    ppermute x1, waiting for transfers between devices, shards(): far_north = lax.ppermute(up, 'gx', ring('gx', 1))  3.16 us
    ppermute x1, starting transfers between devices, shards(): far_layer = lax.ppermute(layer, flat, partner)  3.06 us
    ppermute x1, waiting for transfers between devices, shards(): north = lax.ppermute(row_up, 'gx', ring('gx', 1))  2.94 us
    ppermute x1, starting transfers between devices, shards(): far_south = lax.ppermute(down, 'gx', ring('gx', -1))  2.7 us
    pallas_call x1, Pallas kernels, shards(): pl.pallas_call(prepare, out_shape=(shape(layers, tiles + 2, tall, LANES),...  2.34 us
  transfers between devices with their start and end apart: 12, of which 6 were waited for; matrix products, arithmetic and copies ran while one was open for 0% of the time, Pallas kernels for 29%

commit v1 on v0

--- a/solution.py
+++ b/solution.py
@@ -42,8 +42,14 @@
     left = edges[0].T[:SUBS]
     right = edges[1].T[LANES - SUBS :]
     seam[...] = jnp.where(low, right, left)
-    outer[...] = jnp.where(low, left, right)
     whole.wait()
+    tile = layer.shape[1]
+    sides = jnp.concatenate([layer[:, :LANES], layer[:, tile - LANES :]], 0).T
+    ends = pltpu.roll(sides[LANES - SUBS :], LANES // 2, 1)
+    side = jnp.where(low, sides[:1], ends[SUBS - 1 :])
+    sub = lax.broadcasted_iota(jnp.int32, outer.shape, 0)
+    place = jnp.where(low, SUBS - 1, 0)
+    outer[...] = jnp.where(sub == place, side, jnp.where(low, left, right))
 
 
 def lazy_pack(v_top, v_bottom, v_left, v_right, s_top, s_bottom, s_left, s_right, up, down, to_right, to_left):
@@ -188,56 +194,178 @@
         rims[4:5, lane : lane + LANES] = jnp.where(low, top_pair, side[0:1, :])
 
 
-def prepare(v, sea, far_north, far_south, x_left, x_right, volume, depth, sems):
-    layers, rows, tile = v.shape
-    tiles = tile // LANES
+def prepare(v, sea, volume, depth, sems):
+    _, rows, tile = v.shape
     inner = slice(SUBS, SUBS + rows)
     copies = []
-    for t in range(tiles):
-        copies.append(
-            pltpu.make_async_copy(
-                v.at[:, :, t * LANES : (t + 1) * LANES], volume.at[:, t + 1, inner, :], sems.at[t]
-            )
-        )
+    for t in range(tile // LANES):
+        part = slice(t * LANES, (t + 1) * LANES)
+        copies.append(pltpu.make_async_copy(v.at[:, :, part], volume.at[:, t + 1, inner, :], sems.at[t]))
         copies[-1].start()
+    for t in range(tile // LANES):
+        depth[t + 1, inner, :] = sea[:, t * LANES : (t + 1) * LANES].astype(jnp.float32) * depth_unit
+    for copy in copies:
+        copy.wait()
+
+
+def run_all(copies):
+    for copy in copies:
+        copy.start()
+    for copy in copies:
+        copy.wait()
+
+
+def fill_columns(old_volume, old_depth, x_left, x_right, volume, depth, sides, depths, sems):
+    del old_volume, old_depth
+    layers, tiles, rows = volume.shape[0], volume.shape[1], sides.shape[2]
+    inner = slice(SUBS, SUBS + rows)
     left = square(x_left[...], False).T
     right = square(x_right[...], False).T
     half, pairs = LANES // 2, layers // 2
     for k in range(layers):
         base = (k % 2) * half
-        volume[k, 0, inner, :] = pltpu.roll(left, LANES - 1 - k // 2, 1)[base : base + rows]
-        volume[k, tiles + 1, inner, :] = pltpu.roll(right, (LANES - k // 2) % LANES, 1)[base : base + rows]
-        for t in range(tiles):
-            part = slice(t * LANES, (t + 1) * LANES)
-            volume[k, t + 1, SUBS - 1 : SUBS, :] = far_north[k : k + 1, part]
-            volume[k, t + 1, SUBS + rows : SUBS + rows + 1, :] = far_south[k : k + 1, part]
-    depth[0, inner, :] = pltpu.roll(left, LANES - 1 - pairs, 1)[:rows]
-    depth[tiles + 1, inner, :] = pltpu.roll(right, LANES - pairs, 1)[:rows]
+        sides[0, k] = pltpu.roll(left, LANES - 1 - k // 2, 1)[base : base + rows]
+        sides[1, k] = pltpu.roll(right, (LANES - k // 2) % LANES, 1)[base : base + rows]
+    depths[0] = pltpu.roll(left, LANES - 1 - pairs, 1)[:rows]
+    depths[1] = pltpu.roll(right, LANES - pairs, 1)[:rows]
+    copies = []
+    for side, t in ((0, 0), (1, tiles - 1)):
+        copies.append(pltpu.make_async_copy(sides.at[side], volume.at[:, t, inner, :], sems.at[2 * side]))
+        copies.append(pltpu.make_async_copy(depths.at[side], depth.at[t, inner, :], sems.at[2 * side + 1]))
+    run_all(copies)
+
+
+def fill_rows(old_volume, old_depth, token, far_north, far_south, volume, depth, edges, depths, sems):
+    del old_volume, old_depth, token
+    layers, tiles, tall = volume.shape[0], volume.shape[1], volume.shape[2]
+    tile = (tiles - 2) * LANES
     piece = tile // SUBS // LANES
-    for t in range(tiles):
-        part = slice(t * LANES, (t + 1) * LANES)
-        depth[t + 1, inner, :] = sea[:, part].astype(jnp.float32) * depth_unit
-        q, start = t // piece, tile + (t % piece) * LANES
-        depth[t + 1, SUBS - 1 : SUBS, :] = far_north[q : q + 1, start : start + LANES]
-        depth[t + 1, SUBS + rows : SUBS + rows + 1, :] = far_south[q : q + 1, start : start + LANES]
-    for copy in copies:
-        copy.wait()
-
-
-def laplace(
-    total_layers, group_ref, volume, depth, far_layer, rims, wide_e, wide_p, height,
-    out, part, coefficients, column, ghost,
-):
-    block = pl.program_id(0)
+    for end, source, row in ((0, far_north, SUBS - 1), (1, far_south, 0)):
+        for t in range(tiles - 2):
+            for k in range(layers):
+                edges[end, k, t + 1, row : row + 1, :] = source[k : k + 1, t * LANES : (t + 1) * LANES]
+            q, start = t // piece, tile + (t % piece) * LANES
+            depths[end, t + 1, row : row + 1, :] = source[q : q + 1, start : start + LANES]
+    copies = []
+    for end, rows in ((0, slice(0, SUBS)), (1, slice(tall - SUBS, tall))):
+        copies.append(pltpu.make_async_copy(edges.at[end], volume.at[:, :, rows, :], sems.at[2 * end]))
+        copies.append(pltpu.make_async_copy(depths.at[end], depth.at[:, rows, :], sems.at[2 * end + 1]))
+    run_all(copies)
+
+
+def apply_tile(total_layers, group, block, volume, depth, t, heights, local, ghost, spot, mine, write, rest=None):
+    low = group == 0
+    layers = volume.shape[0]
+    spacing = 1.0 / total_layers
+    sigma = (group * layers).astype(jnp.float32) * spacing + 0.5 * spacing
+    gain = (2 * group).astype(jnp.float32)
+    here = pl.multiple_of((block + 1) * SUBS, SUBS)
+
+    def near(ref, t):
+        at = lambda column, step: ref[column, pl.ds(here + step, SUBS), :]
+        cur = at(t, 0)
+        left, right = at(t - 1, 0), at(t + 1, 0)
+        return cur, at(t, -1), at(t, 1), shift_lanes(left, cur, right, -1), shift_lanes(left, cur, right, 1)
+
+    def differences(ref, t):
+        p, up, down, left, right = near(ref, t)
+        return p, down - up, right - left
+
+    d, d_x, d_y = differences(depth, t)
+    h, h_x, h_y = differences(heights, local)
+    inverse = 1.0 / (d + h)
+    scale = (0.25 / spacing) * inverse
+    bx, by = scale * (d_x + h_x), scale * (d_y + h_y)
+    ux, uy = scale * d_x - sigma * bx, scale * d_y - sigma * by
+    bx, by = spacing * bx, spacing * by
+    scaled = inverse * (1.0 / spacing)
+    weight = 4.0 * (ux * ux + uy * uy) + scaled * scaled
+    bend = 4.0 * (bx * bx + by * by)
+    step = bend - 8.0 * (ux * bx + uy * by)
+    bend = bend + bend
+
+    def level(k):
+        p, up, down, left, right = near(volume.at[k], t)
+        return p, down - up, right - left, ((down + up) + (right + left)) - 4.0 * p
+
+    far = differences(ghost, spot)
+    this = level(0)
+    lower = [jnp.where(low, a, b) for a, b in zip(this, far)]
+    rise_below = this[0] - lower[0]
+    for k in range(layers):
+        if k < layers - 1:
+            upper = level(k + 1)
+        else:
+            upper = [jnp.where(low, a, -b) for a, b in zip(far, this)]
+            if mine is not None:
+                upper = [a + gain * b for a, b in zip(upper, differences(mine, local))]
+        rise = upper[0] - this[0]
+        value = this[3] + ux * (upper[1] - lower[1]) + uy * (upper[2] - lower[2])
+        value = value + weight * (rise - rise_below)
+        write(k, value)
+        if k < layers - 1:
+            ux, uy = ux - bx, uy - by
+            weight, step = weight + step, step + bend
+        elif rest is not None:
+            rest(value, ux, uy, weight)
+        lower, this, rise_below = this, upper, rise
+
+
+def lanes_of(local):
+    return pl.ds(pl.multiple_of((local - 1) * LANES, LANES), LANES)
+
+
+def inside(total_layers, group_ref, volume, depth, far_layer, outer, wide_e, wide_p, out, token, ghost):
     group = group_ref[0]
     low = group == 0
-    layers = volume.shape[0]
+    rows, tile = far_layer.shape
+    width = tile // 2
+    halves = width // LANES
+    inner = slice(SUBS, SUBS + rows)
+
+    @pl.when(pl.program_id(0) == 0)
+    def _():
+        token[...] = jnp.zeros_like(token)
+        edge = square(outer[...], False).T[:rows]
+        at_left = pltpu.roll(edge, LANES - 1, 1)
+        at_right = pltpu.roll(edge, LANES - (SUBS - 1), 1)
+        ghost[0, inner, :] = jnp.where(low, at_left, far_layer[:, width - LANES : width])
+        ghost[halves + 1, inner, :] = jnp.where(low, far_layer[:, width : width + LANES], at_right)
+        for t in range(halves):
+            lanes = pl.ds(pl.multiple_of(group * width + t * LANES, LANES), LANES)
+            ghost[t + 1, inner, :] = far_layer[:, lanes]
+
+    def pair(index, carry):
+        for step in range(2):
+            local = index * 2 + step + 1
+
+            def write(k, value):
+                out[k, :, lanes_of(local)] = value
+
+            apply_tile(
+                total_layers, group, pl.program_id(0) + 1, volume, depth, group * halves + local,
+                wide_e, local, ghost, local, wide_p, write,
+            )
+        return carry
+
+    lax.fori_loop(0, halves // 2, pair, 0)
+
+
+def outside(
+    total_layers, group_ref, before, volume, depth, far_layer, rims, wide_e, wide_p, height,
+    out, part, coefficients, ghost, other_e,
+):
+    del before
+    index = pl.program_id(0)
+    group = group_ref[0]
+    low = group == 0
     rows, tile = far_layer.shape
     width = tile // 2
     tiles, halves = tile // LANES, width // LANES
+    last = rows // SUBS - 1
     inner = slice(SUBS, SUBS + rows)
 
-    @pl.when(block == 0)
+    @pl.when(index == 0)
     def _():
         far_left = pltpu.roll(square(rims[:, :LANES], False).T, LANES - 5, 1)[:rows]
         far_right = pltpu.roll(square(rims[:, LANES : 2 * LANES], False).T, LANES - 4, 1)[:rows]
@@ -248,96 +376,55 @@
             half, spot = t // halves, slice((t % halves) * LANES, (t % halves + 1) * LANES)
             ghost[t + 1, SUBS - 1 : SUBS, :] = rims[half : half + 1, spot]
             ghost[t + 1, SUBS + rows : SUBS + rows + 1, :] = rims[2 + half : 3 + half, spot]
-        own = group * halves + 1
-        other = (1 - group) * halves + 1
         for t in range(halves):
             spot = slice(t * LANES, (t + 1) * LANES)
-            column[own + t, : rows + 2 * SUBS, :] = wide_e[t + 1, : rows + 2 * SUBS, :] + depth[own + t]
-            column[other + t, inner, :] = height[:rows, spot] + depth[other + t, inner, :]
-            for row, at in ((SUBS - 1, rows), (SUBS + rows, rows + 1)):
-                column[other + t, row : row + 1, :] = height[at : at + 1, spot] + depth[other + t, row : row + 1, :]
-        own_side = group * (tiles + 1)
-        other_side = (1 - group) * (tiles + 1)
-        edge = jnp.where(low, wide_e[0, inner, :], wide_e[halves + 1, inner, :])
-        column[own_side, inner, :] = edge + depth[own_side, inner, :]
+            other_e[t + 1, inner, :] = height[:rows, spot]
+            other_e[t + 1, SUBS - 1 : SUBS, :] = height[rows : rows + 1, spot]
+            other_e[t + 1, SUBS + rows : SUBS + rows + 1, :] = height[rows + 1 : rows + 2, spot]
         edge = square(height[rows:, :LANES], False).T[:rows]
-        edge = jnp.where(low, pltpu.roll(edge, LANES - 4, 1), pltpu.roll(edge, LANES - 5, 1))
-        column[other_side, inner, :] = edge + depth[other_side, inner, :]
-
-    spacing = 1.0 / total_layers
-    sigma = (group * layers).astype(jnp.float32) * spacing + 0.5 * spacing
-    sign = (1 - 2 * group).astype(jnp.float32)
-    gain = (2 * group).astype(jnp.float32)
-    here = pl.multiple_of((block + 1) * SUBS, SUBS)
-
-    def near(ref, t):
-        at = lambda column, step: ref[column, pl.ds(here + step, SUBS), :]
-        cur = at(t, 0)
-        left, right = at(t - 1, 0), at(t + 1, 0)
-        return cur, at(t, -1), at(t, 1), shift_lanes(left, cur, right, -1), shift_lanes(left, cur, right, 1)
-
-    def differences(ref, t):
-        p, up, down, left, right = near(ref, t)
-        return p, down - up, right - left
-
-    def chunk(t, mine):
-        c, c_up, c_down, c_left, c_right = near(column, t)
-        _, d_x, d_y = differences(depth, t)
-        inverse = 1.0 / c
-        scale = (0.25 / spacing) * inverse
-        bx, by = scale * (c_down - c_up), scale * (c_right - c_left)
-        ux, uy = scale * d_x - sigma * bx, scale * d_y - sigma * by
-        bx, by = spacing * bx, spacing * by
-        scaled = inverse * (1.0 / spacing)
-        weight = 4.0 * (ux * ux + uy * uy) + scaled * scaled
-        bend = 4.0 * (bx * bx + by * by)
-        step = bend - 8.0 * (ux * bx + uy * by)
-        bend = bend + bend
-
-        def level(k):
-            p, up, down, left, right = near(volume.at[k], t)
-            return p, down - up, right - left, ((down + up) + (right + left)) - 4.0 * p
-
-        far = differences(ghost, t)
-        this = level(0)
-        lower = [jnp.where(low, a, b) for a, b in zip(this, far)]
-        rise_below = this[0] - lower[0]
-        spot = pl.ds(pl.multiple_of((t - 1) * LANES, LANES), LANES)
-        for k in range(layers):
-            if k < layers - 1:
-                upper = level(k + 1)
-            else:
-                upper = [jnp.where(low, a, -b) for a, b in zip(far, this)]
-                if mine is not None:
-                    upper = [a + gain * b for a, b in zip(upper, differences(wide_p, mine))]
-            rise = upper[0] - this[0]
-            value = this[3] + ux * (upper[1] - lower[1]) + uy * (upper[2] - lower[2])
-            value = value + weight * (rise - rise_below)
-            out[k, :, spot] = value
-            if k < layers - 1:
-                ux, uy = ux - bx, uy - by
-                weight, step = weight + step, step + bend
-            elif mine is None:
-                local = pl.ds(pl.multiple_of((t - 1 - (1 - group) * halves) * LANES, LANES), LANES)
-                part[:, local] = value
-                coefficients[0, :, local] = ux
-                coefficients[1, :, local] = uy
-                coefficients[2, :, local] = weight
-            lower, this, rise_below = this, upper, rise
-
-    def own_pair(index, carry):
-        for inside in range(2):
-            mine = index * 2 + inside + 1
-            chunk(group * halves + mine, mine)
+        at_right, at_left = pltpu.roll(edge, LANES - 4, 1), pltpu.roll(edge, LANES - 5, 1)
+        other_e[0, inner, :] = jnp.where(low, wide_e[halves, inner, :], at_left)
+        other_e[halves + 1, inner, :] = jnp.where(low, at_right, wide_e[1, inner, :])
+
+    def own_pair(pair, carry):
+        for step in range(2):
+            local = pair * 2 + step + 1
+            t = group * halves + local
+
+            def write(k, value):
+                out[k, :, lanes_of(local)] = value
+
+            apply_tile(
+                total_layers, group, index * last, volume, depth, t, wide_e, local, ghost, t, wide_p, write
+            )
         return carry
 
-    def other_pair(index, carry):
-        for inside in range(2):
-            chunk((1 - group) * halves + index * 2 + inside + 1, None)
+    def other_pair(pair, carry):
+        for step in range(2):
+            local = pair * 2 + step + 1
+            t = (1 - group) * halves + local
+
+            def write(k, value):
+                out[k, :, lanes_of(local)] = value
+
+            def rest(value, ux, uy, weight):
+                part[:, lanes_of(local)] = value
+                coefficients[0, :, lanes_of(local)] = ux
+                coefficients[1, :, lanes_of(local)] = uy
+                coefficients[2, :, lanes_of(local)] = weight
+
+            apply_tile(
+                total_layers, group, index - 2, volume, depth, t, other_e, local, ghost, t, None, write, rest
+            )
         return carry
 
-    lax.fori_loop(0, halves // 2, own_pair, 0)
-    lax.fori_loop(0, halves // 2, other_pair, 0)
+    @pl.when(index < 2)
+    def _():
+        lax.fori_loop(0, halves // 2, own_pair, 0)
+
+    @pl.when(index >= 2)
+    def _():
+        lax.fori_loop(0, halves // 2, other_pair, 0)
 
 
 def top(group_ref, before, part, coefficients, height, wide_p, other_p, out, potential):
@@ -414,6 +501,20 @@
     seam = lax.ppermute(seam, flat, partner)
     far_layer = lax.ppermute(layer, flat, partner)
     outer = lax.ppermute(outer, flat, across)
+
+    tiles = tile // LANES
+    tall = rows + 2 * SUBS
+    tables = (shape(layers, tiles + 2, tall, LANES), shape(tiles + 2, tall, LANES))
+    anywhere = pl.BlockSpec(memory_space=pl.ANY)
+    volume, depth = pl.pallas_call(
+        prepare,
+        out_shape=tables,
+        in_specs=[hbm, vmem],
+        out_specs=[vmem] * 2,
+        scratch_shapes=[pltpu.SemaphoreType.DMA((tiles,))],
+        compiler_params=params,
+        name="prepare",
+    )(pltpu.with_memory_space_constraint(interior_potential, pltpu.HBM), seabed)
 
     up, down, to_right, to_left = pl.pallas_call(
         lazy_pack,
@@ -471,6 +572,37 @@
     far_south = lax.ppermute(down, "gx", ring("gx", -1))
     x_left = lax.ppermute(to_right, "gy", ring("gy", 1))
     x_right = lax.ppermute(to_left, "gy", ring("gy", -1))
+    volume, depth = pl.pallas_call(
+        fill_columns,
+        out_shape=tables,
+        in_specs=[anywhere] * 2 + [vmem] * 2,
+        out_specs=[anywhere] * 2,
+        scratch_shapes=[
+            pltpu.VMEM((2, layers, rows, LANES), f32),
+            pltpu.VMEM((2, rows, LANES), f32),
+            pltpu.SemaphoreType.DMA((4,)),
+        ],
+        input_output_aliases={0: 0, 1: 1},
+        compiler_params=params,
+        name="fill_columns",
+    )(volume, depth, x_left, x_right)
+    blocks = rows // SUBS
+    partial, token = pl.pallas_call(
+        functools.partial(inside, total_layers),
+        out_shape=(shape(layers, rows, tile), shape(SUBS, LANES)),
+        grid_spec=pltpu.PrefetchScalarGridSpec(
+            num_scalar_prefetch=1,
+            grid=(blocks - 2,),
+            in_specs=[vmem] * 6,
+            out_specs=[
+                pl.BlockSpec((layers, SUBS, width), lambda i, g: (0, i + 1, g[0])),
+                pl.BlockSpec((SUBS, LANES), lambda i, g: (0, 0)),
+            ],
+            scratch_shapes=[pltpu.VMEM((width // LANES + 2, tall, LANES), f32)],
+        ),
+        compiler_params=params,
+        name="inside",
+    )(group, volume, depth, far_layer, outer, wide_e, wide_p)
     rims = pl.pallas_call(
         rim_pack,
         out_shape=shape(SUBS, width),
@@ -482,32 +614,46 @@
     far_rims = lax.ppermute(rims, flat, partner)
     other_p = lax.ppermute(new_p, flat, partner)
 
-    blocks = rows // SUBS
-    tiles = tile // LANES
-    tall = rows + 2 * SUBS
     volume, depth = pl.pallas_call(
-        prepare,
-        out_shape=(shape(layers, tiles + 2, tall, LANES), shape(tiles + 2, tall, LANES)),
-        in_specs=[hbm] + [vmem] * 5,
-        out_specs=[vmem] * 2,
-        scratch_shapes=[pltpu.SemaphoreType.DMA((tiles,))],
-        compiler_params=params,
-        name="prepare",
-    )(pltpu.with_memory_space_constraint(interior_potential, pltpu.HBM), seabed, far_north, far_south, x_left, x_right)
+        fill_rows,
+        out_shape=tables,
+        in_specs=[anywhere] * 2 + [vmem] * 3,
+        out_specs=[anywhere] * 2,
+        scratch_shapes=[
+            pltpu.VMEM((2, layers, tiles + 2, SUBS, LANES), f32),
+            pltpu.VMEM((2, tiles + 2, SUBS, LANES), f32),
+            pltpu.SemaphoreType.DMA((4,)),
+        ],
+        input_output_aliases={0: 0, 1: 1},
+        compiler_params=params,
+        name="fill_rows",
+    )(volume, depth, token, far_north, far_south)
+
+    def place(i, g):
+        own = i < 2
+        return 0, jnp.where(own, i * (blocks - 1), i - 2), jnp.where(own, g[0], 1 - g[0])
+
     partial, part, coefficients = pl.pallas_call(
-        functools.partial(laplace, total_layers),
+        functools.partial(outside, total_layers),
         out_shape=(shape(layers, rows, tile), shape(rows, width), shape(3, rows, width)),
-        grid=(blocks,),
-        in_specs=[scalar] + [vmem] * 7,
-        out_specs=[
-            pl.BlockSpec((layers, SUBS, tile), lambda i: (0, i, 0)),
-            pl.BlockSpec((SUBS, width), lambda i: (i, 0)),
-            pl.BlockSpec((3, SUBS, width), lambda i: (0, i, 0)),
-        ],
-        scratch_shapes=[pltpu.VMEM((tiles + 2, tall, LANES), f32)] * 2,
-        compiler_params=params,
-        name="laplace",
-    )(group, volume, depth, far_layer, far_rims, wide_e, wide_p, far_height)
+        grid_spec=pltpu.PrefetchScalarGridSpec(
+            num_scalar_prefetch=1,
+            grid=(blocks + 2,),
+            in_specs=[hbm] + [vmem] * 7,
+            out_specs=[
+                pl.BlockSpec((layers, SUBS, width), place),
+                pl.BlockSpec((SUBS, width), lambda i, g: (jnp.maximum(i - 2, 0), 0)),
+                pl.BlockSpec((3, SUBS, width), lambda i, g: (0, jnp.maximum(i - 2, 0), 0)),
+            ],
+            scratch_shapes=[
+                pltpu.VMEM((tiles + 2, tall, LANES), f32),
+                pltpu.VMEM((width // LANES + 2, tall, LANES), f32),
+            ],
+        ),
+        input_output_aliases={1: 0},
+        compiler_params=params,
+        name="outside",
+    )(group, partial, volume, depth, far_layer, far_rims, wide_e, wide_p, far_height)
     result = pl.pallas_call(
         top,
         out_shape=shape(layers, rows, tile),

time: 56.6 us -> 58.7 us (1.037)
  the two profiles are of different devices: /device:TPU:0 before, /device:TPU:1 now
where the time goes in v1:
time: 58.7 us; the launch traced here: 57.7 us
  Pallas kernels  22 us (37%)
  waiting for transfers between devices  18.3 us (31%)
  starting transfers between devices  16.6 us (28%)
  between operations  0.75 us (1%)
    ppermute x1, waiting for transfers between devices, shards(): seam = lax.ppermute(seam, flat, partner)  9.17 us
    pallas_call x1, Pallas kernels, shards(): pl.pallas_call(functools.partial(outside, total_layers), out_shape=(shape...  6.93 us
    pallas_call x1, Pallas kernels, shards(): pl.pallas_call(functools.partial(inside, total_layers), out_shape=(shape(...  4.52 us
    pallas_call x1, Pallas kernels, shards(): pl.pallas_call(surface, out_shape=(shape(rows, width),) * 2 + (shape(rows...  3.91 us
    ppermute x1, starting transfers between devices, shards(): x_left = lax.ppermute(to_right, 'gy', ring('gy', 1))  2.77 us
    ppermute x1, starting transfers between devices, shards(): outer = lax.ppermute(outer, flat, across)  2.51 us
    ppermute x1, waiting for transfers between devices, shards(): north = lax.ppermute(row_up, 'gx', ring('gx', 1))  2.35 us
    pallas_call x1, Pallas kernels, shards(): pl.pallas_call(prepare, out_shape=tables, in_specs=[hbm, vmem], out_specs...  2.34 us
  transfers between devices with their start and end apart: 12, of which 8 were waited for; matrix products, arithmetic and copies ran while one was open for 0% of the time, Pallas kernels for 33%

profile of v1, /device:TPU:1, one launch (start us, length us, event | category | flops | bytes accessed | tf_op | source)
XLA Modules:
  0.0 57.7 jit_solution(5084141392849724494)
XLA Ops:
  0.7 1.5 %first_pack.1 = (f32[8,128]{1,0:T(8,128)S(1)}, f32[8,128]{1,0:T(8,128)S(1)}, f32[64,2048]{1,0:T(8,128)S(1)}) custom-call(s32[1]{0:T(128)} %bitcast.group.group_ref, f32[64,1024]{1,0:T(8,128)} %e.3, f32[64,1024]{1,0:T(8,128)} %p.3, f32[8,64,2048]{2,1,0:T(8,128)} %v_right.1), custom_call_target="tpu_custom_call" | custom-call | tf_op jit(solution)/shard_map/first_pack/pallas_call | solution.py:486
  2.2 2.1 %collective-permute-start.6 = (f32[64,2048]{1,0:T(8,128)S(1)}, f32[64,2048]{1,0:T(8,128)S(1)}, u32[]{:S(2)}, u32[]{:S(2)}) collective-permute-start(f32[64,2048]{1,0:T(8,128)S(1)} %get-tuple-element.40), channel_id=1, source_target_pairs={{0,1},{1,0},{2,3},{3,2},{4,5},{5,4},{6,7},{7,6},{8,9},{9,8},{10,11... | collective-permute-start | bytes 1572872 | tf_op jit(solution)/shard_map/ppermute | solution.py:502
  4.4 2.5 %collective-permute-start.1 = (f32[8,128]{1,0:T(8,128)S(1)}, f32[8,128]{1,0:T(8,128)S(1)}, u32[]{:S(2)}, u32[]{:S(2)}) collective-permute-start(f32[8,128]{1,0:T(8,128)S(1)} %get-tuple-element.29), channel_id=1, source_target_pairs={{1,2},{3,4},{5,6},{7,0},{2,1},{4,3},{6,5},{0,7},{9,10},{11,12},{13... | collective-permute-start | bytes 12296 | tf_op jit(solution)/shard_map/ppermute | solution.py:503
  6.9 9.2 %collective-permute-done.seam = f32[8,128]{1,0:T(8,128)S(1)} collective-permute-done((f32[8,128]{1,0:T(8,128)S(1)}, f32[8,128]{1,0:T(8,128)S(1)}, u32[]{:S(2)}, u32[]{:S(2)}) %collective-permute-start) | collective-permute-done | bytes 4128 | tf_op jit(solution)/shard_map/ppermute | solution.py:501
  16.0 0.9 %collective-permute-done.1.outer = f32[8,128]{1,0:T(8,128)S(1)} collective-permute-done((f32[8,128]{1,0:T(8,128)S(1)}, f32[8,128]{1,0:T(8,128)S(1)}, u32[]{:S(2)}, u32[]{:S(2)}) %collective-permute-start.1) | collective-permute-done | bytes 4128 | tf_op jit(solution)/shard_map/ppermute | solution.py:503
  17.0 1.6 %collective-permute-start.2 = (f32[16,1280]{1,0:T(8,128)S(1)}, f32[16,1280]{1,0:T(8,128)S(1)}, u32[]{:S(2)}, u32[]{:S(2)}) collective-permute-start(f32[16,1280]{1,0:T(8,128)S(1)} %get-tuple-element.30), channel_id=1, source_target_pairs={{0,8},{8,16},{16,24},{24,0},{1,9},{9,17},{17,25},{25,1},{2,10},{10... | collective-permute-start | bytes 245768 | tf_op jit(solution)/shard_map/ppermute | solution.py:556
  18.6 2.1 %collective-permute-start.3 = (f32[16,1280]{1,0:T(8,128)S(1)}, f32[16,1280]{1,0:T(8,128)S(1)}, u32[]{:S(2)}, u32[]{:S(2)}) collective-permute-start(f32[16,1280]{1,0:T(8,128)S(1)} %get-tuple-element.31), channel_id=1, source_target_pairs={{0,24},{8,0},{16,8},{24,16},{1,25},{9,1},{17,9},{25,17},{2,26},{10... | collective-permute-start | bytes 245768 | tf_op jit(solution)/shard_map/ppermute | solution.py:557
  20.7 2.4 %collective-permute-done.2.north = f32[16,1280]{1,0:T(8,128)S(1)} collective-permute-done((f32[16,1280]{1,0:T(8,128)S(1)}, f32[16,1280]{1,0:T(8,128)S(1)}, u32[]{:S(2)}, u32[]{:S(2)}) %collective-permute-start.2) | collective-permute-done | bytes 81952 | tf_op jit(solution)/shard_map/ppermute | solution.py:556
  23.0 1.1 %collective-permute-done.3.south = f32[16,1280]{1,0:T(8,128)S(1)} collective-permute-done((f32[16,1280]{1,0:T(8,128)S(1)}, f32[16,1280]{1,0:T(8,128)S(1)}, u32[]{:S(2)}, u32[]{:S(2)}) %collective-permute-start.3) | collective-permute-done | bytes 81952 | tf_op jit(solution)/shard_map/ppermute | solution.py:557
  24.1 3.9 %surface.1 = (f32[64,1024]{1,0:T(8,128)}, f32[64,1024]{1,0:T(8,128)}, f32[72,1024]{1,0:T(8,128)S(1)}, f32[10,88,128]{2,1,0:T(8,128)S(1)}, f32[10,88,128]{2,1,0:T(8,128)S(1)}) custom-call(s32[1]{0:T(128)} %bitcast.group.group_ref, f32[64,1024]{1,0:T(8,128)S(1)} %copy-done.2, f32[64,1024]{1,0:T(8,128)S(1)} %copy-done.3, ...), custom_call_target="tpu_custom_call" | custom-call | tf_op jit(solution)/shard_map/surface/pallas_call | solution.py:561
  28.0 1.5 %collective-permute-start.11 = (f32[64,1024]{1,0:T(8,128)}, f32[64,1024]{1,0:T(8,128)S(1)}, u32[]{:S(2)}, u32[]{:S(2)}) collective-permute-start(f32[64,1024]{1,0:T(8,128)} %get-tuple-element.26), channel_id=1, source_target_pairs={{0,1},{1,0},{2,3},{3,2},{4,5},{5,4},{6,7},{7,6},{8,9},{9,8},{10,11... | collective-permute-start | bytes 786440 | tf_op jit(solution)/shard_map/ppermute | solution.py:615
  29.7 2.8 %collective-permute-start.4 = (f32[8,128]{1,0:T(8,128)S(1)}, f32[8,128]{1,0:T(8,128)S(1)}, u32[]{:S(2)}, u32[]{:S(2)}) collective-permute-start(f32[8,128]{1,0:T(8,128)S(1)} %get-tuple-element.36), channel_id=1, source_target_pairs={{0,2},{2,4},{4,6},{6,0},{1,3},{3,5},{5,7},{7,1},{8,10},{10,12},{12... | collective-permute-start | bytes 12296 | tf_op jit(solution)/shard_map/ppermute | solution.py:573
  32.5 0.8 %collective-permute-done.4.x_left = f32[8,128]{1,0:T(8,128)S(1)} collective-permute-done((f32[8,128]{1,0:T(8,128)S(1)}, f32[8,128]{1,0:T(8,128)S(1)}, u32[]{:S(2)}, u32[]{:S(2)}) %collective-permute-start.4) | collective-permute-done | bytes 4128 | tf_op jit(solution)/shard_map/ppermute | solution.py:573
  33.3 0.8 %collective-permute-start.7 = (f32[8,2304]{1,0:T(8,128)S(1)}, f32[8,2304]{1,0:T(8,128)S(1)}, u32[]{:S(2)}, u32[]{:S(2)}) collective-permute-start(f32[8,2304]{1,0:T(8,128)S(1)} %get-tuple-element.45), channel_id=1, source_target_pairs={{0,8},{8,16},{16,24},{24,0},{1,9},{9,17},{17,25},{25,1},{2,10},{10... | collective-permute-start | bytes 221192 | tf_op jit(solution)/shard_map/ppermute | solution.py:571
  34.1 1.7 %collective-permute-done.5.x_right = f32[8,128]{1,0:T(8,128)S(1)} collective-permute-done((f32[8,128]{1,0:T(8,128)S(1)}, f32[8,128]{1,0:T(8,128)S(1)}, u32[]{:S(2)}, u32[]{:S(2)}) %collective-permute-start.5) | collective-permute-done | bytes 4128 | tf_op jit(solution)/shard_map/ppermute | solution.py:574
  35.8 2.3 %collective-permute-start.8 = (f32[8,2304]{1,0:T(8,128)S(1)}, f32[8,2304]{1,0:T(8,128)S(1)}, u32[]{:S(2)}, u32[]{:S(2)}) collective-permute-start(f32[8,2304]{1,0:T(8,128)S(1)} %get-tuple-element.46), channel_id=1, source_target_pairs={{0,24},{8,0},{16,8},{24,16},{1,25},{9,1},{17,9},{25,17},{2,26},{10... | collective-permute-start | bytes 221192 | tf_op jit(solution)/shard_map/ppermute | solution.py:572
  38.3 2.2 %collective-permute-done.8.far_south = f32[8,2304]{1,0:T(8,128)S(1)} collective-permute-done((f32[8,2304]{1,0:T(8,128)S(1)}, f32[8,2304]{1,0:T(8,128)S(1)}, u32[]{:S(2)}, u32[]{:S(2)}) %collective-permute-start.8) | collective-permute-done | bytes 73760 | tf_op jit(solution)/shard_map/ppermute | solution.py:572
  40.6 0.9 %collective-permute-start.9 = (f32[8,1024]{1,0:T(8,128)S(1)}, f32[8,1024]{1,0:T(8,128)S(1)}, u32[]{:S(2)}, u32[]{:S(2)}) collective-permute-start(f32[8,1024]{1,0:T(8,128)S(1)} %rim_pack.1), channel_id=1, source_target_pairs={{0,1},{1,0},{2,3},{3,2},{4,5},{5,4},{6,7},{7,6},{8,9},{9,8},{10,11... | collective-permute-start | bytes 98312 | tf_op jit(solution)/shard_map/ppermute | solution.py:614
  41.5 2.3 %prepare.1 = (f32[8,18,80,128]{3,2,1,0:T(8,128)S(1)}, f32[18,80,128]{2,1,0:T(8,128)S(1)}) custom-call(f32[8,64,2048]{2,1,0:T(8,128)} %v_right.1, s32[64,2048]{1,0:T(8,128)S(1)} %copy-done.1), custom_call_target="tpu_custom_call" | custom-call | tf_op jit(solution)/shard_map/prepare/pallas_call | solution.py:509
  43.8 0.5 fill_columns.1
  44.3 4.5 %inside.1 = (f32[8,64,2048]{2,1,0:T(8,128)}, f32[8,128]{1,0:T(8,128)S(1)}) custom-call(s32[1]{0:T(128)} %bitcast.group.group_ref, f32[8,18,80,128]{3,2,1,0:T(8,128)S(1)} %get-tuple-element.38.volume.old_volume, f32[18,80,128]{2,1,0:T(8,128)S(1)} %get-tuple-element.39.depth.old_depth, f32[64,2048]{1,0:T(8,128)S(1)} %collective-permute-done.6.far_layer, ...), custom_call_target="tpu_custom_call" | custom-call | tf_op jit(solution)/shard_map/inside/pallas_call | solution.py:590
  48.9 0.2 fill_rows.1
  49.1 6.9 %outside.1 = (f32[8,64,2048]{2,1,0:T(8,128)}, f32[64,1024]{1,0:T(8,128)S(1)}, f32[3,64,1024]{2,1,0:T(8,128)S(1)}) custom-call(s32[1]{0:T(128)} %bitcast.group.group_ref, f32[8,64,2048]{2,1,0:T(8,128)} %get-tuple-element.43.before, f32[8,18,80,128]{3,2,1,0:T(8,128)S(1)} %get-tuple-element.47.volume, ...), custom_call_target="tpu_custom_call", output_to_operand_aliasing={{0}: (1, {})} | custom-call | tf_op jit(solution)/shard_map/outside/pallas_call | solution.py:636
  56.1 1.6 %top.1 = f32[8,64,2048]{2,1,0:T(8,128)} custom-call(s32[1]{0:T(128)} %bitcast.group.group_ref, f32[8,64,2048]{2,1,0:T(8,128)} %get-tuple-element.50.before, f32[64,1024]{1,0:T(8,128)S(1)} %get-tuple-element.51.part, f32[3,64,1024]{2,1,0:T(8,128)S(1)} %get-tuple-element.52.coefficients, ...), custom_call_target="tpu_custom_call", output_to_operand_aliasing={{}: (1, {})} | custom-call | tf_op jit(solution)/shard_map/top/pallas_call | solution.py:657
  (19 shorter events, 0.7 us)
Async XLA Ops:
  0.6 16.3 %copy-start.2 = (f32[64,1024]{1,0:T(8,128)S(1)}, f32[64,1024]{1,0:T(8,128)}, u32[]{:S(2)}) copy-start(f32[64,1024]{1,0:T(8,128)} %e.3) | copy-start | bytes 786436
  0.6 16.3 %copy-start.3 = (f32[64,1024]{1,0:T(8,128)S(1)}, f32[64,1024]{1,0:T(8,128)}, u32[]{:S(2)}) copy-start(f32[64,1024]{1,0:T(8,128)} %p.3) | copy-start | bytes 786436
  0.7 28.8 %copy-start.1 = (s32[64,2048]{1,0:T(8,128)S(1)}, s32[64,2048]{1,0:T(8,128)}, u32[]{:S(2)}) copy-start(s32[64,2048]{1,0:T(8,128)} %s_right.1) | copy-start | bytes 1572868
  0.7 28.8 %copy-start = (f32[8,64,2048]{2,1,0:T(8,128)S(1)}, f32[8,64,2048]{2,1,0:T(8,128)}, u32[]{:S(2)}) copy-start(f32[8,64,2048]{2,1,0:T(8,128)} %v_right.1) | copy-start | bytes 12582916
  2.2 42.2 %collective-permute-start.6 = (f32[64,2048]{1,0:T(8,128)S(1)}, f32[64,2048]{1,0:T(8,128)S(1)}, u32[]{:S(2)}, u32[]{:S(2)}) collective-permute-start(f32[64,2048]{1,0:T(8,128)S(1)} %get-tuple-element.40), channel_id=1, source_target_pairs={{0,1},{1,0},{2,3},{3,2},{4,5},{5,4},{6,7},{7,6},{8,9},{9,8},{10,11... | collective-permute-start | bytes 1572872 | tf_op jit(solution)/shard_map/ppermute | solution.py:502
  4.3 11.8 %collective-permute-start = (f32[8,128]{1,0:T(8,128)S(1)}, f32[8,128]{1,0:T(8,128)S(1)}, u32[]{:S(2)}, u32[]{:S(2)}) collective-permute-start(f32[8,128]{1,0:T(8,128)S(1)} %get-tuple-element.28), channel_id=1, source_target_pairs={{0,1},{1,0},{2,3},{3,2},{4,5},{5,4},{6,7},{7,6},{8,9},{9,8},{10,11... | collective-permute-start | bytes 12296 | tf_op jit(solution)/shard_map/ppermute | solution.py:501
  4.4 12.5 %collective-permute-start.1 = (f32[8,128]{1,0:T(8,128)S(1)}, f32[8,128]{1,0:T(8,128)S(1)}, u32[]{:S(2)}, u32[]{:S(2)}) collective-permute-start(f32[8,128]{1,0:T(8,128)S(1)} %get-tuple-element.29), channel_id=1, source_target_pairs={{1,2},{3,4},{5,6},{7,0},{2,1},{4,3},{6,5},{0,7},{9,10},{11,12},{13... | collective-permute-start | bytes 12296 | tf_op jit(solution)/shard_map/ppermute | solution.py:503
  17.0 6.0 %collective-permute-start.2 = (f32[16,1280]{1,0:T(8,128)S(1)}, f32[16,1280]{1,0:T(8,128)S(1)}, u32[]{:S(2)}, u32[]{:S(2)}) collective-permute-start(f32[16,1280]{1,0:T(8,128)S(1)} %get-tuple-element.30), channel_id=1, source_target_pairs={{0,8},{8,16},{16,24},{24,0},{1,9},{9,17},{17,25},{25,1},{2,10},{10... | collective-permute-start | bytes 245768 | tf_op jit(solution)/shard_map/ppermute | solution.py:556
  18.6 5.6 %collective-permute-start.3 = (f32[16,1280]{1,0:T(8,128)S(1)}, f32[16,1280]{1,0:T(8,128)S(1)}, u32[]{:S(2)}, u32[]{:S(2)}) collective-permute-start(f32[16,1280]{1,0:T(8,128)S(1)} %get-tuple-element.31), channel_id=1, source_target_pairs={{0,24},{8,0},{16,8},{24,16},{1,25},{9,1},{17,9},{25,17},{2,26},{10... | collective-permute-start | bytes 245768 | tf_op jit(solution)/shard_map/ppermute | solution.py:557
  28.0 21.1 %collective-permute-start.10 = (f32[72,1024]{1,0:T(8,128)S(1)}, f32[72,1024]{1,0:T(8,128)S(1)}, u32[]{:S(2)}, u32[]{:S(2)}) collective-permute-start(f32[72,1024]{1,0:T(8,128)S(1)} %get-tuple-element.49), channel_id=1, source_target_pairs={{0,1},{1,0},{2,3},{3,2},{4,5},{5,4},{6,7},{7,6},{8,9},{9,8},{10,11... | collective-permute-start | bytes 884744 | tf_op jit(solution)/shard_map/ppermute | solution.py:570
  28.0 28.0 %collective-permute-start.11 = (f32[64,1024]{1,0:T(8,128)}, f32[64,1024]{1,0:T(8,128)S(1)}, u32[]{:S(2)}, u32[]{:S(2)}) collective-permute-start(f32[64,1024]{1,0:T(8,128)} %get-tuple-element.26), channel_id=1, source_target_pairs={{0,1},{1,0},{2,3},{3,2},{4,5},{5,4},{6,7},{7,6},{8,9},{9,8},{10,11... | collective-permute-start | bytes 786440 | tf_op jit(solution)/shard_map/ppermute | solution.py:615
  29.7 3.5 %collective-permute-start.4 = (f32[8,128]{1,0:T(8,128)S(1)}, f32[8,128]{1,0:T(8,128)S(1)}, u32[]{:S(2)}, u32[]{:S(2)}) collective-permute-start(f32[8,128]{1,0:T(8,128)S(1)} %get-tuple-element.36), channel_id=1, source_target_pairs={{0,2},{2,4},{4,6},{6,0},{1,3},{3,5},{5,7},{7,1},{8,10},{10,12},{12... | collective-permute-start | bytes 12296 | tf_op jit(solution)/shard_map/ppermute | solution.py:573
  32.5 3.3 %collective-permute-start.5 = (f32[8,128]{1,0:T(8,128)S(1)}, f32[8,128]{1,0:T(8,128)S(1)}, u32[]{:S(2)}, u32[]{:S(2)}) collective-permute-start(f32[8,128]{1,0:T(8,128)S(1)} %get-tuple-element.37), channel_id=1, source_target_pairs={{0,6},{2,0},{4,2},{6,4},{1,7},{3,1},{5,3},{7,5},{8,14},{10,8},{12,... | collective-permute-start | bytes 12296 | tf_op jit(solution)/shard_map/ppermute | solution.py:574
  33.3 5.0 %collective-permute-start.7 = (f32[8,2304]{1,0:T(8,128)S(1)}, f32[8,2304]{1,0:T(8,128)S(1)}, u32[]{:S(2)}, u32[]{:S(2)}) collective-permute-start(f32[8,2304]{1,0:T(8,128)S(1)} %get-tuple-element.45), channel_id=1, source_target_pairs={{0,8},{8,16},{16,24},{24,0},{1,9},{9,17},{17,25},{25,1},{2,10},{10... | collective-permute-start | bytes 221192 | tf_op jit(solution)/shard_map/ppermute | solution.py:571
  35.8 4.6 %collective-permute-start.8 = (f32[8,2304]{1,0:T(8,128)S(1)}, f32[8,2304]{1,0:T(8,128)S(1)}, u32[]{:S(2)}, u32[]{:S(2)}) collective-permute-start(f32[8,2304]{1,0:T(8,128)S(1)} %get-tuple-element.46), channel_id=1, source_target_pairs={{0,24},{8,0},{16,8},{24,16},{1,25},{9,1},{17,9},{25,17},{2,26},{10... | collective-permute-start | bytes 221192 | tf_op jit(solution)/shard_map/ppermute | solution.py:572
  40.6 8.6 %collective-permute-start.9 = (f32[8,1024]{1,0:T(8,128)S(1)}, f32[8,1024]{1,0:T(8,128)S(1)}, u32[]{:S(2)}, u32[]{:S(2)}) collective-permute-start(f32[8,1024]{1,0:T(8,128)S(1)} %rim_pack.1), channel_id=1, source_target_pairs={{0,1},{1,0},{2,3},{3,2},{4,5},{5,4},{6,7},{7,6},{8,9},{9,8},{10,11... | collective-permute-start | bytes 98312 | tf_op jit(solution)/shard_map/ppermute | solution.py:614

commit v2 on v0

--- a/solution.py
+++ b/solution.py
@@ -117,11 +117,17 @@
 
 
 def surface(
-    group, e, p, seam, outer, north, south,
-    new_e, new_p, height, wide_e, wide_p, e0, p0, e1, p1,
+    group, e, p, seam, outer, north, south, v, sea,
+    new_e, new_p, height, wide_e, wide_p, volume, depth, e0, p0, e1, p1, sems,
 ):
     rows, width = e.shape
     low = group[0] == 0
+    copies = []
+    for t in range(v.shape[2] // LANES):
+        part = slice(t * LANES, (t + 1) * LANES)
+        into = volume.at[:, t + 1, SUBS : SUBS + rows, :]
+        copies.append(pltpu.make_async_copy(v.at[:, :, part], into, sems.at[t]))
+        copies[-1].start()
     left, right = side_blocks(low, seam[...], outer[...])
     tiles = width // LANES + 2
     inner = slice(SUBS, SUBS + rows)
@@ -171,6 +177,10 @@
     left = jnp.concatenate([wide_e[0, inner, :], wide_p[0, inner, :]], 0).T[LANES - 1 :]
     right = jnp.concatenate([wide_e[tiles - 1, inner, :], wide_p[tiles - 1, inner, :]], 0).T[:1]
     height[rows + 4 : rows + 5, :LANES] = jnp.where(low, left, right)
+    for t in range(v.shape[2] // LANES):
+        depth[t + 1, inner, :] = sea[:, t * LANES : (t + 1) * LANES].astype(jnp.float32) * depth_unit
+    for copy in copies:
+        copy.wait()
 
 
 def rim_pack(group, far_north, far_south, x_left, x_right, rims):
@@ -188,45 +198,85 @@
         rims[4:5, lane : lane + LANES] = jnp.where(low, top_pair, side[0:1, :])
 
 
-def prepare(v, sea, far_north, far_south, x_left, x_right, volume, depth, sems):
-    layers, rows, tile = v.shape
-    tiles = tile // LANES
-    inner = slice(SUBS, SUBS + rows)
-    copies = []
-    for t in range(tiles):
-        copies.append(
-            pltpu.make_async_copy(
-                v.at[:, :, t * LANES : (t + 1) * LANES], volume.at[:, t + 1, inner, :], sems.at[t]
-            )
-        )
-        copies[-1].start()
+def run_all(copies):
+    for copy in copies:
+        copy.start()
+    for copy in copies:
+        copy.wait()
+
+
+def spread(volume, depth, x_left, x_right, east, around, depth_y, left_sides, right_sides):
+    layers, tiles = volume.shape[0], volume.shape[1] - 2
+    rows = east.shape[2]
     left = square(x_left[...], False).T
     right = square(x_right[...], False).T
-    half, pairs = LANES // 2, layers // 2
-    for k in range(layers):
+    half = LANES // 2
+    for k in range(layers + 1):
         base = (k % 2) * half
-        volume[k, 0, inner, :] = pltpu.roll(left, LANES - 1 - k // 2, 1)[base : base + rows]
-        volume[k, tiles + 1, inner, :] = pltpu.roll(right, (LANES - k // 2) % LANES, 1)[base : base + rows]
+        left_sides[k] = pltpu.roll(left, LANES - 1 - k // 2, 1)[base : base + rows]
+        right_sides[k] = pltpu.roll(right, (LANES - k // 2) % LANES, 1)[base : base + rows]
+
+    def both(at, sides, t):
+        cur = at(t)
+        before = sides[0] if t == 0 else at(t - 1)
+        after = sides[1] if t == tiles - 1 else at(t + 1)
+        return cur, shift_lanes(before, cur, after, -1), shift_lanes(before, cur, after, 1)
+
+    def layer(k, carry):
+        def part(quarter, inner_carry):
+            for step in range(4):
+                row = pl.multiple_of((quarter * 4 + step) * SUBS, SUBS)
+                here = pl.ds(pl.multiple_of(row + SUBS, SUBS), SUBS)
+                spot = pl.ds(row, SUBS)
+                sides = left_sides[k, spot, :], right_sides[k, spot, :]
+                for t in range(tiles):
+                    cur, west, far = both(lambda c: volume[k, c + 1, here, :], sides, t)
+                    east[k, t, spot, :] = far - west
+                    around[k, t, spot, :] = (far + west) - 4.0 * cur
+            return inner_carry
+
+        return lax.fori_loop(0, rows // SUBS // 4, part, carry)
+
+    lax.fori_loop(0, layers, layer, 0)
+
+    def floor(block, carry):
+        row = pl.multiple_of(block * SUBS, SUBS)
+        here = pl.ds(pl.multiple_of(row + SUBS, SUBS), SUBS)
+        spot = pl.ds(row, SUBS)
+        sides = left_sides[layers, spot, :], right_sides[layers, spot, :]
         for t in range(tiles):
-            part = slice(t * LANES, (t + 1) * LANES)
-            volume[k, t + 1, SUBS - 1 : SUBS, :] = far_north[k : k + 1, part]
-            volume[k, t + 1, SUBS + rows : SUBS + rows + 1, :] = far_south[k : k + 1, part]
-    depth[0, inner, :] = pltpu.roll(left, LANES - 1 - pairs, 1)[:rows]
-    depth[tiles + 1, inner, :] = pltpu.roll(right, LANES - pairs, 1)[:rows]
+            _, west, far = both(lambda c: depth[c + 1, here, :], sides, t)
+            depth_y[t, spot, :] = far - west
+        return carry
+
+    lax.fori_loop(0, rows // SUBS, floor, 0)
+
+
+def fill_rows(old_volume, old_depth, token, far_north, far_south, volume, depth, edges, depths, sems):
+    del old_volume, old_depth, token
+    layers, tiles, tall = volume.shape[0], volume.shape[1], volume.shape[2]
+    tile = (tiles - 2) * LANES
     piece = tile // SUBS // LANES
-    for t in range(tiles):
-        part = slice(t * LANES, (t + 1) * LANES)
-        depth[t + 1, inner, :] = sea[:, part].astype(jnp.float32) * depth_unit
-        q, start = t // piece, tile + (t % piece) * LANES
-        depth[t + 1, SUBS - 1 : SUBS, :] = far_north[q : q + 1, start : start + LANES]
-        depth[t + 1, SUBS + rows : SUBS + rows + 1, :] = far_south[q : q + 1, start : start + LANES]
-    for copy in copies:
-        copy.wait()
+    for end, source, row in ((0, far_north, SUBS - 1), (1, far_south, 0)):
+        for t in range(tiles - 2):
+            for k in range(layers):
+                edges[end, k, t + 1, row : row + 1, :] = source[k : k + 1, t * LANES : (t + 1) * LANES]
+            q, start = t // piece, tile + (t % piece) * LANES
+            depths[end, t + 1, row : row + 1, :] = source[q : q + 1, start : start + LANES]
+    copies = []
+    for end, rows in ((0, slice(0, SUBS)), (1, slice(tall - SUBS, tall))):
+        copies.append(pltpu.make_async_copy(edges.at[end], volume.at[:, :, rows, :], sems.at[2 * end]))
+        copies.append(pltpu.make_async_copy(depths.at[end], depth.at[:, rows, :], sems.at[2 * end + 1]))
+    run_all(copies)
+
+
+def lanes_of(tile):
+    return pl.ds(pl.multiple_of((tile - 1) * LANES, LANES), LANES)
 
 
 def laplace(
-    total_layers, group_ref, volume, depth, far_layer, rims, wide_e, wide_p, height,
-    out, part, coefficients, column, ghost,
+    total_layers, group_ref, volume, depth, east, around, depth_y, far_layer, rims, wide_e, wide_p, height,
+    out, part, coefficients, ghost, other_e,
 ):
     block = pl.program_id(0)
     group = group_ref[0]
@@ -248,44 +298,35 @@
             half, spot = t // halves, slice((t % halves) * LANES, (t % halves + 1) * LANES)
             ghost[t + 1, SUBS - 1 : SUBS, :] = rims[half : half + 1, spot]
             ghost[t + 1, SUBS + rows : SUBS + rows + 1, :] = rims[2 + half : 3 + half, spot]
-        own = group * halves + 1
-        other = (1 - group) * halves + 1
         for t in range(halves):
             spot = slice(t * LANES, (t + 1) * LANES)
-            column[own + t, : rows + 2 * SUBS, :] = wide_e[t + 1, : rows + 2 * SUBS, :] + depth[own + t]
-            column[other + t, inner, :] = height[:rows, spot] + depth[other + t, inner, :]
-            for row, at in ((SUBS - 1, rows), (SUBS + rows, rows + 1)):
-                column[other + t, row : row + 1, :] = height[at : at + 1, spot] + depth[other + t, row : row + 1, :]
-        own_side = group * (tiles + 1)
-        other_side = (1 - group) * (tiles + 1)
-        edge = jnp.where(low, wide_e[0, inner, :], wide_e[halves + 1, inner, :])
-        column[own_side, inner, :] = edge + depth[own_side, inner, :]
+            other_e[t + 1, inner, :] = height[:rows, spot]
+            other_e[t + 1, SUBS - 1 : SUBS, :] = height[rows : rows + 1, spot]
+            other_e[t + 1, SUBS + rows : SUBS + rows + 1, :] = height[rows + 1 : rows + 2, spot]
         edge = square(height[rows:, :LANES], False).T[:rows]
-        edge = jnp.where(low, pltpu.roll(edge, LANES - 4, 1), pltpu.roll(edge, LANES - 5, 1))
-        column[other_side, inner, :] = edge + depth[other_side, inner, :]
+        at_right, at_left = pltpu.roll(edge, LANES - 4, 1), pltpu.roll(edge, LANES - 5, 1)
+        other_e[0, inner, :] = jnp.where(low, wide_e[halves, inner, :], at_left)
+        other_e[halves + 1, inner, :] = jnp.where(low, at_right, wide_e[1, inner, :])
 
     spacing = 1.0 / total_layers
     sigma = (group * layers).astype(jnp.float32) * spacing + 0.5 * spacing
-    sign = (1 - 2 * group).astype(jnp.float32)
     gain = (2 * group).astype(jnp.float32)
+    row = pl.multiple_of(block * SUBS, SUBS)
     here = pl.multiple_of((block + 1) * SUBS, SUBS)
-
-    def near(ref, t):
+    spot = pl.ds(row, SUBS)
+
+    def differences(ref, t):
         at = lambda column, step: ref[column, pl.ds(here + step, SUBS), :]
-        cur = at(t, 0)
-        left, right = at(t - 1, 0), at(t + 1, 0)
-        return cur, at(t, -1), at(t, 1), shift_lanes(left, cur, right, -1), shift_lanes(left, cur, right, 1)
-
-    def differences(ref, t):
-        p, up, down, left, right = near(ref, t)
-        return p, down - up, right - left
-
-    def chunk(t, mine):
-        c, c_up, c_down, c_left, c_right = near(column, t)
-        _, d_x, d_y = differences(depth, t)
-        inverse = 1.0 / c
+        cur, left, right = at(t, 0), at(t - 1, 0), at(t + 1, 0)
+        return cur, at(t, 1) - at(t, -1), shift_lanes(left, cur, right, 1) - shift_lanes(left, cur, right, -1)
+
+    def apply_tile(t, heights, local, mine):
+        at = lambda ref, step: ref[t, pl.ds(here + step, SUBS), :]
+        d, d_x, d_y = at(depth, 0), at(depth, 1) - at(depth, -1), depth_y[t - 1, spot, :]
+        h, h_x, h_y = differences(heights, local)
+        inverse = 1.0 / (d + h)
         scale = (0.25 / spacing) * inverse
-        bx, by = scale * (c_down - c_up), scale * (c_right - c_left)
+        bx, by = scale * (d_x + h_x), scale * (d_y + h_y)
         ux, uy = scale * d_x - sigma * bx, scale * d_y - sigma * by
         bx, by = spacing * bx, spacing * by
         scaled = inverse * (1.0 / spacing)
@@ -295,45 +336,45 @@
         bend = bend + bend
 
         def level(k):
-            p, up, down, left, right = near(volume.at[k], t)
-            return p, down - up, right - left, ((down + up) + (right + left)) - 4.0 * p
+            at = lambda step: volume[k, t, pl.ds(here + step, SUBS), :]
+            up, down = at(-1), at(1)
+            return at(0), down - up, east[k, t - 1, spot, :], (down + up) + around[k, t - 1, spot, :]
 
         far = differences(ghost, t)
         this = level(0)
         lower = [jnp.where(low, a, b) for a, b in zip(this, far)]
         rise_below = this[0] - lower[0]
-        spot = pl.ds(pl.multiple_of((t - 1) * LANES, LANES), LANES)
         for k in range(layers):
             if k < layers - 1:
                 upper = level(k + 1)
             else:
                 upper = [jnp.where(low, a, -b) for a, b in zip(far, this)]
                 if mine is not None:
-                    upper = [a + gain * b for a, b in zip(upper, differences(wide_p, mine))]
+                    upper = [a + gain * b for a, b in zip(upper, differences(mine, local))]
             rise = upper[0] - this[0]
             value = this[3] + ux * (upper[1] - lower[1]) + uy * (upper[2] - lower[2])
             value = value + weight * (rise - rise_below)
-            out[k, :, spot] = value
+            out[k, :, lanes_of(t)] = value
             if k < layers - 1:
                 ux, uy = ux - bx, uy - by
                 weight, step = weight + step, step + bend
             elif mine is None:
-                local = pl.ds(pl.multiple_of((t - 1 - (1 - group) * halves) * LANES, LANES), LANES)
-                part[:, local] = value
-                coefficients[0, :, local] = ux
-                coefficients[1, :, local] = uy
-                coefficients[2, :, local] = weight
+                part[:, lanes_of(local)] = value
+                coefficients[0, :, lanes_of(local)] = ux
+                coefficients[1, :, lanes_of(local)] = uy
+                coefficients[2, :, lanes_of(local)] = weight
             lower, this, rise_below = this, upper, rise
 
-    def own_pair(index, carry):
-        for inside in range(2):
-            mine = index * 2 + inside + 1
-            chunk(group * halves + mine, mine)
+    def own_pair(pair, carry):
+        for step in range(2):
+            local = pair * 2 + step + 1
+            apply_tile(group * halves + local, wide_e, local, wide_p)
         return carry
 
-    def other_pair(index, carry):
-        for inside in range(2):
-            chunk((1 - group) * halves + index * 2 + inside + 1, None)
+    def other_pair(pair, carry):
+        for step in range(2):
+            local = pair * 2 + step + 1
+            apply_tile((1 - group) * halves + local, other_e, local, None)
         return carry
 
     lax.fori_loop(0, halves // 2, own_pair, 0)
@@ -415,6 +456,10 @@
     far_layer = lax.ppermute(layer, flat, partner)
     outer = lax.ppermute(outer, flat, across)
 
+    tiles = tile // LANES
+    tall = rows + 2 * SUBS
+    tables = (shape(layers, tiles + 2, tall, LANES), shape(tiles + 2, tall, LANES))
+    anywhere = pl.BlockSpec(memory_space=pl.ANY)
     up, down, to_right, to_left = pl.pallas_call(
         lazy_pack,
         out_shape=(shape(SUBS, tile + tile // SUBS),) * 2 + (shape(SUBS, LANES),) * 2,
@@ -455,22 +500,39 @@
     north = lax.ppermute(row_up, "gx", ring("gx", 1))
     south = lax.ppermute(row_down, "gx", ring("gx", -1))
 
+    tiles = tile // LANES
+    tall = rows + 2 * SUBS
+    tables = (shape(layers, tiles + 2, tall, LANES), shape(tiles + 2, tall, LANES))
+    anywhere = pl.BlockSpec(memory_space=pl.ANY)
     deep = rows + 3 * SUBS
     padded = (width // LANES + 2, deep, LANES)
-    new_e, new_p, height, wide_e, wide_p = pl.pallas_call(
+    new_e, new_p, height, wide_e, wide_p, volume, depth = pl.pallas_call(
         surface,
-        out_shape=(shape(rows, width),) * 2 + (shape(rows + SUBS, width),) + (shape(*padded),) * 2,
-        in_specs=[scalar] + [vmem] * 6,
-        out_specs=[vmem] * 5,
-        scratch_shapes=[pltpu.VMEM(padded, f32)] * 4,
+        out_shape=(shape(rows, width),) * 2 + (shape(rows + SUBS, width),) + (shape(*padded),) * 2 + tables,
+        in_specs=[scalar] + [vmem] * 6 + [hbm, vmem],
+        out_specs=[vmem] * 7,
+        scratch_shapes=[pltpu.VMEM(padded, f32)] * 4 + [pltpu.SemaphoreType.DMA((tiles,))],
         compiler_params=params,
         name="surface",
-    )(group, elevation, surface_potential, seam, outer, north, south)
+    )(
+        group, elevation, surface_potential, seam, outer, north, south,
+        pltpu.with_memory_space_constraint(interior_potential, pltpu.HBM), seabed,
+    )
     far_height = lax.ppermute(height, flat, partner)
     far_north = lax.ppermute(up, "gx", ring("gx", 1))
     far_south = lax.ppermute(down, "gx", ring("gx", -1))
     x_left = lax.ppermute(to_right, "gy", ring("gy", 1))
     x_right = lax.ppermute(to_left, "gy", ring("gy", -1))
+    east, around, depth_y = pl.pallas_call(
+        spread,
+        out_shape=(shape(layers, tiles, rows, LANES),) * 2 + (shape(tiles, rows, LANES),),
+        in_specs=[vmem] * 4,
+        out_specs=[vmem] * 3,
+        scratch_shapes=[pltpu.VMEM((layers + 1, rows, LANES), f32)] * 2,
+        compiler_params=params,
+        name="spread",
+    )(volume, depth, x_left, x_right)
+    blocks = rows // SUBS
     rims = pl.pallas_call(
         rim_pack,
         out_shape=shape(SUBS, width),
@@ -482,32 +544,40 @@
     far_rims = lax.ppermute(rims, flat, partner)
     other_p = lax.ppermute(new_p, flat, partner)
 
-    blocks = rows // SUBS
-    tiles = tile // LANES
-    tall = rows + 2 * SUBS
     volume, depth = pl.pallas_call(
-        prepare,
-        out_shape=(shape(layers, tiles + 2, tall, LANES), shape(tiles + 2, tall, LANES)),
-        in_specs=[hbm] + [vmem] * 5,
-        out_specs=[vmem] * 2,
-        scratch_shapes=[pltpu.SemaphoreType.DMA((tiles,))],
-        compiler_params=params,
-        name="prepare",
-    )(pltpu.with_memory_space_constraint(interior_potential, pltpu.HBM), seabed, far_north, far_south, x_left, x_right)
+        fill_rows,
+        out_shape=tables,
+        in_specs=[anywhere] * 3 + [vmem] * 2,
+        out_specs=[anywhere] * 2,
+        scratch_shapes=[
+            pltpu.VMEM((2, layers, tiles + 2, SUBS, LANES), f32),
+            pltpu.VMEM((2, tiles + 2, SUBS, LANES), f32),
+            pltpu.SemaphoreType.DMA((4,)),
+        ],
+        input_output_aliases={0: 0, 1: 1},
+        compiler_params=params,
+        name="fill_rows",
+    )(volume, depth, east, far_north, far_south)
+
     partial, part, coefficients = pl.pallas_call(
         functools.partial(laplace, total_layers),
         out_shape=(shape(layers, rows, tile), shape(rows, width), shape(3, rows, width)),
         grid=(blocks,),
-        in_specs=[scalar] + [vmem] * 7,
+        in_specs=[scalar] + [vmem] * 10,
         out_specs=[
             pl.BlockSpec((layers, SUBS, tile), lambda i: (0, i, 0)),
             pl.BlockSpec((SUBS, width), lambda i: (i, 0)),
             pl.BlockSpec((3, SUBS, width), lambda i: (0, i, 0)),
         ],
-        scratch_shapes=[pltpu.VMEM((tiles + 2, tall, LANES), f32)] * 2,
+        scratch_shapes=[
+            pltpu.VMEM((tiles + 2, tall, LANES), f32),
+            pltpu.VMEM((width // LANES + 2, tall, LANES), f32),
+        ],
         compiler_params=params,
         name="laplace",
-    )(group, volume, depth, far_layer, far_rims, wide_e, wide_p, far_height)
+    )(
+        group, volume, depth, east, around, depth_y, far_layer, far_rims, wide_e, wide_p, far_height,
+    )
     result = pl.pallas_call(
         top,
         out_shape=shape(layers, rows, tile),

time: 56.6 us -> 57.3 us (1.012)
  the two profiles are of different devices: /device:TPU:0 before, /device:TPU:1 now
where the time goes in v2:
time: 57.3 us; the launch traced here: 56.3 us
  Pallas kernels  20.4 us (36%)
  waiting for transfers between devices  18.3 us (32%)
  starting transfers between devices  16.7 us (29%)
  between operations  0.76 us (1%)
    ppermute x1, waiting for transfers between devices, shards(): seam = lax.ppermute(seam, flat, partner)  9.17 us
    pallas_call x1, Pallas kernels, shards(): pl.pallas_call(functools.partial(laplace, total_layers), out_shape=(shape...  8.16 us
    pallas_call x1, Pallas kernels, shards(): pl.pallas_call(spread, out_shape=(shape(layers, tiles, rows, LANES),) * 2...  4.48 us
    pallas_call x1, Pallas kernels, shards(): pl.pallas_call(surface, out_shape=(shape(rows, width),) * 2 + (shape(rows...  4.26 us
    ppermute x1, starting transfers between devices, shards(): x_left = lax.ppermute(to_right, 'gy', ring('gy', 1))  2.77 us
    ppermute x1, starting transfers between devices, shards(): outer = lax.ppermute(outer, flat, across)  2.51 us
    ppermute x1, waiting for transfers between devices, shards(): north = lax.ppermute(row_up, 'gx', ring('gx', 1))  2.35 us
    ppermute x1, starting transfers between devices, shards(): far_south = lax.ppermute(down, 'gx', ring('gx', -1))  2.28 us
  transfers between devices with their start and end apart: 12, of which 8 were waited for; matrix products, arithmetic and copies ran while one was open for 0% of the time, Pallas kernels for 31%

profile of v2, /device:TPU:1, one launch (start us, length us, event | category | flops | bytes accessed | tf_op | source)
XLA Modules:
  0.0 56.3 jit_solution(16118507203266297779)
XLA Ops:
  0.7 1.2 %first_pack.1 = (f32[8,128]{1,0:T(8,128)S(1)}, f32[8,128]{1,0:T(8,128)S(1)}, f32[64,2048]{1,0:T(8,128)S(1)}) custom-call(s32[1]{0:T(128)} %bitcast.group.group_ref, f32[64,1024]{1,0:T(8,128)} %e.3, f32[64,1024]{1,0:T(8,128)} %p.3, f32[8,64,2048]{2,1,0:T(8,128)} %v_right.1), custom_call_target="tpu_custom_call" | custom-call | tf_op jit(solution)/shard_map/first_pack/pallas_call | solution.py:440
  1.9 2.1 %collective-permute-start.8 = (f32[64,2048]{1,0:T(8,128)S(1)}, f32[64,2048]{1,0:T(8,128)S(1)}, u32[]{:S(2)}, u32[]{:S(2)}) collective-permute-start(f32[64,2048]{1,0:T(8,128)S(1)} %get-tuple-element.44), channel_id=1, source_target_pairs={{0,1},{1,0},{2,3},{3,2},{4,5},{5,4},{6,7},{7,6},{8,9},{9,8},{10,11... | collective-permute-start | bytes 1572872 | tf_op jit(solution)/shard_map/ppermute | solution.py:456
  4.1 2.5 %collective-permute-start.1 = (f32[8,128]{1,0:T(8,128)S(1)}, f32[8,128]{1,0:T(8,128)S(1)}, u32[]{:S(2)}, u32[]{:S(2)}) collective-permute-start(f32[8,128]{1,0:T(8,128)S(1)} %get-tuple-element.28), channel_id=1, source_target_pairs={{1,2},{3,4},{5,6},{7,0},{2,1},{4,3},{6,5},{0,7},{9,10},{11,12},{13... | collective-permute-start | bytes 12296 | tf_op jit(solution)/shard_map/ppermute | solution.py:457
  6.6 9.2 %collective-permute-done.seam = f32[8,128]{1,0:T(8,128)S(1)} collective-permute-done((f32[8,128]{1,0:T(8,128)S(1)}, f32[8,128]{1,0:T(8,128)S(1)}, u32[]{:S(2)}, u32[]{:S(2)}) %collective-permute-start) | collective-permute-done | bytes 4128 | tf_op jit(solution)/shard_map/ppermute | solution.py:455
  15.8 0.9 %collective-permute-done.1.outer = f32[8,128]{1,0:T(8,128)S(1)} collective-permute-done((f32[8,128]{1,0:T(8,128)S(1)}, f32[8,128]{1,0:T(8,128)S(1)}, u32[]{:S(2)}, u32[]{:S(2)}) %collective-permute-start.1) | collective-permute-done | bytes 4128 | tf_op jit(solution)/shard_map/ppermute | solution.py:457
  16.8 1.6 %collective-permute-start.2 = (f32[16,1280]{1,0:T(8,128)S(1)}, f32[16,1280]{1,0:T(8,128)S(1)}, u32[]{:S(2)}, u32[]{:S(2)}) collective-permute-start(f32[16,1280]{1,0:T(8,128)S(1)} %get-tuple-element.29), channel_id=1, source_target_pairs={{0,8},{8,16},{16,24},{24,0},{1,9},{9,17},{17,25},{25,1},{2,10},{10... | collective-permute-start | bytes 245768 | tf_op jit(solution)/shard_map/ppermute | solution.py:500
  18.3 2.1 %collective-permute-start.3 = (f32[16,1280]{1,0:T(8,128)S(1)}, f32[16,1280]{1,0:T(8,128)S(1)}, u32[]{:S(2)}, u32[]{:S(2)}) collective-permute-start(f32[16,1280]{1,0:T(8,128)S(1)} %get-tuple-element.30), channel_id=1, source_target_pairs={{0,24},{8,0},{16,8},{24,16},{1,25},{9,1},{17,9},{25,17},{2,26},{10... | collective-permute-start | bytes 245768 | tf_op jit(solution)/shard_map/ppermute | solution.py:501
  20.4 2.4 %collective-permute-done.2.north = f32[16,1280]{1,0:T(8,128)S(1)} collective-permute-done((f32[16,1280]{1,0:T(8,128)S(1)}, f32[16,1280]{1,0:T(8,128)S(1)}, u32[]{:S(2)}, u32[]{:S(2)}) %collective-permute-start.2) | collective-permute-done | bytes 81952 | tf_op jit(solution)/shard_map/ppermute | solution.py:500
  22.8 1.1 %collective-permute-done.3.south = f32[16,1280]{1,0:T(8,128)S(1)} collective-permute-done((f32[16,1280]{1,0:T(8,128)S(1)}, f32[16,1280]{1,0:T(8,128)S(1)}, u32[]{:S(2)}, u32[]{:S(2)}) %collective-permute-start.3) | collective-permute-done | bytes 81952 | tf_op jit(solution)/shard_map/ppermute | solution.py:501
  23.9 4.3 %surface.1 = (f32[64,1024]{1,0:T(8,128)}, f32[64,1024]{1,0:T(8,128)}, f32[72,1024]{1,0:T(8,128)S(1)}, f32[10,88,128]{2,1,0:T(8,128)S(1)}, f32[10,88,128]{2,1,0:T...) custom-call(s32[1]{0:T(128)} %bitcast.group.group_ref, f32[64,1024]{1,0:T(8,128)S(1)} %copy-done.2, ...), custom_call_target="tpu_custom_call" | custom-call | tf_op jit(solution)/shard_map/surface/pallas_call | solution.py:509
  28.2 1.5 %collective-permute-start.11 = (f32[64,1024]{1,0:T(8,128)}, f32[64,1024]{1,0:T(8,128)S(1)}, u32[]{:S(2)}, u32[]{:S(2)}) collective-permute-start(f32[64,1024]{1,0:T(8,128)} %get-tuple-element.25), channel_id=1, source_target_pairs={{0,1},{1,0},{2,3},{3,2},{4,5},{5,4},{6,7},{7,6},{8,9},{9,8},{10,11... | collective-permute-start | bytes 786440 | tf_op jit(solution)/shard_map/ppermute | solution.py:545
  29.7 0.2 lazy_pack.1
  29.9 2.8 %collective-permute-start.4 = (f32[8,128]{1,0:T(8,128)S(1)}, f32[8,128]{1,0:T(8,128)S(1)}, u32[]{:S(2)}, u32[]{:S(2)}) collective-permute-start(f32[8,128]{1,0:T(8,128)S(1)} %get-tuple-element.35), channel_id=1, source_target_pairs={{0,2},{2,4},{4,6},{6,0},{1,3},{3,5},{5,7},{7,1},{8,10},{10,12},{12... | collective-permute-start | bytes 12296 | tf_op jit(solution)/shard_map/ppermute | solution.py:524
  32.7 0.8 %collective-permute-done.4.x_left = f32[8,128]{1,0:T(8,128)S(1)} collective-permute-done((f32[8,128]{1,0:T(8,128)S(1)}, f32[8,128]{1,0:T(8,128)S(1)}, u32[]{:S(2)}, u32[]{:S(2)}) %collective-permute-start.4) | collective-permute-done | bytes 4128 | tf_op jit(solution)/shard_map/ppermute | solution.py:524
  33.5 0.8 %collective-permute-start.6 = (f32[8,2304]{1,0:T(8,128)S(1)}, f32[8,2304]{1,0:T(8,128)S(1)}, u32[]{:S(2)}, u32[]{:S(2)}) collective-permute-start(f32[8,2304]{1,0:T(8,128)S(1)} %get-tuple-element.38), channel_id=1, source_target_pairs={{0,8},{8,16},{16,24},{24,0},{1,9},{9,17},{17,25},{25,1},{2,10},{10... | collective-permute-start | bytes 221192 | tf_op jit(solution)/shard_map/ppermute | solution.py:522
  34.3 1.7 %collective-permute-done.5.x_right = f32[8,128]{1,0:T(8,128)S(1)} collective-permute-done((f32[8,128]{1,0:T(8,128)S(1)}, f32[8,128]{1,0:T(8,128)S(1)}, u32[]{:S(2)}, u32[]{:S(2)}) %collective-permute-start.5) | collective-permute-done | bytes 4128 | tf_op jit(solution)/shard_map/ppermute | solution.py:525
  36.0 2.3 %collective-permute-start.7 = (f32[8,2304]{1,0:T(8,128)S(1)}, f32[8,2304]{1,0:T(8,128)S(1)}, u32[]{:S(2)}, u32[]{:S(2)}) collective-permute-start(f32[8,2304]{1,0:T(8,128)S(1)} %get-tuple-element.39), channel_id=1, source_target_pairs={{0,24},{8,0},{16,8},{24,16},{1,25},{9,1},{17,9},{25,17},{2,26},{10... | collective-permute-start | bytes 221192 | tf_op jit(solution)/shard_map/ppermute | solution.py:523
  38.3 0.2 collective-permute-done.6.far_north
  38.5 2.2 %collective-permute-done.7.far_south = f32[8,2304]{1,0:T(8,128)S(1)} collective-permute-done((f32[8,2304]{1,0:T(8,128)S(1)}, f32[8,2304]{1,0:T(8,128)S(1)}, u32[]{:S(2)}, u32[]{:S(2)}) %collective-permute-start.7) | collective-permute-done | bytes 73760 | tf_op jit(solution)/shard_map/ppermute | solution.py:523
  40.8 0.9 %collective-permute-start.9 = (f32[8,1024]{1,0:T(8,128)S(1)}, f32[8,1024]{1,0:T(8,128)S(1)}, u32[]{:S(2)}, u32[]{:S(2)}) collective-permute-start(f32[8,1024]{1,0:T(8,128)S(1)} %rim_pack.1), channel_id=1, source_target_pairs={{0,1},{1,0},{2,3},{3,2},{4,5},{5,4},{6,7},{7,6},{8,9},{9,8},{10,11... | collective-permute-start | bytes 98312 | tf_op jit(solution)/shard_map/ppermute | solution.py:544
  41.7 4.5 %spread.1 = (f32[8,16,64,128]{3,2,1,0:T(8,128)S(1)}, f32[8,16,64,128]{3,2,1,0:T(8,128)S(1)}, f32[16,64,128]{2,1,0:T(8,128)S(1)}) custom-call(f32[8,18,80,128]{3,2,1,0:T(8,128)S(1)} %get-tuple-element.33.volume.old_volume, f32[18,80,128]{2,1,0:T(8,128)S(1)} %get-tuple-element.34.depth.old_depth, f32[8,128]{1,0:T(8,128)S(1)} %collective-permute-done.4.x_left, ...), custom_call_target="tpu_custom_call" | custom-call | tf_op jit(solution)/shard_map/spread/pallas_call | solution.py:526
  46.2 0.3 fill_rows.1
  46.5 8.2 %laplace.1 = (f32[8,64,2048]{2,1,0:T(8,128)}, f32[64,1024]{1,0:T(8,128)S(1)}, f32[3,64,1024]{2,1,0:T(8,128)S(1)}) custom-call(s32[1]{0:T(128)} %bitcast.group.group_ref, f32[8,18,80,128]{3,2,1,0:T(8,128)S(1)} %get-tuple-element.40.volume, f32[18,80,128]{2,1,0:T(8,128)S(1)} %get-tuple-element.41.depth, f32[8,16,64,128]{3,2,1,0:T(8,128)S(1)} %get-tuple-element.37.token.east, ...), custom_call_target="tpu_custom_call" | custom-call | tf_op jit(solution)/shard_map/laplace/pallas_call | solution.py:562
  54.6 1.6 %top.1 = f32[8,64,2048]{2,1,0:T(8,128)} custom-call(s32[1]{0:T(128)} %bitcast.group.group_ref, f32[8,64,2048]{2,1,0:T(8,128)} %get-tuple-element.48.before, f32[64,1024]{1,0:T(8,128)S(1)} %get-tuple-element.49.part, f32[3,64,1024]{2,1,0:T(8,128)S(1)} %get-tuple-element.50.coefficients, ...), custom_call_target="tpu_custom_call", output_to_operand_aliasing={{}: (1, {})} | custom-call | tf_op jit(solution)/shard_map/top/pallas_call | solution.py:581
  (17 shorter events, 0.3 us)
Async XLA Ops:
  0.6 16.0 %copy-start.2 = (f32[64,1024]{1,0:T(8,128)S(1)}, f32[64,1024]{1,0:T(8,128)}, u32[]{:S(2)}) copy-start(f32[64,1024]{1,0:T(8,128)} %e.3) | copy-start | bytes 786436
  0.6 16.0 %copy-start.3 = (f32[64,1024]{1,0:T(8,128)S(1)}, f32[64,1024]{1,0:T(8,128)}, u32[]{:S(2)}) copy-start(f32[64,1024]{1,0:T(8,128)} %p.3) | copy-start | bytes 786436
  0.7 23.2 %copy-start.1 = (s32[64,2048]{1,0:T(8,128)S(1)}, s32[64,2048]{1,0:T(8,128)}, u32[]{:S(2)}) copy-start(s32[64,2048]{1,0:T(8,128)} %s_right.1) | copy-start | bytes 1572868
  1.9 27.8 %copy-start = (f32[8,64,2048]{2,1,0:T(8,128)S(1)}, f32[8,64,2048]{2,1,0:T(8,128)}, u32[]{:S(2)}) copy-start(f32[8,64,2048]{2,1,0:T(8,128)} %v_right.1) | copy-start | bytes 12582916
  1.9 44.5 %collective-permute-start.8 = (f32[64,2048]{1,0:T(8,128)S(1)}, f32[64,2048]{1,0:T(8,128)S(1)}, u32[]{:S(2)}, u32[]{:S(2)}) collective-permute-start(f32[64,2048]{1,0:T(8,128)S(1)} %get-tuple-element.44), channel_id=1, source_target_pairs={{0,1},{1,0},{2,3},{3,2},{4,5},{5,4},{6,7},{7,6},{8,9},{9,8},{10,11... | collective-permute-start | bytes 1572872 | tf_op jit(solution)/shard_map/ppermute | solution.py:456
  4.1 11.8 %collective-permute-start = (f32[8,128]{1,0:T(8,128)S(1)}, f32[8,128]{1,0:T(8,128)S(1)}, u32[]{:S(2)}, u32[]{:S(2)}) collective-permute-start(f32[8,128]{1,0:T(8,128)S(1)} %get-tuple-element.27), channel_id=1, source_target_pairs={{0,1},{1,0},{2,3},{3,2},{4,5},{5,4},{6,7},{7,6},{8,9},{9,8},{10,11... | collective-permute-start | bytes 12296 | tf_op jit(solution)/shard_map/ppermute | solution.py:455
  4.1 12.5 %collective-permute-start.1 = (f32[8,128]{1,0:T(8,128)S(1)}, f32[8,128]{1,0:T(8,128)S(1)}, u32[]{:S(2)}, u32[]{:S(2)}) collective-permute-start(f32[8,128]{1,0:T(8,128)S(1)} %get-tuple-element.28), channel_id=1, source_target_pairs={{1,2},{3,4},{5,6},{7,0},{2,1},{4,3},{6,5},{0,7},{9,10},{11,12},{13... | collective-permute-start | bytes 12296 | tf_op jit(solution)/shard_map/ppermute | solution.py:457
  16.8 6.0 %collective-permute-start.2 = (f32[16,1280]{1,0:T(8,128)S(1)}, f32[16,1280]{1,0:T(8,128)S(1)}, u32[]{:S(2)}, u32[]{:S(2)}) collective-permute-start(f32[16,1280]{1,0:T(8,128)S(1)} %get-tuple-element.29), channel_id=1, source_target_pairs={{0,8},{8,16},{16,24},{24,0},{1,9},{9,17},{17,25},{25,1},{2,10},{10... | collective-permute-start | bytes 245768 | tf_op jit(solution)/shard_map/ppermute | solution.py:500
  18.3 5.6 %collective-permute-start.3 = (f32[16,1280]{1,0:T(8,128)S(1)}, f32[16,1280]{1,0:T(8,128)S(1)}, u32[]{:S(2)}, u32[]{:S(2)}) collective-permute-start(f32[16,1280]{1,0:T(8,128)S(1)} %get-tuple-element.30), channel_id=1, source_target_pairs={{0,24},{8,0},{16,8},{24,16},{1,25},{9,1},{17,9},{25,17},{2,26},{10... | collective-permute-start | bytes 245768 | tf_op jit(solution)/shard_map/ppermute | solution.py:501
  28.2 18.3 %collective-permute-start.10 = (f32[72,1024]{1,0:T(8,128)S(1)}, f32[72,1024]{1,0:T(8,128)S(1)}, u32[]{:S(2)}, u32[]{:S(2)}) collective-permute-start(f32[72,1024]{1,0:T(8,128)S(1)} %get-tuple-element.47), channel_id=1, source_target_pairs={{0,1},{1,0},{2,3},{3,2},{4,5},{5,4},{6,7},{7,6},{8,9},{9,8},{10,11... | collective-permute-start | bytes 884744 | tf_op jit(solution)/shard_map/ppermute | solution.py:521
  28.2 26.4 %collective-permute-start.11 = (f32[64,1024]{1,0:T(8,128)}, f32[64,1024]{1,0:T(8,128)S(1)}, u32[]{:S(2)}, u32[]{:S(2)}) collective-permute-start(f32[64,1024]{1,0:T(8,128)} %get-tuple-element.25), channel_id=1, source_target_pairs={{0,1},{1,0},{2,3},{3,2},{4,5},{5,4},{6,7},{7,6},{8,9},{9,8},{10,11... | collective-permute-start | bytes 786440 | tf_op jit(solution)/shard_map/ppermute | solution.py:545
  29.9 3.5 %collective-permute-start.4 = (f32[8,128]{1,0:T(8,128)S(1)}, f32[8,128]{1,0:T(8,128)S(1)}, u32[]{:S(2)}, u32[]{:S(2)}) collective-permute-start(f32[8,128]{1,0:T(8,128)S(1)} %get-tuple-element.35), channel_id=1, source_target_pairs={{0,2},{2,4},{4,6},{6,0},{1,3},{3,5},{5,7},{7,1},{8,10},{10,12},{12... | collective-permute-start | bytes 12296 | tf_op jit(solution)/shard_map/ppermute | solution.py:524
  32.7 3.3 %collective-permute-start.5 = (f32[8,128]{1,0:T(8,128)S(1)}, f32[8,128]{1,0:T(8,128)S(1)}, u32[]{:S(2)}, u32[]{:S(2)}) collective-permute-start(f32[8,128]{1,0:T(8,128)S(1)} %get-tuple-element.36), channel_id=1, source_target_pairs={{0,6},{2,0},{4,2},{6,4},{1,7},{3,1},{5,3},{7,5},{8,14},{10,8},{12,... | collective-permute-start | bytes 12296 | tf_op jit(solution)/shard_map/ppermute | solution.py:525
  33.5 5.0 %collective-permute-start.6 = (f32[8,2304]{1,0:T(8,128)S(1)}, f32[8,2304]{1,0:T(8,128)S(1)}, u32[]{:S(2)}, u32[]{:S(2)}) collective-permute-start(f32[8,2304]{1,0:T(8,128)S(1)} %get-tuple-element.38), channel_id=1, source_target_pairs={{0,8},{8,16},{16,24},{24,0},{1,9},{9,17},{17,25},{25,1},{2,10},{10... | collective-permute-start | bytes 221192 | tf_op jit(solution)/shard_map/ppermute | solution.py:522
  36.0 4.6 %collective-permute-start.7 = (f32[8,2304]{1,0:T(8,128)S(1)}, f32[8,2304]{1,0:T(8,128)S(1)}, u32[]{:S(2)}, u32[]{:S(2)}) collective-permute-start(f32[8,2304]{1,0:T(8,128)S(1)} %get-tuple-element.39), channel_id=1, source_target_pairs={{0,24},{8,0},{16,8},{24,16},{1,25},{9,1},{17,9},{25,17},{2,26},{10... | collective-permute-start | bytes 221192 | tf_op jit(solution)/shard_map/ppermute | solution.py:523
  40.8 5.7 %collective-permute-start.9 = (f32[8,1024]{1,0:T(8,128)S(1)}, f32[8,1024]{1,0:T(8,128)S(1)}, u32[]{:S(2)}, u32[]{:S(2)}) collective-permute-start(f32[8,1024]{1,0:T(8,128)S(1)} %rim_pack.1), channel_id=1, source_target_pairs={{0,1},{1,0},{2,3},{3,2},{4,5},{5,4},{6,7},{7,6},{8,9},{9,8},{10,11... | collective-permute-start | bytes 98312 | tf_op jit(solution)/shard_map/ppermute | solution.py:544

commit v3 on v2

--- a/solution.py
+++ b/solution.py
@@ -46,7 +46,24 @@
     whole.wait()
 
 
-def lazy_pack(v_top, v_bottom, v_left, v_right, s_top, s_bottom, s_left, s_right, up, down, to_right, to_left):
+def by_parity(odd, fill, first, second):
+    @pl.when(odd[0] == 0)
+    def _():
+        fill(first, second)
+
+    @pl.when(odd[0] == 1)
+    def _():
+        fill(second, first)
+
+
+def lazy_pack(
+    odd_x, odd_y, v_top, v_bottom, v_left, v_right, s_top, s_bottom, s_left, s_right, row_a, row_b, column_a, column_b
+):
+    by_parity(odd_x, functools.partial(pack_rows, v_top, v_bottom, s_top, s_bottom), row_a, row_b)
+    by_parity(odd_y, functools.partial(pack_columns, v_left, v_right, s_left, s_right), column_a, column_b)
+
+
+def pack_rows(v_top, v_bottom, s_top, s_bottom, up, down):
     layers, _, width = v_top.shape
     piece = width // SUBS
     for k in range(layers):
@@ -56,6 +73,10 @@
         part = slice(q * piece, (q + 1) * piece)
         up[q : q + 1, width:] = s_bottom[SUBS - 1 : SUBS, part].astype(jnp.float32) * depth_unit
         down[q : q + 1, width:] = s_top[0:1, part].astype(jnp.float32) * depth_unit
+
+
+def pack_columns(v_left, v_right, s_left, s_right, to_right, to_left):
+    layers = v_left.shape[0]
     to_right[...] = jnp.zeros_like(to_right)
     to_left[...] = jnp.zeros_like(to_left)
     for j in range(layers // 2):
@@ -76,8 +97,12 @@
     return left, right
 
 
-def row_pack(group, e_top, e_bottom, p_top, p_bottom, seam, outer, up, down):
+def row_pack(group, odd_x, e_top, e_bottom, p_top, p_bottom, seam, outer, row_a, row_b):
     left, right = side_blocks(group[0] == 0, seam[...], outer[...])
+    by_parity(odd_x, functools.partial(pack_surface_rows, left, right, e_top, e_bottom, p_top, p_bottom), row_a, row_b)
+
+
+def pack_surface_rows(left, right, e_top, e_bottom, p_top, p_bottom, up, down):
     rows = LANES // 2
     width = e_top.shape[1]
     for row, tops, bottoms in ((0, e_top, e_bottom), (SUBS, p_top, p_bottom)):
@@ -117,28 +142,28 @@
 
 
 def surface(
-    group, e, p, seam, outer, north, south, v, sea,
-    new_e, new_p, height, wide_e, wide_p, volume, depth, e0, p0, e1, p1, sems,
+    group, odd_x, e, p, seam, outer, row_a, row_b,
+    new_e, new_p, height, wide_e, wide_p, e0, p0, e1, p1,
 ):
     rows, width = e.shape
     low = group[0] == 0
-    copies = []
-    for t in range(v.shape[2] // LANES):
-        part = slice(t * LANES, (t + 1) * LANES)
-        into = volume.at[:, t + 1, SUBS : SUBS + rows, :]
-        copies.append(pltpu.make_async_copy(v.at[:, :, part], into, sems.at[t]))
-        copies[-1].start()
     left, right = side_blocks(low, seam[...], outer[...])
     tiles = width // LANES + 2
     inner = slice(SUBS, SUBS + rows)
-    for old, source, base in ((e0, e, 0), (p0, p, LANES // 2)):
-        half = SUBS if base else 0
-        for t in range(tiles):
-            part = slice(t * LANES, (t + 1) * LANES)
-            old[t, :SUBS, :] = north[half : half + SUBS, part]
-            old[t, SUBS + rows : 2 * SUBS + rows, :] = south[half : half + SUBS, part]
-            if 0 < t < tiles - 1:
-                old[t, inner, :] = source[:, (t - 1) * LANES : t * LANES]
+    fields = ((e0, e, 0), (p0, p, LANES // 2))
+
+    def ends(south, north):
+        for old, _, base in fields:
+            half = SUBS if base else 0
+            for t in range(tiles):
+                part = slice(t * LANES, (t + 1) * LANES)
+                old[t, :SUBS, :] = north[half : half + SUBS, part]
+                old[t, SUBS + rows : 2 * SUBS + rows, :] = south[half : half + SUBS, part]
+
+    by_parity(odd_x, ends, row_a, row_b)
+    for old, source, base in fields:
+        for t in range(1, tiles - 1):
+            old[t, inner, :] = source[:, (t - 1) * LANES : t * LANES]
         old[0, inner, :] = left[base : base + rows]
         old[tiles - 1, inner, :] = right[base : base + rows]
     blocks = rows // SUBS + 1
@@ -177,50 +202,63 @@
     left = jnp.concatenate([wide_e[0, inner, :], wide_p[0, inner, :]], 0).T[LANES - 1 :]
     right = jnp.concatenate([wide_e[tiles - 1, inner, :], wide_p[tiles - 1, inner, :]], 0).T[:1]
     height[rows + 4 : rows + 5, :LANES] = jnp.where(low, left, right)
-    for t in range(v.shape[2] // LANES):
-        depth[t + 1, inner, :] = sea[:, t * LANES : (t + 1) * LANES].astype(jnp.float32) * depth_unit
-    for copy in copies:
-        copy.wait()
-
-
-def rim_pack(group, far_north, far_south, x_left, x_right, rims):
+
+
+def rim_pack(group, odd_x, odd_y, far_a, far_b, x_a, x_b, after, rims):
+    del after
     low = group[0] == 0
-    layers = far_north.shape[0]
+    layers = far_a.shape[0]
     width = rims.shape[1]
     pairs = layers // 2
     rims[...] = jnp.zeros_like(rims)
-    for row, side in ((0, far_north), (2, far_south)):
-        for half in range(2):
-            part = slice(half * width, (half + 1) * width)
-            rims[row + half : row + half + 1, :] = jnp.where(low, side[layers - 1 : layers, part], side[0:1, part])
-    for lane, side in ((0, x_left), (LANES, x_right)):
-        top_pair = pltpu.roll(side[...], LANES // 2, 1)[pairs - 1 : pairs]
-        rims[4:5, lane : lane + LANES] = jnp.where(low, top_pair, side[0:1, :])
-
-
-def run_all(copies):
-    for copy in copies:
-        copy.start()
-    for copy in copies:
-        copy.wait()
-
-
-def spread(volume, depth, x_left, x_right, east, around, depth_y, left_sides, right_sides):
-    layers, tiles = volume.shape[0], volume.shape[1] - 2
-    rows = east.shape[2]
-    left = square(x_left[...], False).T
-    right = square(x_right[...], False).T
+
+    def rows(far_south, far_north):
+        for row, side in ((0, far_north), (2, far_south)):
+            for half in range(2):
+                part = slice(half * width, (half + 1) * width)
+                rims[row + half : row + half + 1, :] = jnp.where(low, side[layers - 1 : layers, part], side[0:1, part])
+
+    by_parity(odd_x, rows, far_a, far_b)
+
+    def columns(x_right, x_left):
+        for lane, side in ((0, x_left), (LANES, x_right)):
+            top_pair = pltpu.roll(side[...], LANES // 2, 1)[pairs - 1 : pairs]
+            rims[4:5, lane : lane + LANES] = jnp.where(low, top_pair, side[0:1, :])
+
+    by_parity(odd_y, columns, x_a, x_b)
+
+
+def spread(
+    odd_x, odd_y, v, sea, far_a, far_b, x_a, x_b, volume, depth, east, around, depth_y, left_sides, right_sides
+):
+    layers, rows, tile = v.shape
+    tiles = tile // LANES
+    even = odd_y[0] == 0
+    left = square(jnp.where(even, x_b[...], x_a[...]), False).T
+    right = square(jnp.where(even, x_a[...], x_b[...]), False).T
     half = LANES // 2
     for k in range(layers + 1):
         base = (k % 2) * half
         left_sides[k] = pltpu.roll(left, LANES - 1 - k // 2, 1)[base : base + rows]
         right_sides[k] = pltpu.roll(right, (LANES - k // 2) % LANES, 1)[base : base + rows]
-
-    def both(at, sides, t):
-        cur = at(t)
-        before = sides[0] if t == 0 else at(t - 1)
-        after = sides[1] if t == tiles - 1 else at(t + 1)
-        return cur, shift_lanes(before, cur, after, -1), shift_lanes(before, cur, after, 1)
+    piece = tile // SUBS // LANES
+
+    def ends(far_south, far_north):
+        for side, row in ((far_north, SUBS - 1), (far_south, SUBS + rows)):
+            for t in range(tiles):
+                for k in range(layers):
+                    volume[k, t, row : row + 1, :] = side[k : k + 1, t * LANES : (t + 1) * LANES]
+                q, start = t // piece, tile + (t % piece) * LANES
+                depth[t, row : row + 1, :] = side[q : q + 1, start : start + LANES]
+
+    by_parity(odd_x, ends, far_a, far_b)
+
+    def both(at, sides):
+        tile_of = [at(t) for t in range(tiles)]
+        padded = [sides[0]] + tile_of + [sides[1]]
+        for t in range(tiles):
+            before, cur, after = padded[t : t + 3]
+            yield t, cur, shift_lanes(before, cur, after, -1), shift_lanes(before, cur, after, 1)
 
     def layer(k, carry):
         def part(quarter, inner_carry):
@@ -229,8 +267,8 @@
                 here = pl.ds(pl.multiple_of(row + SUBS, SUBS), SUBS)
                 spot = pl.ds(row, SUBS)
                 sides = left_sides[k, spot, :], right_sides[k, spot, :]
-                for t in range(tiles):
-                    cur, west, far = both(lambda c: volume[k, c + 1, here, :], sides, t)
+                for t, cur, west, far in both(lambda c: v[k, spot, c * LANES : (c + 1) * LANES], sides):
+                    volume[k, t, here, :] = cur
                     east[k, t, spot, :] = far - west
                     around[k, t, spot, :] = (far + west) - 4.0 * cur
             return inner_carry
@@ -239,65 +277,49 @@
 
     lax.fori_loop(0, layers, layer, 0)
 
-    def floor(block, carry):
-        row = pl.multiple_of(block * SUBS, SUBS)
-        here = pl.ds(pl.multiple_of(row + SUBS, SUBS), SUBS)
-        spot = pl.ds(row, SUBS)
-        sides = left_sides[layers, spot, :], right_sides[layers, spot, :]
-        for t in range(tiles):
-            _, west, far = both(lambda c: depth[c + 1, here, :], sides, t)
-            depth_y[t, spot, :] = far - west
+    def floor(pair, carry):
+        for step in range(2):
+            row = pl.multiple_of((pair * 2 + step) * SUBS, SUBS)
+            here = pl.ds(pl.multiple_of(row + SUBS, SUBS), SUBS)
+            spot = pl.ds(row, SUBS)
+            sides = left_sides[layers, spot, :], right_sides[layers, spot, :]
+            value = lambda c: sea[spot, c * LANES : (c + 1) * LANES].astype(jnp.float32) * depth_unit
+            for t, cur, west, far in both(value, sides):
+                depth[t, here, :] = cur
+                depth_y[t, spot, :] = far - west
         return carry
 
-    lax.fori_loop(0, rows // SUBS, floor, 0)
-
-
-def fill_rows(old_volume, old_depth, token, far_north, far_south, volume, depth, edges, depths, sems):
-    del old_volume, old_depth, token
-    layers, tiles, tall = volume.shape[0], volume.shape[1], volume.shape[2]
-    tile = (tiles - 2) * LANES
-    piece = tile // SUBS // LANES
-    for end, source, row in ((0, far_north, SUBS - 1), (1, far_south, 0)):
-        for t in range(tiles - 2):
-            for k in range(layers):
-                edges[end, k, t + 1, row : row + 1, :] = source[k : k + 1, t * LANES : (t + 1) * LANES]
-            q, start = t // piece, tile + (t % piece) * LANES
-            depths[end, t + 1, row : row + 1, :] = source[q : q + 1, start : start + LANES]
-    copies = []
-    for end, rows in ((0, slice(0, SUBS)), (1, slice(tall - SUBS, tall))):
-        copies.append(pltpu.make_async_copy(edges.at[end], volume.at[:, :, rows, :], sems.at[2 * end]))
-        copies.append(pltpu.make_async_copy(depths.at[end], depth.at[:, rows, :], sems.at[2 * end + 1]))
-    run_all(copies)
-
-
-def lanes_of(tile):
-    return pl.ds(pl.multiple_of((tile - 1) * LANES, LANES), LANES)
-
-
-def laplace(
-    total_layers, group_ref, volume, depth, east, around, depth_y, far_layer, rims, wide_e, wide_p, height,
+    lax.fori_loop(0, rows // SUBS // 2, floor, 0)
+
+
+def own_half(
+    total_layers, group_ref, volume, depth, east, around, depth_y, far_layer, rims, wide_e, wide_p, out, ghost
+):
+    group = group_ref[0]
+
+    @pl.when(pl.program_id(0) == 0)
+    def _():
+        fill_ghost(group == 0, group, far_layer, rims, ghost)
+
+    apply_half(
+        total_layers, group, group, volume, depth, east, around, depth_y, wide_e, wide_p, ghost, out, None, None
+    )
+
+
+def other_half(
+    total_layers, group_ref, before, volume, depth, east, around, depth_y, far_layer, rims, wide_e, height,
     out, part, coefficients, ghost, other_e,
 ):
-    block = pl.program_id(0)
+    del before
     group = group_ref[0]
     low = group == 0
-    layers = volume.shape[0]
-    rows, tile = far_layer.shape
-    width = tile // 2
-    tiles, halves = tile // LANES, width // LANES
+    rows, width = other_e.shape[1] - 2 * SUBS, height.shape[1]
+    halves = width // LANES
     inner = slice(SUBS, SUBS + rows)
 
-    @pl.when(block == 0)
+    @pl.when(pl.program_id(0) == 0)
     def _():
-        far_left = pltpu.roll(square(rims[:, :LANES], False).T, LANES - 5, 1)[:rows]
-        far_right = pltpu.roll(square(rims[:, LANES : 2 * LANES], False).T, LANES - 4, 1)[:rows]
-        ghost[0, inner, :] = far_left
-        ghost[tiles + 1, inner, :] = far_right
-        for t in range(tiles):
-            ghost[t + 1, inner, :] = far_layer[:, t * LANES : (t + 1) * LANES]
-            half, spot = t // halves, slice((t % halves) * LANES, (t % halves + 1) * LANES)
-            ghost[t + 1, SUBS - 1 : SUBS, :] = rims[half : half + 1, spot]
-            ghost[t + 1, SUBS + rows : SUBS + rows + 1, :] = rims[2 + half : 3 + half, spot]
+        fill_ghost(group == 1, 1 - group, far_layer, rims, ghost)
         for t in range(halves):
             spot = slice(t * LANES, (t + 1) * LANES)
             other_e[t + 1, inner, :] = height[:rows, spot]
@@ -308,6 +330,36 @@
         other_e[0, inner, :] = jnp.where(low, wide_e[halves, inner, :], at_left)
         other_e[halves + 1, inner, :] = jnp.where(low, at_right, wide_e[1, inner, :])
 
+    apply_half(
+        total_layers, group, 1 - group, volume, depth, east, around, depth_y, other_e, None, ghost, out, part,
+        coefficients,
+    )
+
+
+def fill_ghost(first, half, far_layer, rims, ghost):
+    rows, tile = far_layer.shape
+    width = tile // 2
+    halves = width // LANES
+    inner = slice(SUBS, SUBS + rows)
+    far_left = pltpu.roll(square(rims[:, :LANES], False).T, LANES - 5, 1)[:rows]
+    far_right = pltpu.roll(square(rims[:, LANES : 2 * LANES], False).T, LANES - 4, 1)[:rows]
+    ghost[0, inner, :] = jnp.where(first, far_left, far_layer[:, width - LANES : width])
+    ghost[halves + 1, inner, :] = jnp.where(first, far_layer[:, width : width + LANES], far_right)
+    for t in range(halves):
+        spot = slice(t * LANES, (t + 1) * LANES)
+        lanes = pl.ds(pl.multiple_of(half * width + t * LANES, LANES), LANES)
+        ghost[t + 1, inner, :] = far_layer[:, lanes]
+        ghost[t + 1, SUBS - 1 : SUBS, :] = jnp.where(first, rims[0:1, spot], rims[1:2, spot])
+        ghost[t + 1, SUBS + rows : SUBS + rows + 1, :] = jnp.where(first, rims[2:3, spot], rims[3:4, spot])
+
+
+def apply_half(
+    total_layers, group, half, volume, depth, east, around, depth_y, heights, mine, ghost, out, part, coefficients
+):
+    block = pl.program_id(0)
+    low = group == 0
+    layers = volume.shape[0]
+    halves = volume.shape[1] // 2
     spacing = 1.0 / total_layers
     sigma = (group * layers).astype(jnp.float32) * spacing + 0.5 * spacing
     gain = (2 * group).astype(jnp.float32)
@@ -322,7 +374,8 @@
 
     def apply_tile(t, heights, local, mine):
         at = lambda ref, step: ref[t, pl.ds(here + step, SUBS), :]
-        d, d_x, d_y = at(depth, 0), at(depth, 1) - at(depth, -1), depth_y[t - 1, spot, :]
+        local_lanes = pl.ds(pl.multiple_of((local - 1) * LANES, LANES), LANES)
+        d, d_x, d_y = at(depth, 0), at(depth, 1) - at(depth, -1), depth_y[t, spot, :]
         h, h_x, h_y = differences(heights, local)
         inverse = 1.0 / (d + h)
         scale = (0.25 / spacing) * inverse
@@ -338,9 +391,9 @@
         def level(k):
             at = lambda step: volume[k, t, pl.ds(here + step, SUBS), :]
             up, down = at(-1), at(1)
-            return at(0), down - up, east[k, t - 1, spot, :], (down + up) + around[k, t - 1, spot, :]
-
-        far = differences(ghost, t)
+            return at(0), down - up, east[k, t, spot, :], (down + up) + around[k, t, spot, :]
+
+        far = differences(ghost, local)
         this = level(0)
         lower = [jnp.where(low, a, b) for a, b in zip(this, far)]
         rise_below = this[0] - lower[0]
@@ -354,31 +407,24 @@
             rise = upper[0] - this[0]
             value = this[3] + ux * (upper[1] - lower[1]) + uy * (upper[2] - lower[2])
             value = value + weight * (rise - rise_below)
-            out[k, :, lanes_of(t)] = value
+            out[k, :, local_lanes] = value
             if k < layers - 1:
                 ux, uy = ux - bx, uy - by
                 weight, step = weight + step, step + bend
             elif mine is None:
-                part[:, lanes_of(local)] = value
-                coefficients[0, :, lanes_of(local)] = ux
-                coefficients[1, :, lanes_of(local)] = uy
-                coefficients[2, :, lanes_of(local)] = weight
+                part[:, local_lanes] = value
+                coefficients[0, :, local_lanes] = ux
+                coefficients[1, :, local_lanes] = uy
+                coefficients[2, :, local_lanes] = weight
             lower, this, rise_below = this, upper, rise
 
-    def own_pair(pair, carry):
+    def pair(index, carry):
         for step in range(2):
-            local = pair * 2 + step + 1
-            apply_tile(group * halves + local, wide_e, local, wide_p)
+            local = index * 2 + step + 1
+            apply_tile(half * halves + local - 1, heights, local, mine)
         return carry
 
-    def other_pair(pair, carry):
-        for step in range(2):
-            local = pair * 2 + step + 1
-            apply_tile((1 - group) * halves + local, other_e, local, None)
-        return carry
-
-    lax.fori_loop(0, halves // 2, own_pair, 0)
-    lax.fori_loop(0, halves // 2, other_pair, 0)
+    lax.fori_loop(0, halves // 2, pair, 0)
 
 
 def top(group_ref, before, part, coefficients, height, wide_p, other_p, out, potential):
@@ -413,9 +459,11 @@
     lax.fori_loop(0, rows // SUBS, body, 0)
 
 
-def ring(axis, step):
+def couples(axis, shifted):
     count = lax.axis_size(axis)
-    return [(i, (i + step) % count) for i in range(count)]
+    start = 1 if shifted else 0
+    one_way = [((i + start) % count, (i + start + 1) % count) for i in range(0, count, 2)]
+    return one_way + [(b, a) for a, b in one_way]
 
 
 def shards(elevation, surface_potential, seabed, interior_potential):
@@ -428,6 +476,9 @@
     shape = lambda *dims: jax.ShapeDtypeStruct(dims, f32)
     whole = lambda *dims: pl.BlockSpec(dims, lambda *_: (0,) * len(dims))
     group = lax.axis_index("gz").astype(jnp.int32).reshape((1,))
+    odd_x = (lax.axis_index("gx") & 1).astype(jnp.int32).reshape((1,))
+    odd_y = (lax.axis_index("gy") & 1).astype(jnp.int32).reshape((1,))
+    assert lax.axis_size("gx") % 2 == 0 and lax.axis_size("gy") % 2 == 0
     scalar = pl.BlockSpec(memory_space=pltpu.SMEM)
     last_row, last_tile = rows // SUBS - 1, tile // LANES - 1
 
@@ -460,11 +511,13 @@
     tall = rows + 2 * SUBS
     tables = (shape(layers, tiles + 2, tall, LANES), shape(tiles + 2, tall, LANES))
     anywhere = pl.BlockSpec(memory_space=pl.ANY)
-    up, down, to_right, to_left = pl.pallas_call(
+    far_a, far_b, x_a, x_b = pl.pallas_call(
         lazy_pack,
         out_shape=(shape(SUBS, tile + tile // SUBS),) * 2 + (shape(SUBS, LANES),) * 2,
         grid=(1,),
         in_specs=[
+            scalar,
+            scalar,
             block((layers, SUBS, tile), 0, 0, 0),
             block((layers, SUBS, tile), 0, last_row, 0),
             block((layers, rows, LANES), 0, 0, 0),
@@ -477,14 +530,15 @@
         out_specs=[whole(SUBS, tile + tile // SUBS)] * 2 + [whole(SUBS, LANES)] * 2,
         compiler_params=params,
         name="lazy_pack",
-    )(*(interior_potential,) * 4, *(seabed,) * 4)
+    )(odd_x, odd_y, *(pltpu.with_memory_space_constraint(interior_potential, pltpu.HBM),) * 4, *(seabed,) * 4)
 
     wide = width + 2 * LANES
-    row_up, row_down = pl.pallas_call(
+    row_a, row_b = pl.pallas_call(
         row_pack,
         out_shape=(shape(2 * SUBS, wide),) * 2,
         grid=(1,),
         in_specs=[
+            scalar,
             scalar,
             block((SUBS, width), 0, 0),
             block((SUBS, width), last_row, 0),
@@ -496,88 +550,85 @@
         out_specs=[whole(2 * SUBS, wide)] * 2,
         compiler_params=params,
         name="row_pack",
-    )(group, elevation, elevation, surface_potential, surface_potential, seam, outer)
-    north = lax.ppermute(row_up, "gx", ring("gx", 1))
-    south = lax.ppermute(row_down, "gx", ring("gx", -1))
+    )(group, odd_x, elevation, elevation, surface_potential, surface_potential, seam, outer)
+    sides = {}
+    for name, value, axis, shifted in (
+        ("row_b", row_b, "gx", True), ("row_a", row_a, "gx", False), ("x_b", x_b, "gy", True),
+        ("x_a", x_a, "gy", False), ("far_b", far_b, "gx", True), ("far_a", far_a, "gx", False),
+    ):
+        sides[name] = lax.ppermute(value, axis, couples(axis, shifted))
 
     tiles = tile // LANES
     tall = rows + 2 * SUBS
-    tables = (shape(layers, tiles + 2, tall, LANES), shape(tiles + 2, tall, LANES))
     anywhere = pl.BlockSpec(memory_space=pl.ANY)
     deep = rows + 3 * SUBS
     padded = (width // LANES + 2, deep, LANES)
-    new_e, new_p, height, wide_e, wide_p, volume, depth = pl.pallas_call(
+    new_e, new_p, height, wide_e, wide_p = pl.pallas_call(
         surface,
-        out_shape=(shape(rows, width),) * 2 + (shape(rows + SUBS, width),) + (shape(*padded),) * 2 + tables,
-        in_specs=[scalar] + [vmem] * 6 + [hbm, vmem],
-        out_specs=[vmem] * 7,
-        scratch_shapes=[pltpu.VMEM(padded, f32)] * 4 + [pltpu.SemaphoreType.DMA((tiles,))],
+        out_shape=(shape(rows, width),) * 2 + (shape(rows + SUBS, width),) + (shape(*padded),) * 2,
+        in_specs=[scalar] * 2 + [vmem] * 6,
+        out_specs=[vmem] * 5,
+        scratch_shapes=[pltpu.VMEM(padded, f32)] * 4,
         compiler_params=params,
         name="surface",
-    )(
-        group, elevation, surface_potential, seam, outer, north, south,
-        pltpu.with_memory_space_constraint(interior_potential, pltpu.HBM), seabed,
-    )
-    far_height = lax.ppermute(height, flat, partner)
-    far_north = lax.ppermute(up, "gx", ring("gx", 1))
-    far_south = lax.ppermute(down, "gx", ring("gx", -1))
-    x_left = lax.ppermute(to_right, "gy", ring("gy", 1))
-    x_right = lax.ppermute(to_left, "gy", ring("gy", -1))
-    east, around, depth_y = pl.pallas_call(
-        spread,
-        out_shape=(shape(layers, tiles, rows, LANES),) * 2 + (shape(tiles, rows, LANES),),
-        in_specs=[vmem] * 4,
-        out_specs=[vmem] * 3,
-        scratch_shapes=[pltpu.VMEM((layers + 1, rows, LANES), f32)] * 2,
-        compiler_params=params,
-        name="spread",
-    )(volume, depth, x_left, x_right)
-    blocks = rows // SUBS
+    )(group, odd_x, elevation, surface_potential, seam, outer, sides["row_a"], sides["row_b"])
+    far_sides = [sides[name] for name in ("far_a", "far_b", "x_a", "x_b")]
     rims = pl.pallas_call(
         rim_pack,
         out_shape=shape(SUBS, width),
-        in_specs=[scalar] + [vmem] * 4,
+        in_specs=[scalar] * 3 + [vmem] * 4 + [anywhere],
         out_specs=vmem,
         compiler_params=params,
         name="rim_pack",
-    )(group, far_north, far_south, x_left, x_right)
+    )(group, odd_x, odd_y, *far_sides, height)
     far_rims = lax.ppermute(rims, flat, partner)
+    far_height = lax.ppermute(height, flat, partner)
     other_p = lax.ppermute(new_p, flat, partner)
-
-    volume, depth = pl.pallas_call(
-        fill_rows,
-        out_shape=tables,
-        in_specs=[anywhere] * 3 + [vmem] * 2,
-        out_specs=[anywhere] * 2,
-        scratch_shapes=[
-            pltpu.VMEM((2, layers, tiles + 2, SUBS, LANES), f32),
-            pltpu.VMEM((2, tiles + 2, SUBS, LANES), f32),
-            pltpu.SemaphoreType.DMA((4,)),
-        ],
-        input_output_aliases={0: 0, 1: 1},
-        compiler_params=params,
-        name="fill_rows",
-    )(volume, depth, east, far_north, far_south)
-
+    spread_shapes = (shape(layers, tiles, tall, LANES), shape(tiles, tall, LANES))
+    spread_shapes = spread_shapes + (shape(layers, tiles, rows, LANES),) * 2 + (shape(tiles, rows, LANES),)
+    volume, depth, east, around, depth_y = pl.pallas_call(
+        spread,
+        out_shape=spread_shapes,
+        in_specs=[scalar] * 2 + [vmem] * 6,
+        out_specs=[vmem] * 5,
+        scratch_shapes=[pltpu.VMEM((layers + 1, rows, LANES), f32)] * 2,
+        compiler_params=params,
+        name="spread",
+    )(odd_x, odd_y, interior_potential, seabed, *far_sides)
+    blocks = rows // SUBS
+    tables = (volume, depth, east, around, depth_y, far_layer, far_rims, wide_e)
+    ghost = pltpu.VMEM((width // LANES + 2, tall, LANES), f32)
+    partial = pl.pallas_call(
+        functools.partial(own_half, total_layers),
+        out_shape=shape(layers, rows, tile),
+        grid_spec=pltpu.PrefetchScalarGridSpec(
+            num_scalar_prefetch=1,
+            grid=(blocks,),
+            in_specs=[vmem] * 9,
+            out_specs=pl.BlockSpec((layers, SUBS, width), lambda i, g: (0, i, g[0])),
+            scratch_shapes=[ghost],
+        ),
+        compiler_params=params,
+        name="own_half",
+    )(group, *tables, wide_p)
     partial, part, coefficients = pl.pallas_call(
-        functools.partial(laplace, total_layers),
+        functools.partial(other_half, total_layers),
         out_shape=(shape(layers, rows, tile), shape(rows, width), shape(3, rows, width)),
-        grid=(blocks,),
-        in_specs=[scalar] + [vmem] * 10,
-        out_specs=[
-            pl.BlockSpec((layers, SUBS, tile), lambda i: (0, i, 0)),
-            pl.BlockSpec((SUBS, width), lambda i: (i, 0)),
-            pl.BlockSpec((3, SUBS, width), lambda i: (0, i, 0)),
-        ],
-        scratch_shapes=[
-            pltpu.VMEM((tiles + 2, tall, LANES), f32),
-            pltpu.VMEM((width // LANES + 2, tall, LANES), f32),
-        ],
-        compiler_params=params,
-        name="laplace",
-    )(
-        group, volume, depth, east, around, depth_y, far_layer, far_rims, wide_e, wide_p, far_height,
-    )
+        grid_spec=pltpu.PrefetchScalarGridSpec(
+            num_scalar_prefetch=1,
+            grid=(blocks,),
+            in_specs=[hbm] + [vmem] * 9,
+            out_specs=[
+                pl.BlockSpec((layers, SUBS, width), lambda i, g: (0, i, 1 - g[0])),
+                pl.BlockSpec((SUBS, width), lambda i, g: (i, 0)),
+                pl.BlockSpec((3, SUBS, width), lambda i, g: (0, i, 0)),
+            ],
+            scratch_shapes=[ghost] * 2,
+        ),
+        input_output_aliases={1: 0},
+        compiler_params=params,
+        name="other_half",
+    )(group, partial, *tables, far_height)
     result = pl.pallas_call(
         top,
         out_shape=shape(layers, rows, tile),

time: 57.3 us -> 61.1 us (1.066)
  Pallas kernels: 20.4 us -> 23.5 us
  waiting for transfers between devices: 18.3 us -> 20.1 us
  starting transfers between devices: 16.7 us -> 15.7 us
    ppermute x6, waiting for transfers between devices: 8.31 us -> 10.1 us  [shards(): sides[name] = lax.ppermute(value, axis, couples(axis, shifted))]
    pallas_call x3, Pallas kernels: 12.9 us -> 14.6 us  [the longest x1 5.19 us: shards(): pl.pallas_call(functools.partial(own_half, total_layers), out_shape=shape...]
    pallas_call x1, Pallas kernels: 0.23 us -> 1.77 us  [shards(): pl.pallas_call(lazy_pack, out_shape=(shape(SUBS, tile + tile // SUBS),) *...]
    ppermute x6, starting transfers between devices: 9.56 us -> 8.73 us  [shards(): sides[name] = lax.ppermute(value, axis, couples(axis, shifted))]
  transfers between devices with their start and end apart: 12 -> 12, of which waited for: 8 -> 5; matrix products, arithmetic and copies ran while one was open for 0% -> 0% of each run, Pallas kernels for 31% -> 34%
where the time goes in v3:
time: 61.1 us; the launch traced here: 60 us
  Pallas kernels  23.5 us (38%)
  waiting for transfers between devices  20.1 us (33%)
  starting transfers between devices  15.7 us (26%)
  between operations  0.72 us (1%)
    ppermute x6, waiting for transfers between devices, shards(): sides[name] = lax.ppermute(value, axis, couples(axis, shifted))  10.1 us
    ppermute x1, waiting for transfers between devices, shards(): seam = lax.ppermute(seam, flat, partner)  9.17 us
    ppermute x6, starting transfers between devices, shards(): sides[name] = lax.ppermute(value, axis, couples(axis, shifted))  8.73 us
    pallas_call x1, Pallas kernels, shards(): pl.pallas_call(functools.partial(own_half, total_layers), out_shape=shape...  5.19 us
    pallas_call x1, Pallas kernels, shards(): pl.pallas_call(functools.partial(other_half, total_layers), out_shape=(sh...  5.18 us
    pallas_call x1, Pallas kernels, shards(): pl.pallas_call(spread, out_shape=spread_shapes, in_specs=[scalar] * 2 + [...  4.26 us
    pallas_call x1, Pallas kernels, shards(): pl.pallas_call(surface, out_shape=(shape(rows, width),) * 2 + (shape(rows...  3.97 us
    ppermute x1, starting transfers between devices, shards(): outer = lax.ppermute(outer, flat, across)  2.51 us
  transfers between devices with their start and end apart: 12, of which 5 were waited for; matrix products, arithmetic and copies ran while one was open for 0% of the time, Pallas kernels for 34%

profile of v3, /device:TPU:1, one launch (start us, length us, event | category | flops | bytes accessed | tf_op | source)
XLA Modules:
  0.0 60.0 jit_solution(8361959213672903141)
XLA Ops:
  0.7 1.2 %first_pack.1 = (f32[8,128]{1,0:T(8,128)S(1)}, f32[8,128]{1,0:T(8,128)S(1)}, f32[64,2048]{1,0:T(8,128)S(1)}) custom-call(s32[1]{0:T(128)} %bitcast.group.group_ref, f32[64,1024]{1,0:T(8,128)} %e.3, f32[64,1024]{1,0:T(8,128)} %p.3, f32[8,64,2048]{2,1,0:T(8,128)} %v.3), custom_call_target="tpu_custom_call" | custom-call | tf_op jit(solution)/shard_map/first_pack/pallas_call | solution.py:491
  1.9 2.1 %collective-permute-start.8 = (f32[64,2048]{1,0:T(8,128)S(1)}, f32[64,2048]{1,0:T(8,128)S(1)}, u32[]{:S(2)}, u32[]{:S(2)}) collective-permute-start(f32[64,2048]{1,0:T(8,128)S(1)} %get-tuple-element.40), channel_id=1, source_target_pairs={{0,1},{1,0},{2,3},{3,2},{4,5},{5,4},{6,7},{7,6},{8,9},{9,8},{10,11... | collective-permute-start | bytes 1572872 | tf_op jit(solution)/shard_map/ppermute | solution.py:507
  4.1 2.5 %collective-permute-start.1 = (f32[8,128]{1,0:T(8,128)S(1)}, f32[8,128]{1,0:T(8,128)S(1)}, u32[]{:S(2)}, u32[]{:S(2)}) collective-permute-start(f32[8,128]{1,0:T(8,128)S(1)} %get-tuple-element.26), channel_id=1, source_target_pairs={{1,2},{3,4},{5,6},{7,0},{2,1},{4,3},{6,5},{0,7},{9,10},{11,12},{13... | collective-permute-start | bytes 12296 | tf_op jit(solution)/shard_map/ppermute | solution.py:508
  6.6 9.2 %collective-permute-done.seam = f32[8,128]{1,0:T(8,128)S(1)} collective-permute-done((f32[8,128]{1,0:T(8,128)S(1)}, f32[8,128]{1,0:T(8,128)S(1)}, u32[]{:S(2)}, u32[]{:S(2)}) %collective-permute-start) | collective-permute-done | bytes 4128 | tf_op jit(solution)/shard_map/ppermute | solution.py:506
  15.8 0.9 %collective-permute-done.1.outer = f32[8,128]{1,0:T(8,128)S(1)} collective-permute-done((f32[8,128]{1,0:T(8,128)S(1)}, f32[8,128]{1,0:T(8,128)S(1)}, u32[]{:S(2)}, u32[]{:S(2)}) %collective-permute-start.1) | collective-permute-done | bytes 4128 | tf_op jit(solution)/shard_map/ppermute | solution.py:508
  16.7 0.1 row_pack.1
  16.8 1.6 %collective-permute-start.2 = (f32[16,1280]{1,0:T(8,128)S(1)}, f32[16,1280]{1,0:T(8,128)S(1)}, u32[]{:S(2)}, u32[]{:S(2)}) collective-permute-start(f32[16,1280]{1,0:T(8,128)S(1)} %get-tuple-element.27), channel_id=1, source_target_pairs={{0,8},{16,24},{8,0},{24,16},{1,9},{17,25},{9,1},{25,17},{2,10},{18... | collective-permute-start | bytes 245768 | tf_op jit(solution)/shard_map/ppermute | solution.py:559
  18.4 2.2 %collective-permute-start.3 = (f32[16,1280]{1,0:T(8,128)S(1)}, f32[16,1280]{1,0:T(8,128)S(1)}, u32[]{:S(2)}, u32[]{:S(2)}) collective-permute-start(f32[16,1280]{1,0:T(8,128)S(1)} %get-tuple-element.28), channel_id=1, source_target_pairs={{8,16},{24,0},{16,8},{0,24},{9,17},{25,1},{17,9},{1,25},{10,18},{2... | collective-permute-start | bytes 245768 | tf_op jit(solution)/shard_map/ppermute | solution.py:559
  20.6 4.1 %collective-permute-done.3.row_b = f32[16,1280]{1,0:T(8,128)S(1)} collective-permute-done((f32[16,1280]{1,0:T(8,128)S(1)}, f32[16,1280]{1,0:T(8,128)S(1)}, u32[]{:S(2)}, u32[]{:S(2)}) %collective-permute-start.3) | collective-permute-done | bytes 81952 | tf_op jit(solution)/shard_map/ppermute | solution.py:559
  24.6 4.0 %surface.1 = (f32[64,1024]{1,0:T(8,128)}, f32[64,1024]{1,0:T(8,128)}, f32[72,1024]{1,0:T(8,128)S(1)}, f32[10,88,128]{2,1,0:T(8,128)S(1)}, f32[10,88,128]{2,1,0:T(8,128)S(1)}) custom-call(s32[1]{0:T(128)} %bitcast.group.group_ref, s32[1]{0:T(128)} %bitcast.1.odd_x, f32[64,1024]{1,0:T(8,128)S(1)} %copy-done.2, f32[64,1024]{1,0:T(8,128)S(1)} %copy-done.3, ...), custom_call_target="tpu_custom_call" | custom-call | tf_op jit(solution)/shard_map/surface/pallas_call | solution.py:566
  28.6 1.5 %collective-permute-start.11 = (f32[64,1024]{1,0:T(8,128)}, f32[64,1024]{1,0:T(8,128)S(1)}, u32[]{:S(2)}, u32[]{:S(2)}) collective-permute-start(f32[64,1024]{1,0:T(8,128)} %get-tuple-element.23), channel_id=1, source_target_pairs={{0,1},{1,0},{2,3},{3,2},{4,5},{5,4},{6,7},{7,6},{8,9},{9,8},{10,11... | collective-permute-start | bytes 786440 | tf_op jit(solution)/shard_map/ppermute | solution.py:586
  30.1 1.8 %lazy_pack.1 = (f32[8,2304]{1,0:T(8,128)S(1)}, f32[8,2304]{1,0:T(8,128)S(1)}, f32[8,128]{1,0:T(8,128)S(1)}, f32[8,128]{1,0:T(8,128)S(1)}) custom-call(s32[1]{0:T(128)} %bitcast.1.odd_x, s32[1]{0:T(128)} %bitcast.2.odd_y, f32[8,64,2048]{2,1,0:T(8,128)} %v.3, f32[8,64,2048]{2,1,0:T(8,128)} %v.3, f32[8,64,2048]{2,1,0:T(8,128)} %v.3, f32[8,64,2048]{2,1,0:T(8,128)} %v.3, ...), custom_call_target="tpu_custom_call" | custom-call | tf_op jit(solution)/shard_map/lazy_pack/pallas_call | solution.py:514
  31.9 1.8 %collective-permute-start.6 = (f32[8,128]{1,0:T(8,128)S(1)}, f32[8,128]{1,0:T(8,128)S(1)}, u32[]{:S(2)}, u32[]{:S(2)}) collective-permute-start(f32[8,128]{1,0:T(8,128)S(1)} %get-tuple-element.33), channel_id=1, source_target_pairs={{0,2},{4,6},{2,0},{6,4},{1,3},{5,7},{3,1},{7,5},{8,10},{12,14},{10... | collective-permute-start | bytes 12296 | tf_op jit(solution)/shard_map/ppermute | solution.py:559
  33.7 1.2 %collective-permute-start.7 = (f32[8,128]{1,0:T(8,128)S(1)}, f32[8,128]{1,0:T(8,128)S(1)}, u32[]{:S(2)}, u32[]{:S(2)}) collective-permute-start(f32[8,128]{1,0:T(8,128)S(1)} %get-tuple-element.34), channel_id=1, source_target_pairs={{2,4},{6,0},{4,2},{0,6},{3,5},{7,1},{5,3},{1,7},{10,12},{14,8},{12... | collective-permute-start | bytes 12296 | tf_op jit(solution)/shard_map/ppermute | solution.py:559
  34.8 0.3 collective-permute-start.4
  35.1 1.8 %collective-permute-done.7.x_b = f32[8,128]{1,0:T(8,128)S(1)} collective-permute-done((f32[8,128]{1,0:T(8,128)S(1)}, f32[8,128]{1,0:T(8,128)S(1)}, u32[]{:S(2)}, u32[]{:S(2)}) %collective-permute-start.7) | collective-permute-done | bytes 4128 | tf_op jit(solution)/shard_map/ppermute | solution.py:559
  37.0 1.7 %collective-permute-start.5 = (f32[8,2304]{1,0:T(8,128)S(1)}, f32[8,2304]{1,0:T(8,128)S(1)}, u32[]{:S(2)}, u32[]{:S(2)}) collective-permute-start(f32[8,2304]{1,0:T(8,128)S(1)} %get-tuple-element.32), channel_id=1, source_target_pairs={{8,16},{24,0},{16,8},{0,24},{9,17},{25,1},{17,9},{1,25},{10,18},{2... | collective-permute-start | bytes 221192 | tf_op jit(solution)/shard_map/ppermute | solution.py:559
  38.7 4.2 %collective-permute-done.5.far_b = f32[8,2304]{1,0:T(8,128)S(1)} collective-permute-done((f32[8,2304]{1,0:T(8,128)S(1)}, f32[8,2304]{1,0:T(8,128)S(1)}, u32[]{:S(2)}, u32[]{:S(2)}) %collective-permute-start.5) | collective-permute-done | bytes 73760 | tf_op jit(solution)/shard_map/ppermute | solution.py:559
  42.8 0.1 rim_pack.1
  42.9 0.8 %collective-permute-start.9 = (f32[8,1024]{1,0:T(8,128)S(1)}, f32[8,1024]{1,0:T(8,128)S(1)}, u32[]{:S(2)}, u32[]{:S(2)}) collective-permute-start(f32[8,1024]{1,0:T(8,128)S(1)} %rim_pack.1), channel_id=1, source_target_pairs={{0,1},{1,0},{2,3},{3,2},{4,5},{5,4},{6,7},{7,6},{8,9},{9,8},{10,11... | collective-permute-start | bytes 98312 | tf_op jit(solution)/shard_map/ppermute | solution.py:584
  43.7 4.3 %spread.1 = (f32[8,16,80,128]{3,2,1,0:T(8,128)S(1)}, f32[16,80,128]{2,1,0:T(8,128)S(1)}, f32[8,16,64,128]{3,2,1,0:T(8,128)S(1)}, f32[8,16,64,128]{3,2,1,0:T(8,128)S(1)}, f32[16,64,128]{2,1,0:T(8,128)S(1)}) custom-call(s32[1]{0:T(128)} %bitcast.1.odd_x, s32[1]{0:T(128)} %bitcast.2.odd_y, f32[8,64,2048]{2,1,0:T(8,128)S(1)} %copy-done, ...), custom_call_target="tpu_custom_call" | custom-call | tf_op jit(solution)/shard_map/spread/pallas_call | solution.py:589
  48.0 5.2 %own_half.1.before = f32[8,64,2048]{2,1,0:T(8,128)} custom-call(s32[1]{0:T(128)} %bitcast.group.group_ref, f32[8,16,80,128]{3,2,1,0:T(8,128)S(1)} %get-tuple-element.35.volume, f32[16,80,128]{2,1,0:T(8,128)S(1)} %get-tuple-element.36.depth, f32[8,16,64,128]{3,2,1,0:T(8,128)S(1)} %get-tuple-element.37.east, f32[8,16,64,128]{3,2,1,0:T(8,128)S(1)} %get-tuple-element.38.around, ...), custom_call_target="tpu_custom_call" | custom-call | tf_op jit(solution)/shard_map/own_half/pallas_call | solution.py:601
  53.2 5.2 %other_half.1 = (f32[8,64,2048]{2,1,0:T(8,128)}, f32[64,1024]{1,0:T(8,128)S(1)}, f32[3,64,1024]{2,1,0:T(8,128)S(1)}) custom-call(s32[1]{0:T(128)} %bitcast.group.group_ref, f32[8,64,2048]{2,1,0:T(8,128)} %own_half.1.before, f32[8,16,80,128]{3,2,1,0:T(8,128)S(1)} %get-tuple-element.35.volume, ...), custom_call_target="tpu_custom_call", output_to_operand_aliasing={{0}: (1, {})} | custom-call | tf_op jit(solution)/shard_map/other_half/pallas_call | solution.py:614
  58.4 1.6 %top.1 = f32[8,64,2048]{2,1,0:T(8,128)} custom-call(s32[1]{0:T(128)} %bitcast.group.group_ref, f32[8,64,2048]{2,1,0:T(8,128)} %get-tuple-element.44.before, f32[64,1024]{1,0:T(8,128)S(1)} %get-tuple-element.45.part, f32[3,64,1024]{2,1,0:T(8,128)S(1)} %get-tuple-element.46.coefficients, ...), custom_call_target="tpu_custom_call", output_to_operand_aliasing={{}: (1, {})} | custom-call | tf_op jit(solution)/shard_map/top/pallas_call | solution.py:632
  (17 shorter events, 0.1 us)
Async XLA Ops:
  0.6 16.0 %copy-start.2 = (f32[64,1024]{1,0:T(8,128)S(1)}, f32[64,1024]{1,0:T(8,128)}, u32[]{:S(2)}) copy-start(f32[64,1024]{1,0:T(8,128)} %e.3) | copy-start | bytes 786436
  0.6 16.0 %copy-start.3 = (f32[64,1024]{1,0:T(8,128)S(1)}, f32[64,1024]{1,0:T(8,128)}, u32[]{:S(2)}) copy-start(f32[64,1024]{1,0:T(8,128)} %p.3) | copy-start | bytes 786436
  0.7 29.4 %copy-start.1 = (s32[64,2048]{1,0:T(8,128)S(1)}, s32[64,2048]{1,0:T(8,128)}, u32[]{:S(2)}) copy-start(s32[64,2048]{1,0:T(8,128)} %sea.1) | copy-start | bytes 1572868
  1.9 46.1 %collective-permute-start.8 = (f32[64,2048]{1,0:T(8,128)S(1)}, f32[64,2048]{1,0:T(8,128)S(1)}, u32[]{:S(2)}, u32[]{:S(2)}) collective-permute-start(f32[64,2048]{1,0:T(8,128)S(1)} %get-tuple-element.40), channel_id=1, source_target_pairs={{0,1},{1,0},{2,3},{3,2},{4,5},{5,4},{6,7},{7,6},{8,9},{9,8},{10,11... | collective-permute-start | bytes 1572872 | tf_op jit(solution)/shard_map/ppermute | solution.py:507
  4.0 11.8 %collective-permute-start = (f32[8,128]{1,0:T(8,128)S(1)}, f32[8,128]{1,0:T(8,128)S(1)}, u32[]{:S(2)}, u32[]{:S(2)}) collective-permute-start(f32[8,128]{1,0:T(8,128)S(1)} %get-tuple-element.25), channel_id=1, source_target_pairs={{0,1},{1,0},{2,3},{3,2},{4,5},{5,4},{6,7},{7,6},{8,9},{9,8},{10,11... | collective-permute-start | bytes 12296 | tf_op jit(solution)/shard_map/ppermute | solution.py:506
  4.1 12.5 %collective-permute-start.1 = (f32[8,128]{1,0:T(8,128)S(1)}, f32[8,128]{1,0:T(8,128)S(1)}, u32[]{:S(2)}, u32[]{:S(2)}) collective-permute-start(f32[8,128]{1,0:T(8,128)S(1)} %get-tuple-element.26), channel_id=1, source_target_pairs={{1,2},{3,4},{5,6},{7,0},{2,1},{4,3},{6,5},{0,7},{9,10},{11,12},{13... | collective-permute-start | bytes 12296 | tf_op jit(solution)/shard_map/ppermute | solution.py:508
  16.8 3.8 %collective-permute-start.2 = (f32[16,1280]{1,0:T(8,128)S(1)}, f32[16,1280]{1,0:T(8,128)S(1)}, u32[]{:S(2)}, u32[]{:S(2)}) collective-permute-start(f32[16,1280]{1,0:T(8,128)S(1)} %get-tuple-element.27), channel_id=1, source_target_pairs={{0,8},{16,24},{8,0},{24,16},{1,9},{17,25},{9,1},{25,17},{2,10},{18... | collective-permute-start | bytes 245768 | tf_op jit(solution)/shard_map/ppermute | solution.py:559
  18.4 6.3 %collective-permute-start.3 = (f32[16,1280]{1,0:T(8,128)S(1)}, f32[16,1280]{1,0:T(8,128)S(1)}, u32[]{:S(2)}, u32[]{:S(2)}) collective-permute-start(f32[16,1280]{1,0:T(8,128)S(1)} %get-tuple-element.28), channel_id=1, source_target_pairs={{8,16},{24,0},{16,8},{0,24},{9,17},{25,1},{17,9},{1,25},{10,18},{2... | collective-permute-start | bytes 245768 | tf_op jit(solution)/shard_map/ppermute | solution.py:559
  28.6 24.6 %collective-permute-start.10 = (f32[72,1024]{1,0:T(8,128)S(1)}, f32[72,1024]{1,0:T(8,128)S(1)}, u32[]{:S(2)}, u32[]{:S(2)}) collective-permute-start(f32[72,1024]{1,0:T(8,128)S(1)} %get-tuple-element.41.after), channel_id=1, source_target_pairs={{0,1},{1,0},{2,3},{3,2},{4,5},{5,4},{6,7},{7,6},{8,9},{9,8},{10,11... | collective-permute-start | bytes 884744 | tf_op jit(solution)/shard_map/ppermute | solution.py:585
  28.6 29.8 %collective-permute-start.11 = (f32[64,1024]{1,0:T(8,128)}, f32[64,1024]{1,0:T(8,128)S(1)}, u32[]{:S(2)}, u32[]{:S(2)}) collective-permute-start(f32[64,1024]{1,0:T(8,128)} %get-tuple-element.23), channel_id=1, source_target_pairs={{0,1},{1,0},{2,3},{3,2},{4,5},{5,4},{6,7},{7,6},{8,9},{9,8},{10,11... | collective-permute-start | bytes 786440 | tf_op jit(solution)/shard_map/ppermute | solution.py:586
  30.1 13.6 %copy-start = (f32[8,64,2048]{2,1,0:T(8,128)S(1)}, f32[8,64,2048]{2,1,0:T(8,128)}, u32[]{:S(2)}) copy-start(f32[8,64,2048]{2,1,0:T(8,128)} %v.3) | copy-start | bytes 12582916
  31.9 3.0 %collective-permute-start.6 = (f32[8,128]{1,0:T(8,128)S(1)}, f32[8,128]{1,0:T(8,128)S(1)}, u32[]{:S(2)}, u32[]{:S(2)}) collective-permute-start(f32[8,128]{1,0:T(8,128)S(1)} %get-tuple-element.33), channel_id=1, source_target_pairs={{0,2},{4,6},{2,0},{6,4},{1,3},{5,7},{3,1},{7,5},{8,10},{12,14},{10... | collective-permute-start | bytes 12296 | tf_op jit(solution)/shard_map/ppermute | solution.py:559
  33.7 3.3 %collective-permute-start.7 = (f32[8,128]{1,0:T(8,128)S(1)}, f32[8,128]{1,0:T(8,128)S(1)}, u32[]{:S(2)}, u32[]{:S(2)}) collective-permute-start(f32[8,128]{1,0:T(8,128)S(1)} %get-tuple-element.34), channel_id=1, source_target_pairs={{2,4},{6,0},{4,2},{0,6},{3,5},{7,1},{5,3},{1,7},{10,12},{14,8},{12... | collective-permute-start | bytes 12296 | tf_op jit(solution)/shard_map/ppermute | solution.py:559
  34.8 3.8 %collective-permute-start.4 = (f32[8,2304]{1,0:T(8,128)S(1)}, f32[8,2304]{1,0:T(8,128)S(1)}, u32[]{:S(2)}, u32[]{:S(2)}) collective-permute-start(f32[8,2304]{1,0:T(8,128)S(1)} %get-tuple-element.31), channel_id=1, source_target_pairs={{0,8},{16,24},{8,0},{24,16},{1,9},{17,25},{9,1},{25,17},{2,10},{18... | collective-permute-start | bytes 221192 | tf_op jit(solution)/shard_map/ppermute | solution.py:559
  37.0 5.8 %collective-permute-start.5 = (f32[8,2304]{1,0:T(8,128)S(1)}, f32[8,2304]{1,0:T(8,128)S(1)}, u32[]{:S(2)}, u32[]{:S(2)}) collective-permute-start(f32[8,2304]{1,0:T(8,128)S(1)} %get-tuple-element.32), channel_id=1, source_target_pairs={{8,16},{24,0},{16,8},{0,24},{9,17},{25,1},{17,9},{1,25},{10,18},{2... | collective-permute-start | bytes 221192 | tf_op jit(solution)/shard_map/ppermute | solution.py:559
  42.9 5.1 %collective-permute-start.9 = (f32[8,1024]{1,0:T(8,128)S(1)}, f32[8,1024]{1,0:T(8,128)S(1)}, u32[]{:S(2)}, u32[]{:S(2)}) collective-permute-start(f32[8,1024]{1,0:T(8,128)S(1)} %rim_pack.1), channel_id=1, source_target_pairs={{0,1},{1,0},{2,3},{3,2},{4,5},{5,4},{6,7},{7,6},{8,9},{9,8},{10,11... | collective-permute-start | bytes 98312 | tf_op jit(solution)/shard_map/ppermute | solution.py:584

commit v4 on v3

--- a/solution.py
+++ b/solution.py
@@ -142,11 +142,17 @@
 
 
 def surface(
-    group, odd_x, e, p, seam, outer, row_a, row_b,
-    new_e, new_p, height, wide_e, wide_p, e0, p0, e1, p1,
+    group, odd_x, e, p, seam, outer, row_a, row_b, v, sea,
+    new_e, new_p, height, wide_e, wide_p, volume, depth, e0, p0, e1, p1, sems,
 ):
     rows, width = e.shape
     low = group[0] == 0
+    copies = []
+    for t in range(v.shape[2] // LANES):
+        part = slice(t * LANES, (t + 1) * LANES)
+        into = volume.at[:, t + 1, SUBS : SUBS + rows, :]
+        copies.append(pltpu.make_async_copy(v.at[:, :, part], into, sems.at[t]))
+        copies[-1].start()
     left, right = side_blocks(low, seam[...], outer[...])
     tiles = width // LANES + 2
     inner = slice(SUBS, SUBS + rows)
@@ -176,7 +182,7 @@
             p1[t, pl.ds(row, SUBS), :] = old_p + step_p
         return carry
 
-    lax.fori_loop(0, blocks, first, 0)
+    lax.fori_loop(0, blocks, first, 0, unroll=True)
 
     def second(block, carry):
         row = block * SUBS + SUBS - 1
@@ -188,7 +194,7 @@
             wide_p[t, pl.ds(row, SUBS), :] = 0.5 * ((old_p + one_p) + step_p)
         return carry
 
-    lax.fori_loop(0, blocks, second, 0)
+    lax.fori_loop(0, blocks, second, 0, unroll=True)
     for t in range(1, tiles - 1):
         part = slice((t - 1) * LANES, t * LANES)
         tile_e = wide_e[t, inner, :]
@@ -202,6 +208,10 @@
     left = jnp.concatenate([wide_e[0, inner, :], wide_p[0, inner, :]], 0).T[LANES - 1 :]
     right = jnp.concatenate([wide_e[tiles - 1, inner, :], wide_p[tiles - 1, inner, :]], 0).T[:1]
     height[rows + 4 : rows + 5, :LANES] = jnp.where(low, left, right)
+    for t in range(v.shape[2] // LANES):
+        depth[t + 1, inner, :] = sea[:, t * LANES : (t + 1) * LANES].astype(jnp.float32) * depth_unit
+    for copy in copies:
+        copy.wait()
 
 
 def rim_pack(group, odd_x, odd_y, far_a, far_b, x_a, x_b, after, rims):
@@ -228,96 +238,140 @@
     by_parity(odd_y, columns, x_a, x_b)
 
 
-def spread(
-    odd_x, odd_y, v, sea, far_a, far_b, x_a, x_b, volume, depth, east, around, depth_y, left_sides, right_sides
+def fill(
+    odd_x, odd_y, old_volume, old_depth, far_a, far_b, x_a, x_b, volume, depth, sides, depths, edges, ends, sems
 ):
-    layers, rows, tile = v.shape
-    tiles = tile // LANES
+    del old_volume, old_depth
+    layers, tiles, tall = volume.shape[0], volume.shape[1], volume.shape[2]
+    rows, tile = tall - 2 * SUBS, (tiles - 2) * LANES
+    inner = slice(SUBS, SUBS + rows)
     even = odd_y[0] == 0
     left = square(jnp.where(even, x_b[...], x_a[...]), False).T
     right = square(jnp.where(even, x_a[...], x_b[...]), False).T
-    half = LANES // 2
-    for k in range(layers + 1):
+    half, pairs = LANES // 2, layers // 2
+    for k in range(layers):
         base = (k % 2) * half
-        left_sides[k] = pltpu.roll(left, LANES - 1 - k // 2, 1)[base : base + rows]
-        right_sides[k] = pltpu.roll(right, (LANES - k // 2) % LANES, 1)[base : base + rows]
+        sides[0, k] = pltpu.roll(left, LANES - 1 - k // 2, 1)[base : base + rows]
+        sides[1, k] = pltpu.roll(right, (LANES - k // 2) % LANES, 1)[base : base + rows]
+    depths[0] = pltpu.roll(left, LANES - 1 - pairs, 1)[:rows]
+    depths[1] = pltpu.roll(right, LANES - pairs, 1)[:rows]
     piece = tile // SUBS // LANES
 
-    def ends(far_south, far_north):
-        for side, row in ((far_north, SUBS - 1), (far_south, SUBS + rows)):
-            for t in range(tiles):
+    def fill_ends(far_south, far_north):
+        for end, source, row in ((0, far_north, SUBS - 1), (1, far_south, 0)):
+            for t in range(tiles - 2):
                 for k in range(layers):
-                    volume[k, t, row : row + 1, :] = side[k : k + 1, t * LANES : (t + 1) * LANES]
+                    edges[end, k, t, row : row + 1, :] = source[k : k + 1, t * LANES : (t + 1) * LANES]
                 q, start = t // piece, tile + (t % piece) * LANES
-                depth[t, row : row + 1, :] = side[q : q + 1, start : start + LANES]
-
-    by_parity(odd_x, ends, far_a, far_b)
-
-    def both(at, sides):
-        tile_of = [at(t) for t in range(tiles)]
-        padded = [sides[0]] + tile_of + [sides[1]]
-        for t in range(tiles):
-            before, cur, after = padded[t : t + 3]
-            yield t, cur, shift_lanes(before, cur, after, -1), shift_lanes(before, cur, after, 1)
-
-    def layer(k, carry):
-        def part(quarter, inner_carry):
-            for step in range(4):
-                row = pl.multiple_of((quarter * 4 + step) * SUBS, SUBS)
-                here = pl.ds(pl.multiple_of(row + SUBS, SUBS), SUBS)
-                spot = pl.ds(row, SUBS)
-                sides = left_sides[k, spot, :], right_sides[k, spot, :]
-                for t, cur, west, far in both(lambda c: v[k, spot, c * LANES : (c + 1) * LANES], sides):
-                    volume[k, t, here, :] = cur
-                    east[k, t, spot, :] = far - west
-                    around[k, t, spot, :] = (far + west) - 4.0 * cur
-            return inner_carry
-
-        return lax.fori_loop(0, rows // SUBS // 4, part, carry)
-
-    lax.fori_loop(0, layers, layer, 0)
-
-    def floor(pair, carry):
-        for step in range(2):
-            row = pl.multiple_of((pair * 2 + step) * SUBS, SUBS)
-            here = pl.ds(pl.multiple_of(row + SUBS, SUBS), SUBS)
-            spot = pl.ds(row, SUBS)
-            sides = left_sides[layers, spot, :], right_sides[layers, spot, :]
-            value = lambda c: sea[spot, c * LANES : (c + 1) * LANES].astype(jnp.float32) * depth_unit
-            for t, cur, west, far in both(value, sides):
-                depth[t, here, :] = cur
-                depth_y[t, spot, :] = far - west
-        return carry
-
-    lax.fori_loop(0, rows // SUBS // 2, floor, 0)
-
-
-def own_half(
-    total_layers, group_ref, volume, depth, east, around, depth_y, far_layer, rims, wide_e, wide_p, out, ghost
-):
+                ends[end, t, row : row + 1, :] = source[q : q + 1, start : start + LANES]
+
+    by_parity(odd_x, fill_ends, far_a, far_b)
+    copies = []
+    for index, (t, at) in enumerate(((0, slice(0, SUBS)), (tiles - 1, slice(tall - SUBS, tall)))):
+        for source, target in (
+            (sides.at[index], volume.at[:, t, inner, :]),
+            (depths.at[index], depth.at[t, inner, :]),
+            (edges.at[index], volume.at[:, 1 : tiles - 1, at, :]),
+            (ends.at[index], depth.at[1 : tiles - 1, at, :]),
+        ):
+            copies.append(pltpu.make_async_copy(source, target, sems.at[len(copies)]))
+    for copy in copies:
+        copy.start()
+    for copy in copies:
+        copy.wait()
+
+
+def apply_tile(total_layers, group, block, volume, depth, t, heights, local, ghost, spot, mine, write, rest=None):
+    low = group == 0
+    layers = volume.shape[0]
+    spacing = 1.0 / total_layers
+    sigma = (group * layers).astype(jnp.float32) * spacing + 0.5 * spacing
+    gain = (2 * group).astype(jnp.float32)
+    here = pl.multiple_of((block + 1) * SUBS, SUBS)
+
+    def near(ref, t):
+        at = lambda column, step: ref[column, pl.ds(here + step, SUBS), :]
+        cur = at(t, 0)
+        left, right = at(t - 1, 0), at(t + 1, 0)
+        return cur, at(t, -1), at(t, 1), shift_lanes(left, cur, right, -1), shift_lanes(left, cur, right, 1)
+
+    def differences(ref, t):
+        p, up, down, left, right = near(ref, t)
+        return p, down - up, right - left
+
+    d, d_x, d_y = differences(depth, t)
+    h, h_x, h_y = differences(heights, local)
+    inverse = 1.0 / (d + h)
+    scale = (0.25 / spacing) * inverse
+    bx, by = scale * (d_x + h_x), scale * (d_y + h_y)
+    ux, uy = scale * d_x - sigma * bx, scale * d_y - sigma * by
+    bx, by = spacing * bx, spacing * by
+    scaled = inverse * (1.0 / spacing)
+    weight = 4.0 * (ux * ux + uy * uy) + scaled * scaled
+    bend = 4.0 * (bx * bx + by * by)
+    step = bend - 8.0 * (ux * bx + uy * by)
+    bend = bend + bend
+
+    def level(k):
+        p, up, down, left, right = near(volume.at[k], t)
+        return p, down - up, right - left, ((down + up) + (right + left)) - 4.0 * p
+
+    far = differences(ghost, spot)
+    this = level(0)
+    lower = [jnp.where(low, a, b) for a, b in zip(this, far)]
+    rise_below = this[0] - lower[0]
+    for k in range(layers):
+        if k < layers - 1:
+            upper = level(k + 1)
+        else:
+            upper = [jnp.where(low, a, -b) for a, b in zip(far, this)]
+            if mine is not None:
+                upper = [a + gain * b for a, b in zip(upper, differences(mine, local))]
+        rise = upper[0] - this[0]
+        value = this[3] + ux * (upper[1] - lower[1]) + uy * (upper[2] - lower[2])
+        value = value + weight * (rise - rise_below)
+        write(k, value)
+        if k < layers - 1:
+            ux, uy = ux - bx, uy - by
+            weight, step = weight + step, step + bend
+        elif rest is not None:
+            rest(value, ux, uy, weight)
+        lower, this, rise_below = this, upper, rise
+
+
+def own_half(total_layers, group_ref, volume, depth, far_layer, rims, wide_e, wide_p, out, ghost):
+    block = pl.program_id(0)
     group = group_ref[0]
-
-    @pl.when(pl.program_id(0) == 0)
+    halves = volume.shape[1] // 2 - 1
+
+    @pl.when(block == 0)
     def _():
         fill_ghost(group == 0, group, far_layer, rims, ghost)
 
-    apply_half(
-        total_layers, group, group, volume, depth, east, around, depth_y, wide_e, wide_p, ghost, out, None, None
-    )
+    for local in range(1, halves + 1):
+
+        def write(k, value):
+            out[k, :, (local - 1) * LANES : local * LANES] = value
+
+        apply_tile(
+            total_layers, group, block, volume, depth, group * halves + local, wide_e, local, ghost, local, wide_p,
+            write,
+        )
 
 
 def other_half(
-    total_layers, group_ref, before, volume, depth, east, around, depth_y, far_layer, rims, wide_e, height,
+    total_layers, group_ref, before, volume, depth, far_layer, rims, wide_e, height,
     out, part, coefficients, ghost, other_e,
 ):
     del before
+    block = pl.program_id(0)
     group = group_ref[0]
     low = group == 0
     rows, width = other_e.shape[1] - 2 * SUBS, height.shape[1]
     halves = width // LANES
     inner = slice(SUBS, SUBS + rows)
 
-    @pl.when(pl.program_id(0) == 0)
+    @pl.when(block == 0)
     def _():
         fill_ghost(group == 1, 1 - group, far_layer, rims, ghost)
         for t in range(halves):
@@ -330,10 +384,22 @@
         other_e[0, inner, :] = jnp.where(low, wide_e[halves, inner, :], at_left)
         other_e[halves + 1, inner, :] = jnp.where(low, at_right, wide_e[1, inner, :])
 
-    apply_half(
-        total_layers, group, 1 - group, volume, depth, east, around, depth_y, other_e, None, ghost, out, part,
-        coefficients,
-    )
+    for local in range(1, halves + 1):
+        spot = slice((local - 1) * LANES, local * LANES)
+
+        def write(k, value):
+            out[k, :, spot] = value
+
+        def rest(value, ux, uy, weight):
+            part[:, spot] = value
+            coefficients[0, :, spot] = ux
+            coefficients[1, :, spot] = uy
+            coefficients[2, :, spot] = weight
+
+        apply_tile(
+            total_layers, group, block, volume, depth, (1 - group) * halves + local, other_e, local, ghost, local,
+            None, write, rest,
+        )
 
 
 def fill_ghost(first, half, far_layer, rims, ghost):
@@ -351,80 +417,6 @@
         ghost[t + 1, inner, :] = far_layer[:, lanes]
         ghost[t + 1, SUBS - 1 : SUBS, :] = jnp.where(first, rims[0:1, spot], rims[1:2, spot])
         ghost[t + 1, SUBS + rows : SUBS + rows + 1, :] = jnp.where(first, rims[2:3, spot], rims[3:4, spot])
-
-
-def apply_half(
-    total_layers, group, half, volume, depth, east, around, depth_y, heights, mine, ghost, out, part, coefficients
-):
-    block = pl.program_id(0)
-    low = group == 0
-    layers = volume.shape[0]
-    halves = volume.shape[1] // 2
-    spacing = 1.0 / total_layers
-    sigma = (group * layers).astype(jnp.float32) * spacing + 0.5 * spacing
-    gain = (2 * group).astype(jnp.float32)
-    row = pl.multiple_of(block * SUBS, SUBS)
-    here = pl.multiple_of((block + 1) * SUBS, SUBS)
-    spot = pl.ds(row, SUBS)
-
-    def differences(ref, t):
-        at = lambda column, step: ref[column, pl.ds(here + step, SUBS), :]
-        cur, left, right = at(t, 0), at(t - 1, 0), at(t + 1, 0)
-        return cur, at(t, 1) - at(t, -1), shift_lanes(left, cur, right, 1) - shift_lanes(left, cur, right, -1)
-
-    def apply_tile(t, heights, local, mine):
-        at = lambda ref, step: ref[t, pl.ds(here + step, SUBS), :]
-        local_lanes = pl.ds(pl.multiple_of((local - 1) * LANES, LANES), LANES)
-        d, d_x, d_y = at(depth, 0), at(depth, 1) - at(depth, -1), depth_y[t, spot, :]
-        h, h_x, h_y = differences(heights, local)
-        inverse = 1.0 / (d + h)
-        scale = (0.25 / spacing) * inverse
-        bx, by = scale * (d_x + h_x), scale * (d_y + h_y)
-        ux, uy = scale * d_x - sigma * bx, scale * d_y - sigma * by
-        bx, by = spacing * bx, spacing * by
-        scaled = inverse * (1.0 / spacing)
-        weight = 4.0 * (ux * ux + uy * uy) + scaled * scaled
-        bend = 4.0 * (bx * bx + by * by)
-        step = bend - 8.0 * (ux * bx + uy * by)
-        bend = bend + bend
-
-        def level(k):
-            at = lambda step: volume[k, t, pl.ds(here + step, SUBS), :]
-            up, down = at(-1), at(1)
-            return at(0), down - up, east[k, t, spot, :], (down + up) + around[k, t, spot, :]
-
-        far = differences(ghost, local)
-        this = level(0)
-        lower = [jnp.where(low, a, b) for a, b in zip(this, far)]
-        rise_below = this[0] - lower[0]
-        for k in range(layers):
-            if k < layers - 1:
-                upper = level(k + 1)
-            else:
-                upper = [jnp.where(low, a, -b) for a, b in zip(far, this)]
-                if mine is not None:
-                    upper = [a + gain * b for a, b in zip(upper, differences(mine, local))]
-            rise = upper[0] - this[0]
-            value = this[3] + ux * (upper[1] - lower[1]) + uy * (upper[2] - lower[2])
-            value = value + weight * (rise - rise_below)
-            out[k, :, local_lanes] = value
-            if k < layers - 1:
-                ux, uy = ux - bx, uy - by
-                weight, step = weight + step, step + bend
-            elif mine is None:
-                part[:, local_lanes] = value
-                coefficients[0, :, local_lanes] = ux
-                coefficients[1, :, local_lanes] = uy
-                coefficients[2, :, local_lanes] = weight
-            lower, this, rise_below = this, upper, rise
-
-    def pair(index, carry):
-        for step in range(2):
-            local = index * 2 + step + 1
-            apply_tile(half * halves + local - 1, heights, local, mine)
-        return carry
-
-    lax.fori_loop(0, halves // 2, pair, 0)
 
 
 def top(group_ref, before, part, coefficients, height, wide_p, other_p, out, potential):
@@ -561,17 +553,21 @@
     tiles = tile // LANES
     tall = rows + 2 * SUBS
     anywhere = pl.BlockSpec(memory_space=pl.ANY)
+    tables = (shape(layers, tiles + 2, tall, LANES), shape(tiles + 2, tall, LANES))
     deep = rows + 3 * SUBS
     padded = (width // LANES + 2, deep, LANES)
-    new_e, new_p, height, wide_e, wide_p = pl.pallas_call(
+    new_e, new_p, height, wide_e, wide_p, volume, depth = pl.pallas_call(
         surface,
-        out_shape=(shape(rows, width),) * 2 + (shape(rows + SUBS, width),) + (shape(*padded),) * 2,
-        in_specs=[scalar] * 2 + [vmem] * 6,
-        out_specs=[vmem] * 5,
-        scratch_shapes=[pltpu.VMEM(padded, f32)] * 4,
+        out_shape=(shape(rows, width),) * 2 + (shape(rows + SUBS, width),) + (shape(*padded),) * 2 + tables,
+        in_specs=[scalar] * 2 + [vmem] * 6 + [hbm, vmem],
+        out_specs=[vmem] * 7,
+        scratch_shapes=[pltpu.VMEM(padded, f32)] * 4 + [pltpu.SemaphoreType.DMA((tiles,))],
         compiler_params=params,
         name="surface",
-    )(group, odd_x, elevation, surface_potential, seam, outer, sides["row_a"], sides["row_b"])
+    )(
+        group, odd_x, elevation, surface_potential, seam, outer, sides["row_a"], sides["row_b"],
+        pltpu.with_memory_space_constraint(interior_potential, pltpu.HBM), seabed,
+    )
     far_sides = [sides[name] for name in ("far_a", "far_b", "x_a", "x_b")]
     rims = pl.pallas_call(
         rim_pack,
@@ -584,19 +580,24 @@
     far_rims = lax.ppermute(rims, flat, partner)
     far_height = lax.ppermute(height, flat, partner)
     other_p = lax.ppermute(new_p, flat, partner)
-    spread_shapes = (shape(layers, tiles, tall, LANES), shape(tiles, tall, LANES))
-    spread_shapes = spread_shapes + (shape(layers, tiles, rows, LANES),) * 2 + (shape(tiles, rows, LANES),)
-    volume, depth, east, around, depth_y = pl.pallas_call(
-        spread,
-        out_shape=spread_shapes,
-        in_specs=[scalar] * 2 + [vmem] * 6,
-        out_specs=[vmem] * 5,
-        scratch_shapes=[pltpu.VMEM((layers + 1, rows, LANES), f32)] * 2,
-        compiler_params=params,
-        name="spread",
-    )(odd_x, odd_y, interior_potential, seabed, *far_sides)
+    volume, depth = pl.pallas_call(
+        fill,
+        out_shape=tables,
+        in_specs=[scalar] * 2 + [anywhere] * 2 + [vmem] * 4,
+        out_specs=[anywhere] * 2,
+        scratch_shapes=[
+            pltpu.VMEM((2, layers, rows, LANES), f32),
+            pltpu.VMEM((2, rows, LANES), f32),
+            pltpu.VMEM((2, layers, tiles, SUBS, LANES), f32),
+            pltpu.VMEM((2, tiles, SUBS, LANES), f32),
+            pltpu.SemaphoreType.DMA((8,)),
+        ],
+        input_output_aliases={2: 0, 3: 1},
+        compiler_params=params,
+        name="fill",
+    )(odd_x, odd_y, volume, depth, *far_sides)
     blocks = rows // SUBS
-    tables = (volume, depth, east, around, depth_y, far_layer, far_rims, wide_e)
+    tables = (volume, depth, far_layer, far_rims, wide_e)
     ghost = pltpu.VMEM((width // LANES + 2, tall, LANES), f32)
     partial = pl.pallas_call(
         functools.partial(own_half, total_layers),
@@ -604,7 +605,7 @@
         grid_spec=pltpu.PrefetchScalarGridSpec(
             num_scalar_prefetch=1,
             grid=(blocks,),
-            in_specs=[vmem] * 9,
+            in_specs=[vmem] * 6,
             out_specs=pl.BlockSpec((layers, SUBS, width), lambda i, g: (0, i, g[0])),
             scratch_shapes=[ghost],
         ),
@@ -617,7 +618,7 @@
         grid_spec=pltpu.PrefetchScalarGridSpec(
             num_scalar_prefetch=1,
             grid=(blocks,),
-            in_specs=[hbm] + [vmem] * 9,
+            in_specs=[hbm] + [vmem] * 6,
             out_specs=[
                 pl.BlockSpec((layers, SUBS, width), lambda i, g: (0, i, 1 - g[0])),
                 pl.BlockSpec((SUBS, width), lambda i, g: (i, 0)),

time: 61.1 us -> 62.5 us (1.023)
  the two profiles are of different devices: /device:TPU:1 before, /device:TPU:0 now
where the time goes in v4:
time: 62.5 us; the launch traced here: 62.3 us
  waiting for transfers between devices  22.6 us (36%)
  Pallas kernels  19.9 us (32%)
  starting transfers between devices  16.5 us (26%)
  local copies, waits for them, and re-layouts  2.55 us (4%)
  between operations  0.74 us (1%)
    ppermute x1, waiting for transfers between devices, shards(): seam = lax.ppermute(seam, flat, partner)  10.4 us
    ppermute x6, waiting for transfers between devices, shards(): sides[name] = lax.ppermute(value, axis, couples(axis, shifted))  9.95 us
    ppermute x6, starting transfers between devices, shards(): sides[name] = lax.ppermute(value, axis, couples(axis, shifted))  8.54 us
    pallas_call x1, Pallas kernels, shards(): pl.pallas_call(functools.partial(other_half, total_layers), out_shape=(sh...  4.77 us
    pallas_call x1, Pallas kernels, shards(): pl.pallas_call(functools.partial(own_half, total_layers), out_shape=shape...  4.74 us
    pallas_call x1, Pallas kernels, shards(): pl.pallas_call(surface, out_shape=(shape(rows, width),) * 2 + (shape(rows...  3.14 us
    ppermute x1, starting transfers between devices, shards(): far_layer = lax.ppermute(layer, flat, partner)  3.06 us
    pallas_call x1, Pallas kernels, shards(): pl.pallas_call(top, out_shape=shape(layers, rows, tile), grid_spec=pltpu....  2.62 us
  transfers between devices with their start and end apart: 12, of which 7 were waited for; matrix products, arithmetic and copies ran while one was open for 0% of the time, Pallas kernels for 25%

profile of v4, /device:TPU:0, one launch (start us, length us, event | category | flops | bytes accessed | tf_op | source)
XLA Modules:
  0.0 62.3 jit_solution(15169331569845826936)
XLA Ops:
  0.7 2.0 %first_pack.1 = (f32[8,128]{1,0:T(8,128)S(1)}, f32[8,128]{1,0:T(8,128)S(1)}, f32[64,2048]{1,0:T(8,128)}) custom-call(s32[1]{0:T(128)} %bitcast.group.group_ref, f32[64,1024]{1,0:T(8,128)} %e.3, f32[64,1024]{1,0:T(8,128)} %p.3, f32[8,64,2048]{2,1,0:T(8,128)} %v_right.1), custom_call_target="tpu_custom_call" | custom-call | tf_op jit(solution)/shard_map/first_pack/pallas_call | solution.py:483
  2.7 3.1 %collective-permute-start.8 = (f32[64,2048]{1,0:T(8,128)}, f32[64,2048]{1,0:T(8,128)S(1)}, u32[]{:S(2)}, u32[]{:S(2)}) collective-permute-start(f32[64,2048]{1,0:T(8,128)} %get-tuple-element.38), channel_id=1, source_target_pairs={{0,1},{1,0},{2,3},{3,2},{4,5},{5,4},{6,7},{7,6},{8,9},{9,8},{10,11... | collective-permute-start | bytes 1572872 | tf_op jit(solution)/shard_map/ppermute | solution.py:499
  5.9 1.8 %collective-permute-start.1 = (f32[8,128]{1,0:T(8,128)S(1)}, f32[8,128]{1,0:T(8,128)S(1)}, u32[]{:S(2)}, u32[]{:S(2)}) collective-permute-start(f32[8,128]{1,0:T(8,128)S(1)} %get-tuple-element.25), channel_id=1, source_target_pairs={{1,2},{3,4},{5,6},{7,0},{2,1},{4,3},{6,5},{0,7},{9,10},{11,12},{13... | collective-permute-start | bytes 12296 | tf_op jit(solution)/shard_map/ppermute | solution.py:500
  7.6 10.4 %collective-permute-done.seam = f32[8,128]{1,0:T(8,128)S(1)} collective-permute-done((f32[8,128]{1,0:T(8,128)S(1)}, f32[8,128]{1,0:T(8,128)S(1)}, u32[]{:S(2)}, u32[]{:S(2)}) %collective-permute-start) | collective-permute-done | bytes 4128 | tf_op jit(solution)/shard_map/ppermute | solution.py:498
  18.2 1.9 %collective-permute-start.2 = (f32[16,1280]{1,0:T(8,128)S(1)}, f32[16,1280]{1,0:T(8,128)S(1)}, u32[]{:S(2)}, u32[]{:S(2)}) collective-permute-start(f32[16,1280]{1,0:T(8,128)S(1)} %get-tuple-element.26), channel_id=1, source_target_pairs={{0,8},{16,24},{8,0},{24,16},{1,9},{17,25},{9,1},{25,17},{2,10},{18... | collective-permute-start | bytes 245768 | tf_op jit(solution)/shard_map/ppermute | solution.py:551
  20.0 2.5 %collective-permute-start.3 = (f32[16,1280]{1,0:T(8,128)S(1)}, f32[16,1280]{1,0:T(8,128)S(1)}, u32[]{:S(2)}, u32[]{:S(2)}) collective-permute-start(f32[16,1280]{1,0:T(8,128)S(1)} %get-tuple-element.27), channel_id=1, source_target_pairs={{8,16},{24,0},{16,8},{0,24},{9,17},{25,1},{17,9},{1,25},{10,18},{2... | collective-permute-start | bytes 245768 | tf_op jit(solution)/shard_map/ppermute | solution.py:551
  22.8 4.0 %collective-permute-done.3.row_b = f32[16,1280]{1,0:T(8,128)S(1)} collective-permute-done((f32[16,1280]{1,0:T(8,128)S(1)}, f32[16,1280]{1,0:T(8,128)S(1)}, u32[]{:S(2)}, u32[]{:S(2)}) %collective-permute-start.3) | collective-permute-done | bytes 81952 | tf_op jit(solution)/shard_map/ppermute | solution.py:551
  26.8 3.1 %surface.1 = (f32[64,1024]{1,0:T(8,128)}, f32[64,1024]{1,0:T(8,128)}, f32[72,1024]{1,0:T(8,128)S(1)}, f32[10,88,128]{2,1,0:T(8,128)S(1)}, f32[10,88,128]{2,1,0:T...) custom-call(s32[1]{0:T(128)} %bitcast.group.group_ref, s32[1]{0:T(128)} %bitcast.1.odd_x, ...), custom_call_target="tpu_custom_call" | custom-call | tf_op jit(solution)/shard_map/surface/pallas_call | solution.py:559
  30.0 2.5 %copy-done = f32[8,18,80,128]{3,2,1,0:T(8,128)} copy-done((f32[8,18,80,128]{3,2,1,0:T(8,128)}, f32[8,18,80,128]{3,2,1,0:T(8,128)S(1)}, u32[]{:S(2)}) %copy-start) | copy-done | bytes 5898264
  32.5 1.1 %collective-permute-start.10 = (f32[72,1024]{1,0:T(8,128)S(1)}, f32[72,1024]{1,0:T(8,128)S(1)}, u32[]{:S(2)}, u32[]{:S(2)}) collective-permute-start(f32[72,1024]{1,0:T(8,128)S(1)} %get-tuple-element.39.after), channel_id=1, source_target_pairs={{0,1},{1,0},{2,3},{3,2},{4,5},{5,4},{6,7},{7,6},{8,9},{9,8},{10,11... | collective-permute-start | bytes 884744 | tf_op jit(solution)/shard_map/ppermute | solution.py:581
  33.5 1.0 %collective-permute-start.11 = (f32[64,1024]{1,0:T(8,128)}, f32[64,1024]{1,0:T(8,128)}, u32[]{:S(2)}, u32[]{:S(2)}) collective-permute-start(f32[64,1024]{1,0:T(8,128)} %get-tuple-element.22), channel_id=1, source_target_pairs={{0,1},{1,0},{2,3},{3,2},{4,5},{5,4},{6,7},{7,6},{8,9},{9,8},{10,11... | collective-permute-start | bytes 786440 | tf_op jit(solution)/shard_map/ppermute | solution.py:582
  34.5 1.8 %lazy_pack.1 = (f32[8,2304]{1,0:T(8,128)S(1)}, f32[8,2304]{1,0:T(8,128)S(1)}, f32[8,128]{1,0:T(8,128)S(1)}, f32[8,128]{1,0:T(8,128)S(1)}) custom-call(s32[1]{0:T(128)} %bitcast.1.odd_x, s32[1]{0:T(128)} %bitcast.2.odd_y, f32[8,64,2048]{2,1,0:T(8,128)} %v_right.1, f32[8,64,2048]{2,1,0:T(8,128)} %v_right.1, f32[8,64,2048]{2,1,0:T(8,128)} %v_right.1, ...), custom_call_target="tpu_custom_call" | custom-call | tf_op jit(solution)/shard_map/lazy_pack/pallas_call | solution.py:506
  36.4 1.6 %collective-permute-start.7 = (f32[8,128]{1,0:T(8,128)S(1)}, f32[8,128]{1,0:T(8,128)S(1)}, u32[]{:S(2)}, u32[]{:S(2)}) collective-permute-start(f32[8,128]{1,0:T(8,128)S(1)} %get-tuple-element.35), channel_id=1, source_target_pairs={{2,4},{6,0},{4,2},{0,6},{3,5},{7,1},{5,3},{1,7},{10,12},{14,8},{12... | collective-permute-start | bytes 12296 | tf_op jit(solution)/shard_map/ppermute | solution.py:551
  38.0 0.6 collective-permute-start.4
  38.5 0.9 %collective-permute-done.7.x_b = f32[8,128]{1,0:T(8,128)S(1)} collective-permute-done((f32[8,128]{1,0:T(8,128)S(1)}, f32[8,128]{1,0:T(8,128)S(1)}, u32[]{:S(2)}, u32[]{:S(2)}) %collective-permute-start.7) | collective-permute-done | bytes 4128 | tf_op jit(solution)/shard_map/ppermute | solution.py:551
  39.5 1.9 %collective-permute-start.5 = (f32[8,2304]{1,0:T(8,128)S(1)}, f32[8,2304]{1,0:T(8,128)S(1)}, u32[]{:S(2)}, u32[]{:S(2)}) collective-permute-start(f32[8,2304]{1,0:T(8,128)S(1)} %get-tuple-element.33), channel_id=1, source_target_pairs={{8,16},{24,0},{16,8},{0,24},{9,17},{25,1},{17,9},{1,25},{10,18},{2... | collective-permute-start | bytes 221192 | tf_op jit(solution)/shard_map/ppermute | solution.py:551
  41.4 0.9 %collective-permute-done.4.far_a = f32[8,2304]{1,0:T(8,128)S(1)} collective-permute-done((f32[8,2304]{1,0:T(8,128)S(1)}, f32[8,2304]{1,0:T(8,128)S(1)}, u32[]{:S(2)}, u32[]{:S(2)}) %collective-permute-start.4) | collective-permute-done | bytes 73760 | tf_op jit(solution)/shard_map/ppermute | solution.py:551
  42.3 3.8 %collective-permute-done.5.far_b = f32[8,2304]{1,0:T(8,128)S(1)} collective-permute-done((f32[8,2304]{1,0:T(8,128)S(1)}, f32[8,2304]{1,0:T(8,128)S(1)}, u32[]{:S(2)}, u32[]{:S(2)}) %collective-permute-start.5) | collective-permute-done | bytes 73760 | tf_op jit(solution)/shard_map/ppermute | solution.py:551
  46.3 1.1 %collective-permute-start.9 = (f32[8,1024]{1,0:T(8,128)S(1)}, f32[8,1024]{1,0:T(8,128)S(1)}, u32[]{:S(2)}, u32[]{:S(2)}) collective-permute-start(f32[8,1024]{1,0:T(8,128)S(1)} %rim_pack.1), channel_id=1, source_target_pairs={{0,1},{1,0},{2,3},{3,2},{4,5},{5,4},{6,7},{7,6},{8,9},{9,8},{10,11... | collective-permute-start | bytes 98312 | tf_op jit(solution)/shard_map/ppermute | solution.py:580
  47.3 0.7 %fill.1 = (f32[8,18,80,128]{3,2,1,0:T(8,128)S(1)}, f32[18,80,128]{2,1,0:T(8,128)S(1)}) custom-call(s32[1]{0:T(128)} %bitcast.1.odd_x, s32[1]{0:T(128)} %bitcast.2.odd_y, f32[8,18,80,128]{3,2,1,0:T(8,128)S(1)} %bitcast.4, f32[18,80,128]{2,1,0:T(8,128)S(1)} %get-tuple-element.31.old_depth, ...), custom_call_target="tpu_custom_call", output_to_operand_aliasing={{0}: (2, {}), {1}: (3, {})} | custom-call | tf_op jit(solution)/shard_map/fill/pallas_call | solution.py:583
  48.0 2.2 %collective-permute-done.9.rims = f32[8,1024]{1,0:T(8,128)S(1)} collective-permute-done((f32[8,1024]{1,0:T(8,128)S(1)}, f32[8,1024]{1,0:T(8,128)S(1)}, u32[]{:S(2)}, u32[]{:S(2)}) %collective-permute-start.9) | collective-permute-done | bytes 32800 | tf_op jit(solution)/shard_map/ppermute | solution.py:580
  50.2 4.7 %own_half.1.before = f32[8,64,2048]{2,1,0:T(8,128)} custom-call(s32[1]{0:T(128)} %bitcast.group.group_ref, f32[8,18,80,128]{3,2,1,0:T(8,128)S(1)} %get-tuple-element.36.volume, f32[18,80,128]{2,1,0:T(8,128)S(1)} %get-tuple-element.37.depth, f32[64,2048]{1,0:T(8,128)S(1)} %collective-permute-done.8.far_layer, f32[8,1024]{1,0:T(8,128)S(1)} %collective-permute-done.9.rims, ...), custom_call_target="tpu_custom_call" | custom-call | tf_op jit(solution)/shard_map/own_half/pallas_call | solution.py:602
  54.9 4.8 %other_half.1 = (f32[8,64,2048]{2,1,0:T(8,128)}, f32[64,1024]{1,0:T(8,128)S(1)}, f32[3,64,1024]{2,1,0:T(8,128)S(1)}) custom-call(s32[1]{0:T(128)} %bitcast.group.group_ref, f32[8,64,2048]{2,1,0:T(8,128)} %own_half.1.before, f32[8,18,80,128]{3,2,1,0:T(8,128)S(1)} %get-tuple-element.36.volume, ...), custom_call_target="tpu_custom_call", output_to_operand_aliasing={{0}: (1, {})} | custom-call | tf_op jit(solution)/shard_map/other_half/pallas_call | solution.py:615
  59.7 2.6 %top.1 = f32[8,64,2048]{2,1,0:T(8,128)} custom-call(s32[1]{0:T(128)} %bitcast.group.group_ref, f32[8,64,2048]{2,1,0:T(8,128)} %get-tuple-element.42.before, f32[64,1024]{1,0:T(8,128)S(1)} %get-tuple-element.43.part, f32[3,64,1024]{2,1,0:T(8,128)S(1)} %get-tuple-element.44.coefficients, ...), custom_call_target="tpu_custom_call", output_to_operand_aliasing={{}: (1, {})} | custom-call | tf_op jit(solution)/shard_map/top/pallas_call | solution.py:633
  (22 shorter events, 0.6 us)
Async XLA Ops:
  0.6 17.4 %copy-start.2 = (f32[64,1024]{1,0:T(8,128)S(1)}, f32[64,1024]{1,0:T(8,128)}, u32[]{:S(2)}) copy-start(f32[64,1024]{1,0:T(8,128)} %e.3) | copy-start | bytes 786436
  0.6 17.4 %copy-start.3 = (f32[64,1024]{1,0:T(8,128)S(1)}, f32[64,1024]{1,0:T(8,128)}, u32[]{:S(2)}) copy-start(f32[64,1024]{1,0:T(8,128)} %p.3) | copy-start | bytes 786436
  0.7 26.1 %copy-start.1 = (s32[64,2048]{1,0:T(8,128)S(1)}, s32[64,2048]{1,0:T(8,128)}, u32[]{:S(2)}) copy-start(s32[64,2048]{1,0:T(8,128)} %s_right.1) | copy-start | bytes 1572868
  2.7 47.5 %collective-permute-start.8 = (f32[64,2048]{1,0:T(8,128)}, f32[64,2048]{1,0:T(8,128)S(1)}, u32[]{:S(2)}, u32[]{:S(2)}) collective-permute-start(f32[64,2048]{1,0:T(8,128)} %get-tuple-element.38), channel_id=1, source_target_pairs={{0,1},{1,0},{2,3},{3,2},{4,5},{5,4},{6,7},{7,6},{8,9},{9,8},{10,11... | collective-permute-start | bytes 1572872 | tf_op jit(solution)/shard_map/ppermute | solution.py:499
  5.8 12.3 %collective-permute-start = (f32[8,128]{1,0:T(8,128)S(1)}, f32[8,128]{1,0:T(8,128)S(1)}, u32[]{:S(2)}, u32[]{:S(2)}) collective-permute-start(f32[8,128]{1,0:T(8,128)S(1)} %get-tuple-element.24), channel_id=1, source_target_pairs={{0,1},{1,0},{2,3},{3,2},{4,5},{5,4},{6,7},{7,6},{8,9},{9,8},{10,11... | collective-permute-start | bytes 12296 | tf_op jit(solution)/shard_map/ppermute | solution.py:498
  5.9 12.2 %collective-permute-start.1 = (f32[8,128]{1,0:T(8,128)S(1)}, f32[8,128]{1,0:T(8,128)S(1)}, u32[]{:S(2)}, u32[]{:S(2)}) collective-permute-start(f32[8,128]{1,0:T(8,128)S(1)} %get-tuple-element.25), channel_id=1, source_target_pairs={{1,2},{3,4},{5,6},{7,0},{2,1},{4,3},{6,5},{0,7},{9,10},{11,12},{13... | collective-permute-start | bytes 12296 | tf_op jit(solution)/shard_map/ppermute | solution.py:500
  18.2 4.6 %collective-permute-start.2 = (f32[16,1280]{1,0:T(8,128)S(1)}, f32[16,1280]{1,0:T(8,128)S(1)}, u32[]{:S(2)}, u32[]{:S(2)}) collective-permute-start(f32[16,1280]{1,0:T(8,128)S(1)} %get-tuple-element.26), channel_id=1, source_target_pairs={{0,8},{16,24},{8,0},{24,16},{1,9},{17,25},{9,1},{25,17},{2,10},{18... | collective-permute-start | bytes 245768 | tf_op jit(solution)/shard_map/ppermute | solution.py:551
  20.0 6.7 %collective-permute-start.3 = (f32[16,1280]{1,0:T(8,128)S(1)}, f32[16,1280]{1,0:T(8,128)S(1)}, u32[]{:S(2)}, u32[]{:S(2)}) collective-permute-start(f32[16,1280]{1,0:T(8,128)S(1)} %get-tuple-element.27), channel_id=1, source_target_pairs={{8,16},{24,0},{16,8},{0,24},{9,17},{25,1},{17,9},{1,25},{10,18},{2... | collective-permute-start | bytes 245768 | tf_op jit(solution)/shard_map/ppermute | solution.py:551
  29.9 2.5 %copy-start = (f32[8,18,80,128]{3,2,1,0:T(8,128)}, f32[8,18,80,128]{3,2,1,0:T(8,128)S(1)}, u32[]{:S(2)}) copy-start(f32[8,18,80,128]{3,2,1,0:T(8,128)S(1)} %get-tuple-element.30.old_volume) | copy-start | bytes 17694724
  32.5 22.5 %collective-permute-start.10 = (f32[72,1024]{1,0:T(8,128)S(1)}, f32[72,1024]{1,0:T(8,128)S(1)}, u32[]{:S(2)}, u32[]{:S(2)}) collective-permute-start(f32[72,1024]{1,0:T(8,128)S(1)} %get-tuple-element.39.after), channel_id=1, source_target_pairs={{0,1},{1,0},{2,3},{3,2},{4,5},{5,4},{6,7},{7,6},{8,9},{9,8},{10,11... | collective-permute-start | bytes 884744 | tf_op jit(solution)/shard_map/ppermute | solution.py:581
  33.5 26.2 %collective-permute-start.11 = (f32[64,1024]{1,0:T(8,128)}, f32[64,1024]{1,0:T(8,128)}, u32[]{:S(2)}, u32[]{:S(2)}) collective-permute-start(f32[64,1024]{1,0:T(8,128)} %get-tuple-element.22), channel_id=1, source_target_pairs={{0,1},{1,0},{2,3},{3,2},{4,5},{5,4},{6,7},{7,6},{8,9},{9,8},{10,11... | collective-permute-start | bytes 786440 | tf_op jit(solution)/shard_map/ppermute | solution.py:582
  34.5 12.8 %slice-start = ((s8[5898240]{0:T(1024)(128)(4,1)}), s8[4194304]{0:T(1024)(128)(4,1)S(1)}, s32[]{:S(2)}) async-start(s8[5898240]{0:T(1024)(128)(4,1)} %bitcast.3), calls=%async_computation | async-start | bytes 8388608
  34.5 12.8 %slice-start.1 = ((s8[5898240]{0:T(1024)(128)(4,1)}), s8[1703936]{0:T(1024)(128)(4,1)S(1)}, s32[]{:S(2)}) async-start(s8[5898240]{0:T(1024)(128)(4,1)} %bitcast.3), calls=%async_computation.1 | async-start | bytes 3407872
  36.3 1.7 %collective-permute-start.6 = (f32[8,128]{1,0:T(8,128)S(1)}, f32[8,128]{1,0:T(8,128)S(1)}, u32[]{:S(2)}, u32[]{:S(2)}) collective-permute-start(f32[8,128]{1,0:T(8,128)S(1)} %get-tuple-element.34), channel_id=1, source_target_pairs={{0,2},{4,6},{2,0},{6,4},{1,3},{5,7},{3,1},{7,5},{8,10},{12,14},{10... | collective-permute-start | bytes 12296 | tf_op jit(solution)/shard_map/ppermute | solution.py:551
  36.4 3.1 %collective-permute-start.7 = (f32[8,128]{1,0:T(8,128)S(1)}, f32[8,128]{1,0:T(8,128)S(1)}, u32[]{:S(2)}, u32[]{:S(2)}) collective-permute-start(f32[8,128]{1,0:T(8,128)S(1)} %get-tuple-element.35), channel_id=1, source_target_pairs={{2,4},{6,0},{4,2},{0,6},{3,5},{7,1},{5,3},{1,7},{10,12},{14,8},{12... | collective-permute-start | bytes 12296 | tf_op jit(solution)/shard_map/ppermute | solution.py:551
  38.0 4.4 %collective-permute-start.4 = (f32[8,2304]{1,0:T(8,128)S(1)}, f32[8,2304]{1,0:T(8,128)S(1)}, u32[]{:S(2)}, u32[]{:S(2)}) collective-permute-start(f32[8,2304]{1,0:T(8,128)S(1)} %get-tuple-element.32), channel_id=1, source_target_pairs={{0,8},{16,24},{8,0},{24,16},{1,9},{17,25},{9,1},{25,17},{2,10},{18... | collective-permute-start | bytes 221192 | tf_op jit(solution)/shard_map/ppermute | solution.py:551
  39.5 6.7 %collective-permute-start.5 = (f32[8,2304]{1,0:T(8,128)S(1)}, f32[8,2304]{1,0:T(8,128)S(1)}, u32[]{:S(2)}, u32[]{:S(2)}) collective-permute-start(f32[8,2304]{1,0:T(8,128)S(1)} %get-tuple-element.33), channel_id=1, source_target_pairs={{8,16},{24,0},{16,8},{0,24},{9,17},{25,1},{17,9},{1,25},{10,18},{2... | collective-permute-start | bytes 221192 | tf_op jit(solution)/shard_map/ppermute | solution.py:551
  46.3 3.9 %collective-permute-start.9 = (f32[8,1024]{1,0:T(8,128)S(1)}, f32[8,1024]{1,0:T(8,128)S(1)}, u32[]{:S(2)}, u32[]{:S(2)}) collective-permute-start(f32[8,1024]{1,0:T(8,128)S(1)} %rim_pack.1), channel_id=1, source_target_pairs={{0,1},{1,0},{2,3},{3,2},{4,5},{5,4},{6,7},{7,6},{8,9},{9,8},{10,11... | collective-permute-start | bytes 98312 | tf_op jit(solution)/shard_map/ppermute | solution.py:580

commit v5 on v4

--- a/solution.py
+++ b/solution.py
@@ -102,17 +102,35 @@
     by_parity(odd_x, functools.partial(pack_surface_rows, left, right, e_top, e_bottom, p_top, p_bottom), row_a, row_b)
 
 
+REACH = 5
+
+
+def spare_piece(index, tiles):
+    start = (tiles + index // SUBS) * LANES
+    return slice(index % SUBS, index % SUBS + 1), slice(start, start + LANES)
+
+
 def pack_surface_rows(left, right, e_top, e_bottom, p_top, p_bottom, up, down):
     rows = LANES // 2
-    width = e_top.shape[1]
-    for row, tops, bottoms in ((0, e_top, e_bottom), (SUBS, p_top, p_bottom)):
-        base = 0 if row == 0 else rows
-        up[row : row + SUBS, :LANES] = left[base + rows - SUBS : base + rows]
-        up[row : row + SUBS, LANES : LANES + width] = bottoms[...]
-        up[row : row + SUBS, LANES + width :] = right[base + rows - SUBS : base + rows]
-        down[row : row + SUBS, :LANES] = left[base : base + SUBS]
-        down[row : row + SUBS, LANES : LANES + width] = tops[...]
-        down[row : row + SUBS, LANES + width :] = right[base : base + SUBS]
+    tiles = e_top.shape[1] // LANES + 2
+    fit = SUBS - REACH
+    for into, first, e_rows, p_rows in ((up, rows - REACH, e_bottom, p_bottom), (down, 0, e_top, p_top)):
+        start = first % SUBS
+        for t in range(tiles):
+            part = slice(t * LANES, (t + 1) * LANES)
+            if 0 < t < tiles - 1:
+                own = slice((t - 1) * LANES, t * LANES)
+                e_part = e_rows[start : start + REACH, own]
+                p_part = p_rows[start : start + REACH, own]
+            else:
+                side = left if t == 0 else right
+                e_part = side[first : first + REACH]
+                p_part = side[rows + first : rows + first + REACH]
+            into[:REACH, part] = e_part
+            into[REACH:, part] = p_part[:fit]
+            for extra in range(REACH - fit):
+                row, lanes = spare_piece(extra * tiles + t, tiles)
+                into[row, lanes] = p_part[fit + extra : fit + extra + 1]
 
 
 def neighbourhood(ref, lane_tile, row):
@@ -157,14 +175,17 @@
     tiles = width // LANES + 2
     inner = slice(SUBS, SUBS + rows)
     fields = ((e0, e, 0), (p0, p, LANES // 2))
+    fit = SUBS - REACH
 
     def ends(south, north):
-        for old, _, base in fields:
-            half = SUBS if base else 0
+        for source, first in ((north, SUBS - REACH), (south, SUBS + rows)):
             for t in range(tiles):
                 part = slice(t * LANES, (t + 1) * LANES)
-                old[t, :SUBS, :] = north[half : half + SUBS, part]
-                old[t, SUBS + rows : 2 * SUBS + rows, :] = south[half : half + SUBS, part]
+                e0[t, first : first + REACH, :] = source[:REACH, part]
+                p0[t, first : first + fit, :] = source[REACH:, part]
+                for extra in range(REACH - fit):
+                    row = first + fit + extra
+                    p0[t, row : row + 1, :] = source[spare_piece(extra * tiles + t, tiles)]
 
     by_parity(odd_x, ends, row_a, row_b)
     for old, source, base in fields:
@@ -525,9 +546,10 @@
     )(odd_x, odd_y, *(pltpu.with_memory_space_constraint(interior_potential, pltpu.HBM),) * 4, *(seabed,) * 4)
 
     wide = width + 2 * LANES
+    packed = wide + pl.cdiv((2 * REACH - SUBS) * (wide // LANES), SUBS) * LANES
     row_a, row_b = pl.pallas_call(
         row_pack,
-        out_shape=(shape(2 * SUBS, wide),) * 2,
+        out_shape=(shape(SUBS, packed),) * 2,
         grid=(1,),
         in_specs=[
             scalar,
@@ -539,7 +561,7 @@
             whole(SUBS, LANES),
             whole(SUBS, LANES),
         ],
-        out_specs=[whole(2 * SUBS, wide)] * 2,
+        out_specs=[whole(SUBS, packed)] * 2,
         compiler_params=params,
         name="row_pack",
     )(group, odd_x, elevation, elevation, surface_potential, surface_potential, seam, outer)

time: 62.5 us -> 61.7 us (0.987)
  waiting for transfers between devices: 22.6 us -> 21.3 us
    ppermute x6, waiting for transfers between devices: 9.95 us -> 9.21 us  [shards(): sides[name] = lax.ppermute(value, axis, couples(axis, shifted))]
  transfers between devices with their start and end apart: 12 -> 12, of which waited for: 7 -> 6; matrix products, arithmetic and copies ran while one was open for 0% -> 0% of each run, Pallas kernels for 25% -> 25%
where the time goes in v5:
time: 61.7 us; the launch traced here: 61.5 us
  waiting for transfers between devices  21.3 us (35%)
  Pallas kernels  19.9 us (32%)
  starting transfers between devices  17 us (28%)
  local copies, waits for them, and re-layouts  2.55 us (4%)
  between operations  0.74 us (1%)
    ppermute x1, waiting for transfers between devices, shards(): seam = lax.ppermute(seam, flat, partner)  10.4 us
    ppermute x6, waiting for transfers between devices, shards(): sides[name] = lax.ppermute(value, axis, couples(axis, shifted))  9.21 us
    ppermute x6, starting transfers between devices, shards(): sides[name] = lax.ppermute(value, axis, couples(axis, shifted))  8.46 us
    pallas_call x1, Pallas kernels, shards(): pl.pallas_call(functools.partial(other_half, total_layers), out_shape=(sh...  4.77 us
    pallas_call x1, Pallas kernels, shards(): pl.pallas_call(functools.partial(own_half, total_layers), out_shape=shape...  4.74 us
    pallas_call x1, Pallas kernels, shards(): pl.pallas_call(surface, out_shape=(shape(rows, width),) * 2 + (shape(rows...  3.14 us
    ppermute x1, starting transfers between devices, shards(): far_layer = lax.ppermute(layer, flat, partner)  3.06 us
    pallas_call x1, Pallas kernels, shards(): pl.pallas_call(top, out_shape=shape(layers, rows, tile), grid_spec=pltpu....  2.62 us
  transfers between devices with their start and end apart: 12, of which 6 were waited for; matrix products, arithmetic and copies ran while one was open for 0% of the time, Pallas kernels for 25%

profile of v5, /device:TPU:0, one launch (start us, length us, event | category | flops | bytes accessed | tf_op | source)
XLA Modules:
  0.0 61.5 jit_solution(3253777652022120213)
XLA Ops:
  0.7 2.0 %first_pack.1 = (f32[8,128]{1,0:T(8,128)S(1)}, f32[8,128]{1,0:T(8,128)S(1)}, f32[64,2048]{1,0:T(8,128)}) custom-call(s32[1]{0:T(128)} %bitcast.group.group_ref, f32[64,1024]{1,0:T(8,128)} %e.3, f32[64,1024]{1,0:T(8,128)} %p.3, f32[8,64,2048]{2,1,0:T(8,128)} %v_right.1), custom_call_target="tpu_custom_call" | custom-call | tf_op jit(solution)/shard_map/first_pack/pallas_call | solution.py:504
  2.7 3.1 %collective-permute-start.8 = (f32[64,2048]{1,0:T(8,128)}, f32[64,2048]{1,0:T(8,128)S(1)}, u32[]{:S(2)}, u32[]{:S(2)}) collective-permute-start(f32[64,2048]{1,0:T(8,128)} %get-tuple-element.38), channel_id=1, source_target_pairs={{0,1},{1,0},{2,3},{3,2},{4,5},{5,4},{6,7},{7,6},{8,9},{9,8},{10,11... | collective-permute-start | bytes 1572872 | tf_op jit(solution)/shard_map/ppermute | solution.py:520
  5.9 1.8 %collective-permute-start.1 = (f32[8,128]{1,0:T(8,128)S(1)}, f32[8,128]{1,0:T(8,128)S(1)}, u32[]{:S(2)}, u32[]{:S(2)}) collective-permute-start(f32[8,128]{1,0:T(8,128)S(1)} %get-tuple-element.25), channel_id=1, source_target_pairs={{1,2},{3,4},{5,6},{7,0},{2,1},{4,3},{6,5},{0,7},{9,10},{11,12},{13... | collective-permute-start | bytes 12296 | tf_op jit(solution)/shard_map/ppermute | solution.py:521
  7.6 10.4 %collective-permute-done.seam = f32[8,128]{1,0:T(8,128)S(1)} collective-permute-done((f32[8,128]{1,0:T(8,128)S(1)}, f32[8,128]{1,0:T(8,128)S(1)}, u32[]{:S(2)}, u32[]{:S(2)}) %collective-permute-start) | collective-permute-done | bytes 4128 | tf_op jit(solution)/shard_map/ppermute | solution.py:519
  18.1 0.1 row_pack.1
  18.2 1.9 %collective-permute-start.2 = (f32[8,1664]{1,0:T(8,128)S(1)}, f32[8,1664]{1,0:T(8,128)S(1)}, u32[]{:S(2)}, u32[]{:S(2)}) collective-permute-start(f32[8,1664]{1,0:T(8,128)S(1)} %get-tuple-element.26), channel_id=1, source_target_pairs={{0,8},{16,24},{8,0},{24,16},{1,9},{17,25},{9,1},{25,17},{2,10},{18... | collective-permute-start | bytes 159752 | tf_op jit(solution)/shard_map/ppermute | solution.py:573
  20.1 2.5 %collective-permute-start.3 = (f32[8,1664]{1,0:T(8,128)S(1)}, f32[8,1664]{1,0:T(8,128)S(1)}, u32[]{:S(2)}, u32[]{:S(2)}) collective-permute-start(f32[8,1664]{1,0:T(8,128)S(1)} %get-tuple-element.27), channel_id=1, source_target_pairs={{8,16},{24,0},{16,8},{0,24},{9,17},{25,1},{17,9},{1,25},{10,18},{2... | collective-permute-start | bytes 159752 | tf_op jit(solution)/shard_map/ppermute | solution.py:573
  22.5 3.5 %collective-permute-done.3.row_b = f32[8,1664]{1,0:T(8,128)S(1)} collective-permute-done((f32[8,1664]{1,0:T(8,128)S(1)}, f32[8,1664]{1,0:T(8,128)S(1)}, u32[]{:S(2)}, u32[]{:S(2)}) %collective-permute-start.3) | collective-permute-done | bytes 53280 | tf_op jit(solution)/shard_map/ppermute | solution.py:573
  26.0 3.1 %surface.1 = (f32[64,1024]{1,0:T(8,128)}, f32[64,1024]{1,0:T(8,128)}, f32[72,1024]{1,0:T(8,128)S(1)}, f32[10,88,128]{2,1,0:T(8,128)S(1)}, f32[10,88,128]{2,1,0:T...) custom-call(s32[1]{0:T(128)} %bitcast.group.group_ref, s32[1]{0:T(128)} %bitcast.1.odd_x, ...), custom_call_target="tpu_custom_call" | custom-call | tf_op jit(solution)/shard_map/surface/pallas_call | solution.py:581
  29.1 2.5 %copy-done = f32[8,18,80,128]{3,2,1,0:T(8,128)} copy-done((f32[8,18,80,128]{3,2,1,0:T(8,128)}, f32[8,18,80,128]{3,2,1,0:T(8,128)S(1)}, u32[]{:S(2)}) %copy-start) | copy-done | bytes 5898264
  31.7 1.6 %collective-permute-start.10 = (f32[72,1024]{1,0:T(8,128)S(1)}, f32[72,1024]{1,0:T(8,128)S(1)}, u32[]{:S(2)}, u32[]{:S(2)}) collective-permute-start(f32[72,1024]{1,0:T(8,128)S(1)} %get-tuple-element.39.after), channel_id=1, source_target_pairs={{0,1},{1,0},{2,3},{3,2},{4,5},{5,4},{6,7},{7,6},{8,9},{9,8},{10,11... | collective-permute-start | bytes 884744 | tf_op jit(solution)/shard_map/ppermute | solution.py:603
  33.2 0.5 collective-permute-start.11
  33.7 1.8 %lazy_pack.1 = (f32[8,2304]{1,0:T(8,128)S(1)}, f32[8,2304]{1,0:T(8,128)S(1)}, f32[8,128]{1,0:T(8,128)S(1)}, f32[8,128]{1,0:T(8,128)S(1)}) custom-call(s32[1]{0:T(128)} %bitcast.1.odd_x, s32[1]{0:T(128)} %bitcast.2.odd_y, f32[8,64,2048]{2,1,0:T(8,128)} %v_right.1, f32[8,64,2048]{2,1,0:T(8,128)} %v_right.1, f32[8,64,2048]{2,1,0:T(8,128)} %v_right.1, ...), custom_call_target="tpu_custom_call" | custom-call | tf_op jit(solution)/shard_map/lazy_pack/pallas_call | solution.py:527
  35.6 1.6 %collective-permute-start.7 = (f32[8,128]{1,0:T(8,128)S(1)}, f32[8,128]{1,0:T(8,128)S(1)}, u32[]{:S(2)}, u32[]{:S(2)}) collective-permute-start(f32[8,128]{1,0:T(8,128)S(1)} %get-tuple-element.35), channel_id=1, source_target_pairs={{2,4},{6,0},{4,2},{0,6},{3,5},{7,1},{5,3},{1,7},{10,12},{14,8},{12... | collective-permute-start | bytes 12296 | tf_op jit(solution)/shard_map/ppermute | solution.py:573
  37.2 1.5 %collective-permute-done.7.x_b = f32[8,128]{1,0:T(8,128)S(1)} collective-permute-done((f32[8,128]{1,0:T(8,128)S(1)}, f32[8,128]{1,0:T(8,128)S(1)}, u32[]{:S(2)}, u32[]{:S(2)}) %collective-permute-start.7) | collective-permute-done | bytes 4128 | tf_op jit(solution)/shard_map/ppermute | solution.py:573
  38.7 2.5 %collective-permute-start.5 = (f32[8,2304]{1,0:T(8,128)S(1)}, f32[8,2304]{1,0:T(8,128)S(1)}, u32[]{:S(2)}, u32[]{:S(2)}) collective-permute-start(f32[8,2304]{1,0:T(8,128)S(1)} %get-tuple-element.33), channel_id=1, source_target_pairs={{8,16},{24,0},{16,8},{0,24},{9,17},{25,1},{17,9},{1,25},{10,18},{2... | collective-permute-start | bytes 221192 | tf_op jit(solution)/shard_map/ppermute | solution.py:573
  41.1 0.4 collective-permute-done.4.far_a
  41.5 3.8 %collective-permute-done.5.far_b = f32[8,2304]{1,0:T(8,128)S(1)} collective-permute-done((f32[8,2304]{1,0:T(8,128)S(1)}, f32[8,2304]{1,0:T(8,128)S(1)}, u32[]{:S(2)}, u32[]{:S(2)}) %collective-permute-start.5) | collective-permute-done | bytes 73760 | tf_op jit(solution)/shard_map/ppermute | solution.py:573
  45.4 1.6 %collective-permute-start.9 = (f32[8,1024]{1,0:T(8,128)S(1)}, f32[8,1024]{1,0:T(8,128)S(1)}, u32[]{:S(2)}, u32[]{:S(2)}) collective-permute-start(f32[8,1024]{1,0:T(8,128)S(1)} %rim_pack.1), channel_id=1, source_target_pairs={{0,1},{1,0},{2,3},{3,2},{4,5},{5,4},{6,7},{7,6},{8,9},{9,8},{10,11... | collective-permute-start | bytes 98312 | tf_op jit(solution)/shard_map/ppermute | solution.py:602
  47.0 0.7 %fill.1 = (f32[8,18,80,128]{3,2,1,0:T(8,128)S(1)}, f32[18,80,128]{2,1,0:T(8,128)S(1)}) custom-call(s32[1]{0:T(128)} %bitcast.1.odd_x, s32[1]{0:T(128)} %bitcast.2.odd_y, f32[8,18,80,128]{3,2,1,0:T(8,128)S(1)} %bitcast.4, f32[18,80,128]{2,1,0:T(8,128)S(1)} %get-tuple-element.31.old_depth, ...), custom_call_target="tpu_custom_call", output_to_operand_aliasing={{0}: (2, {}), {1}: (3, {})} | custom-call | tf_op jit(solution)/shard_map/fill/pallas_call | solution.py:605
  47.7 1.7 %collective-permute-done.9.rims = f32[8,1024]{1,0:T(8,128)S(1)} collective-permute-done((f32[8,1024]{1,0:T(8,128)S(1)}, f32[8,1024]{1,0:T(8,128)S(1)}, u32[]{:S(2)}, u32[]{:S(2)}) %collective-permute-start.9) | collective-permute-done | bytes 32800 | tf_op jit(solution)/shard_map/ppermute | solution.py:602
  49.4 4.7 %own_half.1.before = f32[8,64,2048]{2,1,0:T(8,128)} custom-call(s32[1]{0:T(128)} %bitcast.group.group_ref, f32[8,18,80,128]{3,2,1,0:T(8,128)S(1)} %get-tuple-element.36.volume, f32[18,80,128]{2,1,0:T(8,128)S(1)} %get-tuple-element.37.depth, f32[64,2048]{1,0:T(8,128)S(1)} %collective-permute-done.8.far_layer, f32[8,1024]{1,0:T(8,128)S(1)} %collective-permute-done.9.rims, ...), custom_call_target="tpu_custom_call" | custom-call | tf_op jit(solution)/shard_map/own_half/pallas_call | solution.py:624
  54.1 4.8 %other_half.1 = (f32[8,64,2048]{2,1,0:T(8,128)}, f32[64,1024]{1,0:T(8,128)S(1)}, f32[3,64,1024]{2,1,0:T(8,128)S(1)}) custom-call(s32[1]{0:T(128)} %bitcast.group.group_ref, f32[8,64,2048]{2,1,0:T(8,128)} %own_half.1.before, f32[8,18,80,128]{3,2,1,0:T(8,128)S(1)} %get-tuple-element.36.volume, ...), custom_call_target="tpu_custom_call", output_to_operand_aliasing={{0}: (1, {})} | custom-call | tf_op jit(solution)/shard_map/other_half/pallas_call | solution.py:637
  58.9 2.6 %top.1 = f32[8,64,2048]{2,1,0:T(8,128)} custom-call(s32[1]{0:T(128)} %bitcast.group.group_ref, f32[8,64,2048]{2,1,0:T(8,128)} %get-tuple-element.42.before, f32[64,1024]{1,0:T(8,128)S(1)} %get-tuple-element.43.part, f32[3,64,1024]{2,1,0:T(8,128)S(1)} %get-tuple-element.44.coefficients, ...), custom_call_target="tpu_custom_call", output_to_operand_aliasing={{}: (1, {})} | custom-call | tf_op jit(solution)/shard_map/top/pallas_call | solution.py:655
  (22 shorter events, 0.3 us)
Async XLA Ops:
  0.6 17.4 %copy-start.2 = (f32[64,1024]{1,0:T(8,128)S(1)}, f32[64,1024]{1,0:T(8,128)}, u32[]{:S(2)}) copy-start(f32[64,1024]{1,0:T(8,128)} %e.3) | copy-start | bytes 786436
  0.6 17.4 %copy-start.3 = (f32[64,1024]{1,0:T(8,128)S(1)}, f32[64,1024]{1,0:T(8,128)}, u32[]{:S(2)}) copy-start(f32[64,1024]{1,0:T(8,128)} %p.3) | copy-start | bytes 786436
  0.7 25.3 %copy-start.1 = (s32[64,2048]{1,0:T(8,128)S(1)}, s32[64,2048]{1,0:T(8,128)}, u32[]{:S(2)}) copy-start(s32[64,2048]{1,0:T(8,128)} %s_right.1) | copy-start | bytes 1572868
  2.7 46.7 %collective-permute-start.8 = (f32[64,2048]{1,0:T(8,128)}, f32[64,2048]{1,0:T(8,128)S(1)}, u32[]{:S(2)}, u32[]{:S(2)}) collective-permute-start(f32[64,2048]{1,0:T(8,128)} %get-tuple-element.38), channel_id=1, source_target_pairs={{0,1},{1,0},{2,3},{3,2},{4,5},{5,4},{6,7},{7,6},{8,9},{9,8},{10,11... | collective-permute-start | bytes 1572872 | tf_op jit(solution)/shard_map/ppermute | solution.py:520
  5.8 12.3 %collective-permute-start = (f32[8,128]{1,0:T(8,128)S(1)}, f32[8,128]{1,0:T(8,128)S(1)}, u32[]{:S(2)}, u32[]{:S(2)}) collective-permute-start(f32[8,128]{1,0:T(8,128)S(1)} %get-tuple-element.24), channel_id=1, source_target_pairs={{0,1},{1,0},{2,3},{3,2},{4,5},{5,4},{6,7},{7,6},{8,9},{9,8},{10,11... | collective-permute-start | bytes 12296 | tf_op jit(solution)/shard_map/ppermute | solution.py:519
  5.9 12.2 %collective-permute-start.1 = (f32[8,128]{1,0:T(8,128)S(1)}, f32[8,128]{1,0:T(8,128)S(1)}, u32[]{:S(2)}, u32[]{:S(2)}) collective-permute-start(f32[8,128]{1,0:T(8,128)S(1)} %get-tuple-element.25), channel_id=1, source_target_pairs={{1,2},{3,4},{5,6},{7,0},{2,1},{4,3},{6,5},{0,7},{9,10},{11,12},{13... | collective-permute-start | bytes 12296 | tf_op jit(solution)/shard_map/ppermute | solution.py:521
  18.2 4.3 %collective-permute-start.2 = (f32[8,1664]{1,0:T(8,128)S(1)}, f32[8,1664]{1,0:T(8,128)S(1)}, u32[]{:S(2)}, u32[]{:S(2)}) collective-permute-start(f32[8,1664]{1,0:T(8,128)S(1)} %get-tuple-element.26), channel_id=1, source_target_pairs={{0,8},{16,24},{8,0},{24,16},{1,9},{17,25},{9,1},{25,17},{2,10},{18... | collective-permute-start | bytes 159752 | tf_op jit(solution)/shard_map/ppermute | solution.py:573
  20.1 5.9 %collective-permute-start.3 = (f32[8,1664]{1,0:T(8,128)S(1)}, f32[8,1664]{1,0:T(8,128)S(1)}, u32[]{:S(2)}, u32[]{:S(2)}) collective-permute-start(f32[8,1664]{1,0:T(8,128)S(1)} %get-tuple-element.27), channel_id=1, source_target_pairs={{8,16},{24,0},{16,8},{0,24},{9,17},{25,1},{17,9},{1,25},{10,18},{2... | collective-permute-start | bytes 159752 | tf_op jit(solution)/shard_map/ppermute | solution.py:573
  29.1 2.5 %copy-start = (f32[8,18,80,128]{3,2,1,0:T(8,128)}, f32[8,18,80,128]{3,2,1,0:T(8,128)S(1)}, u32[]{:S(2)}) copy-start(f32[8,18,80,128]{3,2,1,0:T(8,128)S(1)} %get-tuple-element.30.old_volume) | copy-start | bytes 17694724
  31.7 22.5 %collective-permute-start.10 = (f32[72,1024]{1,0:T(8,128)S(1)}, f32[72,1024]{1,0:T(8,128)S(1)}, u32[]{:S(2)}, u32[]{:S(2)}) collective-permute-start(f32[72,1024]{1,0:T(8,128)S(1)} %get-tuple-element.39.after), channel_id=1, source_target_pairs={{0,1},{1,0},{2,3},{3,2},{4,5},{5,4},{6,7},{7,6},{8,9},{9,8},{10,11... | collective-permute-start | bytes 884744 | tf_op jit(solution)/shard_map/ppermute | solution.py:603
  33.2 25.7 %collective-permute-start.11 = (f32[64,1024]{1,0:T(8,128)}, f32[64,1024]{1,0:T(8,128)}, u32[]{:S(2)}, u32[]{:S(2)}) collective-permute-start(f32[64,1024]{1,0:T(8,128)} %get-tuple-element.22), channel_id=1, source_target_pairs={{0,1},{1,0},{2,3},{3,2},{4,5},{5,4},{6,7},{7,6},{8,9},{9,8},{10,11... | collective-permute-start | bytes 786440 | tf_op jit(solution)/shard_map/ppermute | solution.py:604
  33.7 13.3 %slice-start = ((s8[5898240]{0:T(1024)(128)(4,1)}), s8[4194304]{0:T(1024)(128)(4,1)S(1)}, s32[]{:S(2)}) async-start(s8[5898240]{0:T(1024)(128)(4,1)} %bitcast.3), calls=%async_computation | async-start | bytes 8388608
  33.7 13.3 %slice-start.1 = ((s8[5898240]{0:T(1024)(128)(4,1)}), s8[1703936]{0:T(1024)(128)(4,1)S(1)}, s32[]{:S(2)}) async-start(s8[5898240]{0:T(1024)(128)(4,1)} %bitcast.3), calls=%async_computation.1 | async-start | bytes 3407872
  35.5 1.7 %collective-permute-start.6 = (f32[8,128]{1,0:T(8,128)S(1)}, f32[8,128]{1,0:T(8,128)S(1)}, u32[]{:S(2)}, u32[]{:S(2)}) collective-permute-start(f32[8,128]{1,0:T(8,128)S(1)} %get-tuple-element.34), channel_id=1, source_target_pairs={{0,2},{4,6},{2,0},{6,4},{1,3},{5,7},{3,1},{7,5},{8,10},{12,14},{10... | collective-permute-start | bytes 12296 | tf_op jit(solution)/shard_map/ppermute | solution.py:573
  35.6 3.1 %collective-permute-start.7 = (f32[8,128]{1,0:T(8,128)S(1)}, f32[8,128]{1,0:T(8,128)S(1)}, u32[]{:S(2)}, u32[]{:S(2)}) collective-permute-start(f32[8,128]{1,0:T(8,128)S(1)} %get-tuple-element.35), channel_id=1, source_target_pairs={{2,4},{6,0},{4,2},{0,6},{3,5},{7,1},{5,3},{1,7},{10,12},{14,8},{12... | collective-permute-start | bytes 12296 | tf_op jit(solution)/shard_map/ppermute | solution.py:573
  37.2 4.4 %collective-permute-start.4 = (f32[8,2304]{1,0:T(8,128)S(1)}, f32[8,2304]{1,0:T(8,128)S(1)}, u32[]{:S(2)}, u32[]{:S(2)}) collective-permute-start(f32[8,2304]{1,0:T(8,128)S(1)} %get-tuple-element.32), channel_id=1, source_target_pairs={{0,8},{16,24},{8,0},{24,16},{1,9},{17,25},{9,1},{25,17},{2,10},{18... | collective-permute-start | bytes 221192 | tf_op jit(solution)/shard_map/ppermute | solution.py:573
  38.7 6.7 %collective-permute-start.5 = (f32[8,2304]{1,0:T(8,128)S(1)}, f32[8,2304]{1,0:T(8,128)S(1)}, u32[]{:S(2)}, u32[]{:S(2)}) collective-permute-start(f32[8,2304]{1,0:T(8,128)S(1)} %get-tuple-element.33), channel_id=1, source_target_pairs={{8,16},{24,0},{16,8},{0,24},{9,17},{25,1},{17,9},{1,25},{10,18},{2... | collective-permute-start | bytes 221192 | tf_op jit(solution)/shard_map/ppermute | solution.py:573
  45.4 3.9 %collective-permute-start.9 = (f32[8,1024]{1,0:T(8,128)S(1)}, f32[8,1024]{1,0:T(8,128)S(1)}, u32[]{:S(2)}, u32[]{:S(2)}) collective-permute-start(f32[8,1024]{1,0:T(8,128)S(1)} %rim_pack.1), channel_id=1, source_target_pairs={{0,1},{1,0},{2,3},{3,2},{4,5},{5,4},{6,7},{7,6},{8,9},{9,8},{10,11... | collective-permute-start | bytes 98312 | tf_op jit(solution)/shard_map/ppermute | solution.py:602

commit v6 on v5

--- a/solution.py
+++ b/solution.py
@@ -95,6 +95,10 @@
     left = square(jnp.where(low, outer, seam), True).T
     right = square(jnp.where(low, seam, outer), False).T
     return left, right
+
+
+def block_pack(group, seam, outer, blocks):
+    blocks[0], blocks[1] = side_blocks(group[0] == 0, seam[...], outer[...])
 
 
 def row_pack(group, odd_x, e_top, e_bottom, p_top, p_bottom, seam, outer, row_a, row_b):
@@ -160,18 +164,18 @@
 
 
 def surface(
-    group, odd_x, e, p, seam, outer, row_a, row_b, v, sea,
+    odd_x, e, p, side_tiles, group, row_a, row_b, v, sea,
     new_e, new_p, height, wide_e, wide_p, volume, depth, e0, p0, e1, p1, sems,
 ):
     rows, width = e.shape
     low = group[0] == 0
+    left, right = side_tiles[0], side_tiles[1]
     copies = []
     for t in range(v.shape[2] // LANES):
         part = slice(t * LANES, (t + 1) * LANES)
         into = volume.at[:, t + 1, SUBS : SUBS + rows, :]
         copies.append(pltpu.make_async_copy(v.at[:, :, part], into, sems.at[t]))
         copies[-1].start()
-    left, right = side_blocks(low, seam[...], outer[...])
     tiles = width // LANES + 2
     inner = slice(SUBS, SUBS + rows)
     fields = ((e0, e, 0), (p0, p, LANES // 2))
@@ -520,6 +524,14 @@
     far_layer = lax.ppermute(layer, flat, partner)
     outer = lax.ppermute(outer, flat, across)
 
+    side_tiles = pl.pallas_call(
+        block_pack,
+        out_shape=shape(2, LANES, LANES),
+        in_specs=[scalar] + [vmem] * 2,
+        out_specs=vmem,
+        compiler_params=params,
+        name="block_pack",
+    )(group, seam, outer)
     tiles = tile // LANES
     tall = rows + 2 * SUBS
     tables = (shape(layers, tiles + 2, tall, LANES), shape(tiles + 2, tall, LANES))
@@ -581,13 +593,13 @@
     new_e, new_p, height, wide_e, wide_p, volume, depth = pl.pallas_call(
         surface,
         out_shape=(shape(rows, width),) * 2 + (shape(rows + SUBS, width),) + (shape(*padded),) * 2 + tables,
-        in_specs=[scalar] * 2 + [vmem] * 6 + [hbm, vmem],
+        in_specs=[scalar] + [vmem] * 3 + [scalar] + [vmem] * 2 + [hbm, vmem],
         out_specs=[vmem] * 7,
         scratch_shapes=[pltpu.VMEM(padded, f32)] * 4 + [pltpu.SemaphoreType.DMA((tiles,))],
         compiler_params=params,
         name="surface",
     )(
-        group, odd_x, elevation, surface_potential, seam, outer, sides["row_a"], sides["row_b"],
+        odd_x, elevation, surface_potential, side_tiles, group, sides["row_a"], sides["row_b"],
         pltpu.with_memory_space_constraint(interior_potential, pltpu.HBM), seabed,
     )
     far_sides = [sides[name] for name in ("far_a", "far_b", "x_a", "x_b")]

time: 61.7 us -> 61.7 us (level)
  no operation moved by 1% of the time
where the time goes in v6:
time: 61.7 us; the launch traced here: 61.5 us
  waiting for transfers between devices  21.2 us (34%)
  Pallas kernels  20 us (32%)
  starting transfers between devices  17 us (28%)
  local copies, waits for them, and re-layouts  2.55 us (4%)
  between operations  0.75 us (1%)
    ppermute x1, waiting for transfers between devices, shards(): seam = lax.ppermute(seam, flat, partner)  10.4 us
    ppermute x6, waiting for transfers between devices, shards(): sides[name] = lax.ppermute(value, axis, couples(axis, shifted))  9.1 us
    ppermute x6, starting transfers between devices, shards(): sides[name] = lax.ppermute(value, axis, couples(axis, shifted))  8.46 us
    pallas_call x1, Pallas kernels, shards(): pl.pallas_call(functools.partial(other_half, total_layers), out_shape=(sh...  4.77 us
    pallas_call x1, Pallas kernels, shards(): pl.pallas_call(functools.partial(own_half, total_layers), out_shape=shape...  4.74 us
    pallas_call x1, Pallas kernels, shards(): pl.pallas_call(surface, out_shape=(shape(rows, width),) * 2 + (shape(rows...  3.15 us
    ppermute x1, starting transfers between devices, shards(): far_layer = lax.ppermute(layer, flat, partner)  3.06 us
    pallas_call x1, Pallas kernels, shards(): pl.pallas_call(top, out_shape=shape(layers, rows, tile), grid_spec=pltpu....  2.62 us
  transfers between devices with their start and end apart: 12, of which 6 were waited for; matrix products, arithmetic and copies ran while one was open for 0% of the time, Pallas kernels for 25%

profile of v6, /device:TPU:0, one launch (start us, length us, event | category | flops | bytes accessed | tf_op | source)
XLA Modules:
  0.0 61.5 jit_solution(9343196033625417894)
XLA Ops:
  0.7 2.0 %first_pack.1 = (f32[8,128]{1,0:T(8,128)S(1)}, f32[8,128]{1,0:T(8,128)S(1)}, f32[64,2048]{1,0:T(8,128)}) custom-call(s32[1]{0:T(128)} %bitcast.1.group.group_ref, f32[64,1024]{1,0:T(8,128)} %e.3, f32[64,1024]{1,0:T(8,128)} %p.3, f32[8,64,2048]{2,1,0:T(8,128)} %v_right.1), custom_call_target="tpu_custom_call" | custom-call | tf_op jit(solution)/shard_map/first_pack/pallas_call | solution.py:508
  2.7 3.1 %collective-permute-start.8 = (f32[64,2048]{1,0:T(8,128)}, f32[64,2048]{1,0:T(8,128)S(1)}, u32[]{:S(2)}, u32[]{:S(2)}) collective-permute-start(f32[64,2048]{1,0:T(8,128)} %get-tuple-element.38), channel_id=1, source_target_pairs={{0,1},{1,0},{2,3},{3,2},{4,5},{5,4},{6,7},{7,6},{8,9},{9,8},{10,11... | collective-permute-start | bytes 1572872 | tf_op jit(solution)/shard_map/ppermute | solution.py:524
  5.9 1.8 %collective-permute-start.1 = (f32[8,128]{1,0:T(8,128)S(1)}, f32[8,128]{1,0:T(8,128)S(1)}, u32[]{:S(2)}, u32[]{:S(2)}) collective-permute-start(f32[8,128]{1,0:T(8,128)S(1)} %get-tuple-element.25), channel_id=1, source_target_pairs={{1,2},{3,4},{5,6},{7,0},{2,1},{4,3},{6,5},{0,7},{9,10},{11,12},{13... | collective-permute-start | bytes 12296 | tf_op jit(solution)/shard_map/ppermute | solution.py:525
  7.6 10.4 %collective-permute-done.seam = f32[8,128]{1,0:T(8,128)S(1)} collective-permute-done((f32[8,128]{1,0:T(8,128)S(1)}, f32[8,128]{1,0:T(8,128)S(1)}, u32[]{:S(2)}, u32[]{:S(2)}) %collective-permute-start) | collective-permute-done | bytes 4128 | tf_op jit(solution)/shard_map/ppermute | solution.py:523
  18.1 0.1 row_pack.1
  18.2 1.9 %collective-permute-start.2 = (f32[8,1664]{1,0:T(8,128)S(1)}, f32[8,1664]{1,0:T(8,128)S(1)}, u32[]{:S(2)}, u32[]{:S(2)}) collective-permute-start(f32[8,1664]{1,0:T(8,128)S(1)} %get-tuple-element.26), channel_id=1, source_target_pairs={{0,8},{16,24},{8,0},{24,16},{1,9},{17,25},{9,1},{25,17},{2,10},{18... | collective-permute-start | bytes 159752 | tf_op jit(solution)/shard_map/ppermute | solution.py:585
  20.1 2.5 %collective-permute-start.3 = (f32[8,1664]{1,0:T(8,128)S(1)}, f32[8,1664]{1,0:T(8,128)S(1)}, u32[]{:S(2)}, u32[]{:S(2)}) collective-permute-start(f32[8,1664]{1,0:T(8,128)S(1)} %get-tuple-element.27), channel_id=1, source_target_pairs={{8,16},{24,0},{16,8},{0,24},{9,17},{25,1},{17,9},{1,25},{10,18},{2... | collective-permute-start | bytes 159752 | tf_op jit(solution)/shard_map/ppermute | solution.py:585
  22.6 3.4 %collective-permute-done.3.row_b = f32[8,1664]{1,0:T(8,128)S(1)} collective-permute-done((f32[8,1664]{1,0:T(8,128)S(1)}, f32[8,1664]{1,0:T(8,128)S(1)}, u32[]{:S(2)}, u32[]{:S(2)}) %collective-permute-start.3) | collective-permute-done | bytes 53280 | tf_op jit(solution)/shard_map/ppermute | solution.py:585
  26.0 3.1 %surface.1 = (f32[64,1024]{1,0:T(8,128)}, f32[64,1024]{1,0:T(8,128)}, f32[72,1024]{1,0:T(8,128)S(1)}, f32[10,88,128]{2,1,0:T(8,128)S(1)}, f32[10,88,128]{2,1,0:T...) custom-call(s32[1]{0:T(128)} %bitcast.odd_x, f32[64,1024]{1,0:T(8,128)S(1)} %copy-done.2, ...), custom_call_target="tpu_custom_call" | custom-call | tf_op jit(solution)/shard_map/surface/pallas_call | solution.py:593
  29.2 2.5 %copy-done = f32[8,18,80,128]{3,2,1,0:T(8,128)} copy-done((f32[8,18,80,128]{3,2,1,0:T(8,128)}, f32[8,18,80,128]{3,2,1,0:T(8,128)S(1)}, u32[]{:S(2)}) %copy-start) | copy-done | bytes 5898264
  31.7 1.6 %collective-permute-start.10 = (f32[72,1024]{1,0:T(8,128)S(1)}, f32[72,1024]{1,0:T(8,128)S(1)}, u32[]{:S(2)}, u32[]{:S(2)}) collective-permute-start(f32[72,1024]{1,0:T(8,128)S(1)} %get-tuple-element.39.after), channel_id=1, source_target_pairs={{0,1},{1,0},{2,3},{3,2},{4,5},{5,4},{6,7},{7,6},{8,9},{9,8},{10,11... | collective-permute-start | bytes 884744 | tf_op jit(solution)/shard_map/ppermute | solution.py:615
  33.2 0.5 collective-permute-start.11
  33.7 1.8 %lazy_pack.1 = (f32[8,2304]{1,0:T(8,128)S(1)}, f32[8,2304]{1,0:T(8,128)S(1)}, f32[8,128]{1,0:T(8,128)S(1)}, f32[8,128]{1,0:T(8,128)S(1)}) custom-call(s32[1]{0:T(128)} %bitcast.odd_x, s32[1]{0:T(128)} %bitcast.2.odd_y, f32[8,64,2048]{2,1,0:T(8,128)} %v_right.1, f32[8,64,2048]{2,1,0:T(8,128)} %v_right.1, f32[8,64,2048]{2,1,0:T(8,128)} %v_right.1, ...), custom_call_target="tpu_custom_call" | custom-call | tf_op jit(solution)/shard_map/lazy_pack/pallas_call | solution.py:539
  35.6 1.6 %collective-permute-start.7 = (f32[8,128]{1,0:T(8,128)S(1)}, f32[8,128]{1,0:T(8,128)S(1)}, u32[]{:S(2)}, u32[]{:S(2)}) collective-permute-start(f32[8,128]{1,0:T(8,128)S(1)} %get-tuple-element.35), channel_id=1, source_target_pairs={{2,4},{6,0},{4,2},{0,6},{3,5},{7,1},{5,3},{1,7},{10,12},{14,8},{12... | collective-permute-start | bytes 12296 | tf_op jit(solution)/shard_map/ppermute | solution.py:585
  37.2 1.5 %collective-permute-done.7.x_b = f32[8,128]{1,0:T(8,128)S(1)} collective-permute-done((f32[8,128]{1,0:T(8,128)S(1)}, f32[8,128]{1,0:T(8,128)S(1)}, u32[]{:S(2)}, u32[]{:S(2)}) %collective-permute-start.7) | collective-permute-done | bytes 4128 | tf_op jit(solution)/shard_map/ppermute | solution.py:585
  38.7 2.5 %collective-permute-start.5 = (f32[8,2304]{1,0:T(8,128)S(1)}, f32[8,2304]{1,0:T(8,128)S(1)}, u32[]{:S(2)}, u32[]{:S(2)}) collective-permute-start(f32[8,2304]{1,0:T(8,128)S(1)} %get-tuple-element.33), channel_id=1, source_target_pairs={{8,16},{24,0},{16,8},{0,24},{9,17},{25,1},{17,9},{1,25},{10,18},{2... | collective-permute-start | bytes 221192 | tf_op jit(solution)/shard_map/ppermute | solution.py:585
  41.1 0.4 collective-permute-done.4.far_a
  41.5 3.8 %collective-permute-done.5.far_b = f32[8,2304]{1,0:T(8,128)S(1)} collective-permute-done((f32[8,2304]{1,0:T(8,128)S(1)}, f32[8,2304]{1,0:T(8,128)S(1)}, u32[]{:S(2)}, u32[]{:S(2)}) %collective-permute-start.5) | collective-permute-done | bytes 73760 | tf_op jit(solution)/shard_map/ppermute | solution.py:585
  45.5 1.6 %collective-permute-start.9 = (f32[8,1024]{1,0:T(8,128)S(1)}, f32[8,1024]{1,0:T(8,128)S(1)}, u32[]{:S(2)}, u32[]{:S(2)}) collective-permute-start(f32[8,1024]{1,0:T(8,128)S(1)} %rim_pack.1), channel_id=1, source_target_pairs={{0,1},{1,0},{2,3},{3,2},{4,5},{5,4},{6,7},{7,6},{8,9},{9,8},{10,11... | collective-permute-start | bytes 98312 | tf_op jit(solution)/shard_map/ppermute | solution.py:614
  47.0 0.7 %fill.1 = (f32[8,18,80,128]{3,2,1,0:T(8,128)S(1)}, f32[18,80,128]{2,1,0:T(8,128)S(1)}) custom-call(s32[1]{0:T(128)} %bitcast.odd_x, s32[1]{0:T(128)} %bitcast.2.odd_y, f32[8,18,80,128]{3,2,1,0:T(8,128)S(1)} %bitcast.4, f32[18,80,128]{2,1,0:T(8,128)S(1)} %get-tuple-element.31.old_depth, ...), custom_call_target="tpu_custom_call", output_to_operand_aliasing={{0}: (2, {}), {1}: (3, {})} | custom-call | tf_op jit(solution)/shard_map/fill/pallas_call | solution.py:617
  47.7 1.7 %collective-permute-done.9.rims = f32[8,1024]{1,0:T(8,128)S(1)} collective-permute-done((f32[8,1024]{1,0:T(8,128)S(1)}, f32[8,1024]{1,0:T(8,128)S(1)}, u32[]{:S(2)}, u32[]{:S(2)}) %collective-permute-start.9) | collective-permute-done | bytes 32800 | tf_op jit(solution)/shard_map/ppermute | solution.py:614
  49.4 4.7 %own_half.1.before = f32[8,64,2048]{2,1,0:T(8,128)} custom-call(s32[1]{0:T(128)} %bitcast.1.group.group_ref, f32[8,18,80,128]{3,2,1,0:T(8,128)S(1)} %get-tuple-element.36.volume, f32[18,80,128]{2,1,0:T(8,128)S(1)} %get-tuple-element.37.depth, f32[64,2048]{1,0:T(8,128)S(1)} %collective-permute-done.8.far_layer, f32[8,1024]{1,0:T(8,128)S(1)} %collective-permute-done.9.rims, ...), custom_call_target="tpu_custom_call" | custom-call | tf_op jit(solution)/shard_map/own_half/pallas_call | solution.py:636
  54.1 4.8 %other_half.1 = (f32[8,64,2048]{2,1,0:T(8,128)}, f32[64,1024]{1,0:T(8,128)S(1)}, f32[3,64,1024]{2,1,0:T(8,128)S(1)}) custom-call(s32[1]{0:T(128)} %bitcast.1.group.group_ref, f32[8,64,2048]{2,1,0:T(8,128)} %own_half.1.before, f32[8,18,80,128]{3,2,1,0:T(8,128)S(1)} %get-tuple-element.36.volume, ...), custom_call_target="tpu_custom_call", output_to_operand_aliasing={{0}: (1, {})} | custom-call | tf_op jit(solution)/shard_map/other_half/pallas_call | solution.py:649
  58.9 2.6 %top.1 = f32[8,64,2048]{2,1,0:T(8,128)} custom-call(s32[1]{0:T(128)} %bitcast.1.group.group_ref, f32[8,64,2048]{2,1,0:T(8,128)} %get-tuple-element.42.before, f32[64,1024]{1,0:T(8,128)S(1)} %get-tuple-element.43.part, f32[3,64,1024]{2,1,0:T(8,128)S(1)} %get-tuple-element.44.coefficients, ...), custom_call_target="tpu_custom_call", output_to_operand_aliasing={{}: (1, {})} | custom-call | tf_op jit(solution)/shard_map/top/pallas_call | solution.py:667
  (23 shorter events, 0.4 us)
Async XLA Ops:
  0.6 17.4 %copy-start.2 = (f32[64,1024]{1,0:T(8,128)S(1)}, f32[64,1024]{1,0:T(8,128)}, u32[]{:S(2)}) copy-start(f32[64,1024]{1,0:T(8,128)} %e.3) | copy-start | bytes 786436
  0.6 17.4 %copy-start.3 = (f32[64,1024]{1,0:T(8,128)S(1)}, f32[64,1024]{1,0:T(8,128)}, u32[]{:S(2)}) copy-start(f32[64,1024]{1,0:T(8,128)} %p.3) | copy-start | bytes 786436
  0.7 25.3 %copy-start.1 = (s32[64,2048]{1,0:T(8,128)S(1)}, s32[64,2048]{1,0:T(8,128)}, u32[]{:S(2)}) copy-start(s32[64,2048]{1,0:T(8,128)} %s_right.1) | copy-start | bytes 1572868
  2.7 46.7 %collective-permute-start.8 = (f32[64,2048]{1,0:T(8,128)}, f32[64,2048]{1,0:T(8,128)S(1)}, u32[]{:S(2)}, u32[]{:S(2)}) collective-permute-start(f32[64,2048]{1,0:T(8,128)} %get-tuple-element.38), channel_id=1, source_target_pairs={{0,1},{1,0},{2,3},{3,2},{4,5},{5,4},{6,7},{7,6},{8,9},{9,8},{10,11... | collective-permute-start | bytes 1572872 | tf_op jit(solution)/shard_map/ppermute | solution.py:524
  5.8 12.3 %collective-permute-start = (f32[8,128]{1,0:T(8,128)S(1)}, f32[8,128]{1,0:T(8,128)S(1)}, u32[]{:S(2)}, u32[]{:S(2)}) collective-permute-start(f32[8,128]{1,0:T(8,128)S(1)} %get-tuple-element.24), channel_id=1, source_target_pairs={{0,1},{1,0},{2,3},{3,2},{4,5},{5,4},{6,7},{7,6},{8,9},{9,8},{10,11... | collective-permute-start | bytes 12296 | tf_op jit(solution)/shard_map/ppermute | solution.py:523
  5.9 12.2 %collective-permute-start.1 = (f32[8,128]{1,0:T(8,128)S(1)}, f32[8,128]{1,0:T(8,128)S(1)}, u32[]{:S(2)}, u32[]{:S(2)}) collective-permute-start(f32[8,128]{1,0:T(8,128)S(1)} %get-tuple-element.25), channel_id=1, source_target_pairs={{1,2},{3,4},{5,6},{7,0},{2,1},{4,3},{6,5},{0,7},{9,10},{11,12},{13... | collective-permute-start | bytes 12296 | tf_op jit(solution)/shard_map/ppermute | solution.py:525
  18.2 4.4 %collective-permute-start.2 = (f32[8,1664]{1,0:T(8,128)S(1)}, f32[8,1664]{1,0:T(8,128)S(1)}, u32[]{:S(2)}, u32[]{:S(2)}) collective-permute-start(f32[8,1664]{1,0:T(8,128)S(1)} %get-tuple-element.26), channel_id=1, source_target_pairs={{0,8},{16,24},{8,0},{24,16},{1,9},{17,25},{9,1},{25,17},{2,10},{18... | collective-permute-start | bytes 159752 | tf_op jit(solution)/shard_map/ppermute | solution.py:585
  20.1 5.9 %collective-permute-start.3 = (f32[8,1664]{1,0:T(8,128)S(1)}, f32[8,1664]{1,0:T(8,128)S(1)}, u32[]{:S(2)}, u32[]{:S(2)}) collective-permute-start(f32[8,1664]{1,0:T(8,128)S(1)} %get-tuple-element.27), channel_id=1, source_target_pairs={{8,16},{24,0},{16,8},{0,24},{9,17},{25,1},{17,9},{1,25},{10,18},{2... | collective-permute-start | bytes 159752 | tf_op jit(solution)/shard_map/ppermute | solution.py:585
  29.1 2.5 %copy-start = (f32[8,18,80,128]{3,2,1,0:T(8,128)}, f32[8,18,80,128]{3,2,1,0:T(8,128)S(1)}, u32[]{:S(2)}) copy-start(f32[8,18,80,128]{3,2,1,0:T(8,128)S(1)} %get-tuple-element.30.old_volume) | copy-start | bytes 17694724
  31.7 22.5 %collective-permute-start.10 = (f32[72,1024]{1,0:T(8,128)S(1)}, f32[72,1024]{1,0:T(8,128)S(1)}, u32[]{:S(2)}, u32[]{:S(2)}) collective-permute-start(f32[72,1024]{1,0:T(8,128)S(1)} %get-tuple-element.39.after), channel_id=1, source_target_pairs={{0,1},{1,0},{2,3},{3,2},{4,5},{5,4},{6,7},{7,6},{8,9},{9,8},{10,11... | collective-permute-start | bytes 884744 | tf_op jit(solution)/shard_map/ppermute | solution.py:615
  33.2 25.7 %collective-permute-start.11 = (f32[64,1024]{1,0:T(8,128)}, f32[64,1024]{1,0:T(8,128)}, u32[]{:S(2)}, u32[]{:S(2)}) collective-permute-start(f32[64,1024]{1,0:T(8,128)} %get-tuple-element.22), channel_id=1, source_target_pairs={{0,1},{1,0},{2,3},{3,2},{4,5},{5,4},{6,7},{7,6},{8,9},{9,8},{10,11... | collective-permute-start | bytes 786440 | tf_op jit(solution)/shard_map/ppermute | solution.py:616
  33.7 13.3 %slice-start = ((s8[5898240]{0:T(1024)(128)(4,1)}), s8[4194304]{0:T(1024)(128)(4,1)S(1)}, s32[]{:S(2)}) async-start(s8[5898240]{0:T(1024)(128)(4,1)} %bitcast.3), calls=%async_computation | async-start | bytes 8388608
  33.7 13.3 %slice-start.1 = ((s8[5898240]{0:T(1024)(128)(4,1)}), s8[1703936]{0:T(1024)(128)(4,1)S(1)}, s32[]{:S(2)}) async-start(s8[5898240]{0:T(1024)(128)(4,1)} %bitcast.3), calls=%async_computation.1 | async-start | bytes 3407872
  35.5 1.7 %collective-permute-start.6 = (f32[8,128]{1,0:T(8,128)S(1)}, f32[8,128]{1,0:T(8,128)S(1)}, u32[]{:S(2)}, u32[]{:S(2)}) collective-permute-start(f32[8,128]{1,0:T(8,128)S(1)} %get-tuple-element.34), channel_id=1, source_target_pairs={{0,2},{4,6},{2,0},{6,4},{1,3},{5,7},{3,1},{7,5},{8,10},{12,14},{10... | collective-permute-start | bytes 12296 | tf_op jit(solution)/shard_map/ppermute | solution.py:585
  35.6 3.1 %collective-permute-start.7 = (f32[8,128]{1,0:T(8,128)S(1)}, f32[8,128]{1,0:T(8,128)S(1)}, u32[]{:S(2)}, u32[]{:S(2)}) collective-permute-start(f32[8,128]{1,0:T(8,128)S(1)} %get-tuple-element.35), channel_id=1, source_target_pairs={{2,4},{6,0},{4,2},{0,6},{3,5},{7,1},{5,3},{1,7},{10,12},{14,8},{12... | collective-permute-start | bytes 12296 | tf_op jit(solution)/shard_map/ppermute | solution.py:585
  37.2 4.4 %collective-permute-start.4 = (f32[8,2304]{1,0:T(8,128)S(1)}, f32[8,2304]{1,0:T(8,128)S(1)}, u32[]{:S(2)}, u32[]{:S(2)}) collective-permute-start(f32[8,2304]{1,0:T(8,128)S(1)} %get-tuple-element.32), channel_id=1, source_target_pairs={{0,8},{16,24},{8,0},{24,16},{1,9},{17,25},{9,1},{25,17},{2,10},{18... | collective-permute-start | bytes 221192 | tf_op jit(solution)/shard_map/ppermute | solution.py:585
  38.7 6.7 %collective-permute-start.5 = (f32[8,2304]{1,0:T(8,128)S(1)}, f32[8,2304]{1,0:T(8,128)S(1)}, u32[]{:S(2)}, u32[]{:S(2)}) collective-permute-start(f32[8,2304]{1,0:T(8,128)S(1)} %get-tuple-element.33), channel_id=1, source_target_pairs={{8,16},{24,0},{16,8},{0,24},{9,17},{25,1},{17,9},{1,25},{10,18},{2... | collective-permute-start | bytes 221192 | tf_op jit(solution)/shard_map/ppermute | solution.py:585
  45.5 3.9 %collective-permute-start.9 = (f32[8,1024]{1,0:T(8,128)S(1)}, f32[8,1024]{1,0:T(8,128)S(1)}, u32[]{:S(2)}, u32[]{:S(2)}) collective-permute-start(f32[8,1024]{1,0:T(8,128)S(1)} %rim_pack.1), channel_id=1, source_target_pairs={{0,1},{1,0},{2,3},{3,2},{4,5},{5,4},{6,7},{7,6},{8,9},{9,8},{10,11... | collective-permute-start | bytes 98312 | tf_op jit(solution)/shard_map/ppermute | solution.py:614

commit v7 on v6

--- a/solution.py
+++ b/solution.py
@@ -25,7 +25,7 @@
     return jnp.concatenate([rest, tile] if at_end else [tile, rest], 0)
 
 
-def first_pack(group, e, p, v, seam, outer, layer, edges, sems):
+def first_pack(group, e, p, v, seam, outer, layer, v_top, v_bottom, v_left, v_right, edges, sems):
     rows, width = e.shape
     low = group[0] == 0
     source = jnp.where(low, v.shape[0] - 1, 0)
@@ -34,9 +34,23 @@
     for index, (field, start) in enumerate(((e, 0), (p, 0), (e, width - LANES), (p, width - LANES))):
         into = edges.at[index // 2, (index % 2) * rows : (index % 2 + 1) * rows, :]
         copies.append(pltpu.make_async_copy(field.at[:, start : start + LANES], into, sems.at[index]))
+    tile = v.shape[2]
+    ends = [
+        pltpu.make_async_copy(source, into, sems.at[5 + index])
+        for index, (source, into) in enumerate(
+            (
+                (v.at[:, :SUBS, :], v_top),
+                (v.at[:, rows - SUBS :, :], v_bottom),
+                (v.at[:, :, :LANES], v_left),
+                (v.at[:, :, tile - LANES :], v_right),
+            )
+        )
+    ]
     for copy in copies:
         copy.start()
     whole.start()
+    for copy in ends:
+        copy.start()
     for copy in copies:
         copy.wait()
     left = edges[0].T[:SUBS]
@@ -44,6 +58,8 @@
     seam[...] = jnp.where(low, right, left)
     outer[...] = jnp.where(low, left, right)
     whole.wait()
+    for copy in ends:
+        copy.wait()
 
 
 def by_parity(odd, fill, first, second):
@@ -165,10 +181,9 @@
 
 def surface(
     odd_x, e, p, side_tiles, group, row_a, row_b, v, sea,
-    new_e, new_p, height, wide_e, wide_p, volume, depth, e0, p0, e1, p1, sems,
+    new_e, new_p, wide_e, wide_p, volume, depth, e0, p0, e1, p1, sems,
 ):
     rows, width = e.shape
-    low = group[0] == 0
     left, right = side_tiles[0], side_tiles[1]
     copies = []
     for t in range(v.shape[2] // LANES):
@@ -222,43 +237,44 @@
     lax.fori_loop(0, blocks, second, 0, unroll=True)
     for t in range(1, tiles - 1):
         part = slice((t - 1) * LANES, t * LANES)
-        tile_e = wide_e[t, inner, :]
-        new_e[:, part] = tile_e
-        height[:rows, part] = tile_e
+        new_e[:, part] = wide_e[t, inner, :]
         new_p[:, part] = wide_p[t, inner, :]
-        for row, wide in ((0, wide_e), (2, wide_p)):
-            height[rows + row : rows + row + 1, part] = wide[t, SUBS - 1 : SUBS, :]
-            height[rows + row + 1 : rows + row + 2, part] = wide[t, SUBS + rows : SUBS + rows + 1, :]
-        height[rows + 4 :, part] = jnp.zeros((4, LANES), jnp.float32)
-    left = jnp.concatenate([wide_e[0, inner, :], wide_p[0, inner, :]], 0).T[LANES - 1 :]
-    right = jnp.concatenate([wide_e[tiles - 1, inner, :], wide_p[tiles - 1, inner, :]], 0).T[:1]
-    height[rows + 4 : rows + 5, :LANES] = jnp.where(low, left, right)
     for t in range(v.shape[2] // LANES):
         depth[t + 1, inner, :] = sea[:, t * LANES : (t + 1) * LANES].astype(jnp.float32) * depth_unit
     for copy in copies:
         copy.wait()
 
 
-def rim_pack(group, odd_x, odd_y, far_a, far_b, x_a, x_b, after, rims):
-    del after
+def rim_pack(group, odd_x, odd_y, far_a, far_b, x_a, x_b, wide_e, wide_p, rims):
     low = group[0] == 0
     layers = far_a.shape[0]
-    width = rims.shape[1]
+    width = rims.shape[1] - LANES
     pairs = layers // 2
-    rims[...] = jnp.zeros_like(rims)
+    last = width // LANES + 1
+    half_lanes = LANES // 2
+    inner = slice(SUBS, SUBS + half_lanes)
+    rims[:, width:] = jnp.zeros((SUBS, LANES), jnp.float32)
+    for row, wide in ((4, wide_e), (6, wide_p)):
+        for t in range(1, last):
+            part = slice((t - 1) * LANES, t * LANES)
+            rims[row : row + 1, part] = wide[t, SUBS - 1 : SUBS, :]
+            rims[row + 1 : row + 2, part] = wide[t, SUBS + half_lanes : SUBS + half_lanes + 1, :]
+    left = jnp.concatenate([wide_e[0, inner, :], wide_p[0, inner, :]], 0).T[LANES - 1 :]
+    right = jnp.concatenate([wide_e[last, inner, :], wide_p[last, inner, :]], 0).T[:1]
+    rims[2:3, width:] = jnp.where(low, left, right)
 
     def rows(far_south, far_north):
         for row, side in ((0, far_north), (2, far_south)):
             for half in range(2):
                 part = slice(half * width, (half + 1) * width)
-                rims[row + half : row + half + 1, :] = jnp.where(low, side[layers - 1 : layers, part], side[0:1, part])
+                rims[row + half : row + half + 1, :width] = jnp.where(low, side[layers - 1 : layers, part], side[0:1, part])
 
     by_parity(odd_x, rows, far_a, far_b)
 
     def columns(x_right, x_left):
-        for lane, side in ((0, x_left), (LANES, x_right)):
+        for row, side in ((0, x_left), (1, x_right)):
             top_pair = pltpu.roll(side[...], LANES // 2, 1)[pairs - 1 : pairs]
-            rims[4:5, lane : lane + LANES] = jnp.where(low, top_pair, side[0:1, :])
+            rims[row : row + 1, width:] = jnp.where(low, top_pair, side[0:1, :])
 
     by_parity(odd_y, columns, x_a, x_b)
 
@@ -401,11 +417,11 @@
         fill_ghost(group == 1, 1 - group, far_layer, rims, ghost)
         for t in range(halves):
             spot = slice(t * LANES, (t + 1) * LANES)
-            other_e[t + 1, inner, :] = height[:rows, spot]
-            other_e[t + 1, SUBS - 1 : SUBS, :] = height[rows : rows + 1, spot]
-            other_e[t + 1, SUBS + rows : SUBS + rows + 1, :] = height[rows + 1 : rows + 2, spot]
-        edge = square(height[rows:, :LANES], False).T[:rows]
-        at_right, at_left = pltpu.roll(edge, LANES - 4, 1), pltpu.roll(edge, LANES - 5, 1)
+            other_e[t + 1, inner, :] = height[:, spot]
+            other_e[t + 1, SUBS - 1 : SUBS, :] = rims[4:5, spot]
+            other_e[t + 1, SUBS + rows : SUBS + rows + 1, :] = rims[5:6, spot]
+        edge = square(rims[:, width:], False).T[:rows]
+        at_right, at_left = pltpu.roll(edge, LANES - 2, 1), pltpu.roll(edge, LANES - 3, 1)
         other_e[0, inner, :] = jnp.where(low, wide_e[halves, inner, :], at_left)
         other_e[halves + 1, inner, :] = jnp.where(low, at_right, wide_e[1, inner, :])
 
@@ -432,10 +448,9 @@
     width = tile // 2
     halves = width // LANES
     inner = slice(SUBS, SUBS + rows)
-    far_left = pltpu.roll(square(rims[:, :LANES], False).T, LANES - 5, 1)[:rows]
-    far_right = pltpu.roll(square(rims[:, LANES : 2 * LANES], False).T, LANES - 4, 1)[:rows]
-    ghost[0, inner, :] = jnp.where(first, far_left, far_layer[:, width - LANES : width])
-    ghost[halves + 1, inner, :] = jnp.where(first, far_layer[:, width : width + LANES], far_right)
+    side = pltpu.roll(square(rims[:, width:], False).T, LANES - 1, 1)[:rows]
+    ghost[0, inner, :] = jnp.where(first, side, far_layer[:, width - LANES : width])
+    ghost[halves + 1, inner, :] = jnp.where(first, far_layer[:, width : width + LANES], side)
     for t in range(halves):
         spot = slice(t * LANES, (t + 1) * LANES)
         lanes = pl.ds(pl.multiple_of(half * width + t * LANES, LANES), LANES)
@@ -444,20 +459,20 @@
         ghost[t + 1, SUBS + rows : SUBS + rows + 1, :] = jnp.where(first, rims[2:3, spot], rims[3:4, spot])
 
 
-def top(group_ref, before, part, coefficients, height, wide_p, other_p, out, potential):
+def top(group_ref, before, part, coefficients, rims, wide_p, other_p, out, potential):
     del before
     low = group_ref[0] == 0
     rows, width = other_p.shape
     halves = width // LANES
     inner = slice(SUBS, SUBS + rows)
-    edge = square(height[rows:, :LANES], False).T[LANES // 2 : LANES // 2 + rows]
-    potential[0, inner, :] = pltpu.roll(edge, LANES - 5, 1)
+    edge = square(rims[:, width:], False).T[LANES // 2 : LANES // 2 + rows]
+    potential[0, inner, :] = pltpu.roll(edge, LANES - 3, 1)
     potential[halves + 1, inner, :] = wide_p[1, inner, :]
     for t in range(halves):
         spot = slice(t * LANES, (t + 1) * LANES)
         potential[t + 1, inner, :] = other_p[:, spot]
-        potential[t + 1, SUBS - 1 : SUBS, :] = height[rows + 2 : rows + 3, spot]
-        potential[t + 1, SUBS + rows : SUBS + rows + 1, :] = height[rows + 3 : rows + 4, spot]
+        potential[t + 1, SUBS - 1 : SUBS, :] = rims[6:7, spot]
+        potential[t + 1, SUBS + rows : SUBS + rows + 1, :] = rims[7:8, spot]
 
     def body(block, carry):
         here = pl.multiple_of((block + 1) * SUBS, SUBS)
@@ -473,7 +488,7 @@
             out[0, to, spot] = jnp.where(low, partial, partial + 2.0 * value)
         return carry
 
-    lax.fori_loop(0, rows // SUBS, body, 0)
+    lax.fori_loop(0, rows // SUBS, body, 0, unroll=True)
 
 
 def couples(axis, shifted):
@@ -505,12 +520,14 @@
     params = pltpu.CompilerParams(vmem_limit_bytes=24 * 1024 * 1024)
     vmem = pl.BlockSpec(memory_space=pltpu.VMEM)
     hbm = pl.BlockSpec(memory_space=pltpu.HBM)
-    seam, outer, layer = pl.pallas_call(
+    seam, outer, layer, *ends = pl.pallas_call(
         first_pack,
-        out_shape=(shape(SUBS, LANES), shape(SUBS, LANES), shape(rows, tile)),
+        out_shape=(shape(SUBS, LANES), shape(SUBS, LANES), shape(rows, tile))
+        + (shape(layers, SUBS, tile),) * 2
+        + (shape(layers, rows, LANES),) * 2,
         in_specs=[scalar, hbm, hbm, hbm],
-        out_specs=[vmem] * 3,
-        scratch_shapes=[pltpu.VMEM((2, LANES, LANES), f32), pltpu.SemaphoreType.DMA((5,))],
+        out_specs=[vmem] * 7,
+        scratch_shapes=[pltpu.VMEM((2, LANES, LANES), f32), pltpu.SemaphoreType.DMA((9,))],
         compiler_params=params,
         name="first_pack",
     )(group, *(pltpu.with_memory_space_constraint(x, pltpu.HBM) for x in (elevation, surface_potential, interior_potential)))
@@ -543,10 +560,7 @@
         in_specs=[
             scalar,
             scalar,
-            block((layers, SUBS, tile), 0, 0, 0),
-            block((layers, SUBS, tile), 0, last_row, 0),
-            block((layers, rows, LANES), 0, 0, 0),
-            block((layers, rows, LANES), 0, 0, last_tile),
+            *[vmem] * 4,
             block((SUBS, tile), 0, 0),
             block((SUBS, tile), last_row, 0),
             block((rows, LANES), 0, 0),
@@ -555,7 +569,7 @@
         out_specs=[whole(SUBS, tile + tile // SUBS)] * 2 + [whole(SUBS, LANES)] * 2,
         compiler_params=params,
         name="lazy_pack",
-    )(odd_x, odd_y, *(pltpu.with_memory_space_constraint(interior_potential, pltpu.HBM),) * 4, *(seabed,) * 4)
+    )(odd_x, odd_y, *ends, *(seabed,) * 4)
 
     wide = width + 2 * LANES
     packed = wide + pl.cdiv((2 * REACH - SUBS) * (wide // LANES), SUBS) * LANES
@@ -590,11 +604,11 @@
     tables = (shape(layers, tiles + 2, tall, LANES), shape(tiles + 2, tall, LANES))
     deep = rows + 3 * SUBS
     padded = (width // LANES + 2, deep, LANES)
-    new_e, new_p, height, wide_e, wide_p, volume, depth = pl.pallas_call(
+    new_e, new_p, wide_e, wide_p, volume, depth = pl.pallas_call(
         surface,
-        out_shape=(shape(rows, width),) * 2 + (shape(rows + SUBS, width),) + (shape(*padded),) * 2 + tables,
+        out_shape=(shape(rows, width),) * 2 + (shape(*padded),) * 2 + tables,
         in_specs=[scalar] + [vmem] * 3 + [scalar] + [vmem] * 2 + [hbm, vmem],
-        out_specs=[vmem] * 7,
+        out_specs=[vmem] * 6,
         scratch_shapes=[pltpu.VMEM(padded, f32)] * 4 + [pltpu.SemaphoreType.DMA((tiles,))],
         compiler_params=params,
         name="surface",
@@ -605,14 +619,14 @@
     far_sides = [sides[name] for name in ("far_a", "far_b", "x_a", "x_b")]
     rims = pl.pallas_call(
         rim_pack,
-        out_shape=shape(SUBS, width),
-        in_specs=[scalar] * 3 + [vmem] * 4 + [anywhere],
+        out_shape=shape(SUBS, width + LANES),
+        in_specs=[scalar] * 3 + [vmem] * 6,
         out_specs=vmem,
         compiler_params=params,
         name="rim_pack",
-    )(group, odd_x, odd_y, *far_sides, height)
+    )(group, odd_x, odd_y, *far_sides, wide_e, wide_p)
     far_rims = lax.ppermute(rims, flat, partner)
-    far_height = lax.ppermute(height, flat, partner)
+    far_height = lax.ppermute(new_e, flat, partner)
     other_p = lax.ppermute(new_p, flat, partner)
     volume, depth = pl.pallas_call(
         fill,
@@ -677,7 +691,7 @@
         input_output_aliases={1: 0},
         compiler_params=params,
         name="top",
-    )(group, partial, part, coefficients, far_height, wide_p, other_p)
+    )(group, partial, part, coefficients, far_rims, wide_p, other_p)
     return new_e, new_p, result
 
 

time: 61.7 us -> 71.7 us (1.16)
  the two profiles are of different devices: /device:TPU:0 before, /device:TPU:1 now
where the time goes in v7:
time: 71.7 us; the launch traced here: 70.4 us
  waiting for transfers between devices  19 us (26%)
  Pallas kernels  17.4 us (24%)
  local copies, waits for them, and re-layouts  16.7 us (23%)
  starting transfers between devices  16.5 us (23%)
  between operations  0.78 us (1%)
    unnamed x32, local copies, waits for them, and re-layouts  16.7 us
    ppermute x1, waiting for transfers between devices, shards(): seam = lax.ppermute(seam, flat, partner)  9.38 us
    ppermute x6, starting transfers between devices, shards(): sides[name] = lax.ppermute(value, axis, couples(axis, shifted))  9.14 us
    ppermute x6, waiting for transfers between devices, shards(): sides[name] = lax.ppermute(value, axis, couples(axis, shifted))  8.75 us
    pallas_call x1, Pallas kernels, shards(): pl.pallas_call(functools.partial(own_half, total_layers), out_shape=shape...  4.7 us
    pallas_call x1, Pallas kernels, shards(): pl.pallas_call(functools.partial(other_half, total_layers), out_shape=(sh...  4.69 us
    pallas_call x1, Pallas kernels, shards(): pl.pallas_call(surface, out_shape=(shape(rows, width),) * 2 + (shape(*pad...  3.15 us
    ppermute x1, starting transfers between devices, shards(): outer = lax.ppermute(outer, flat, across)  2.57 us
  transfers between devices with their start and end apart: 12, of which 5 were waited for; matrix products, arithmetic and copies ran while one was open for 0% of the time, Pallas kernels for 20%

profile of v7, /device:TPU:1, one launch (start us, length us, event | category | flops | bytes accessed | tf_op | source)
XLA Modules:
  0.0 70.4 jit_solution(11471462366672208188)
XLA Ops:
  0.7 2.5 %first_pack.1 = (f32[8,128]{1,0:T(8,128)S(1)}, f32[8,128]{1,0:T(8,128)S(1)}, f32[64,2048]{1,0:T(8,128)}, f32[8,8,2048]{2,1,0:T(8,128)S(1)}, f32[8,8,2048]{2,1,0:...) custom-call(s32[1]{0:T(128)} %bitcast.1.group.group_ref, f32[64,1024]{1,0:T(8,128)} %e.3, ...), custom_call_target="tpu_custom_call" | custom-call | tf_op jit(solution)/shard_map/first_pack/pallas_call | solution.py:523
  5.5 2.1 %collective-permute-start.8 = (f32[64,2048]{1,0:T(8,128)}, f32[64,2048]{1,0:T(8,128)S(1)}, u32[]{:S(2)}, u32[]{:S(2)}) collective-permute-start(f32[64,2048]{1,0:T(8,128)} %get-tuple-element.45), channel_id=1, source_target_pairs={{0,1},{1,0},{2,3},{3,2},{4,5},{5,4},{6,7},{7,6},{8,9},{9,8},{10,11... | collective-permute-start | bytes 1572872 | tf_op jit(solution)/shard_map/ppermute | solution.py:541
  7.6 2.6 %collective-permute-start.1 = (f32[8,128]{1,0:T(8,128)S(1)}, f32[8,128]{1,0:T(8,128)S(1)}, u32[]{:S(2)}, u32[]{:S(2)}) collective-permute-start(f32[8,128]{1,0:T(8,128)S(1)} %get-tuple-element.28), channel_id=1, source_target_pairs={{1,2},{3,4},{5,6},{7,0},{2,1},{4,3},{6,5},{0,7},{9,10},{11,12},{13... | collective-permute-start | bytes 12296 | tf_op jit(solution)/shard_map/ppermute | solution.py:542
  10.2 9.4 %collective-permute-done.seam = f32[8,128]{1,0:T(8,128)S(1)} collective-permute-done((f32[8,128]{1,0:T(8,128)S(1)}, f32[8,128]{1,0:T(8,128)S(1)}, u32[]{:S(2)}, u32[]{:S(2)}) %collective-permute-start) | collective-permute-done | bytes 4128 | tf_op jit(solution)/shard_map/ppermute | solution.py:540
  20.5 1.6 %collective-permute-start.2 = (f32[8,1664]{1,0:T(8,128)S(1)}, f32[8,1664]{1,0:T(8,128)S(1)}, u32[]{:S(2)}, u32[]{:S(2)}) collective-permute-start(f32[8,1664]{1,0:T(8,128)S(1)} %get-tuple-element.29), channel_id=1, source_target_pairs={{0,8},{16,24},{8,0},{24,16},{1,9},{17,25},{9,1},{25,17},{2,10},{18... | collective-permute-start | bytes 159752 | tf_op jit(solution)/shard_map/ppermute | solution.py:599
  22.1 2.2 %collective-permute-start.3 = (f32[8,1664]{1,0:T(8,128)S(1)}, f32[8,1664]{1,0:T(8,128)S(1)}, u32[]{:S(2)}, u32[]{:S(2)}) collective-permute-start(f32[8,1664]{1,0:T(8,128)S(1)} %get-tuple-element.30), channel_id=1, source_target_pairs={{8,16},{24,0},{16,8},{0,24},{9,17},{25,1},{17,9},{1,25},{10,18},{2... | collective-permute-start | bytes 159752 | tf_op jit(solution)/shard_map/ppermute | solution.py:599
  24.4 2.9 %collective-permute-done.3.row_b = f32[8,1664]{1,0:T(8,128)S(1)} collective-permute-done((f32[8,1664]{1,0:T(8,128)S(1)}, f32[8,1664]{1,0:T(8,128)S(1)}, u32[]{:S(2)}, u32[]{:S(2)}) %collective-permute-start.3) | collective-permute-done | bytes 53280 | tf_op jit(solution)/shard_map/ppermute | solution.py:599
  27.4 3.1 %surface.1 = (f32[64,1024]{1,0:T(8,128)}, f32[64,1024]{1,0:T(8,128)}, f32[10,88,128]{2,1,0:T(8,128)S(1)}, f32[10,88,128]{2,1,0:T(8,128)S(1)}, f32[8,18,80,128]{3...) custom-call(s32[1]{0:T(128)} %bitcast.odd_x, f32[64,1024]{1,0:T(8,128)S(1)} %copy-done.6, f32[64,1024]{1,0:T(8,128)S(1)} %copy-done.7, ...), custom_call_target="tpu_custom_call" | custom-call | tf_op jit(solution)/shard_map/surface/pallas_call | solution.py:607
  30.5 2.5 %copy-done = f32[8,18,80,128]{3,2,1,0:T(8,128)} copy-done((f32[8,18,80,128]{3,2,1,0:T(8,128)}, f32[8,18,80,128]{3,2,1,0:T(8,128)S(1)}, u32[]{:S(2)}) %copy-start) | copy-done | bytes 5898264
  33.1 1.5 %collective-permute-start.11 = (f32[64,1024]{1,0:T(8,128)}, f32[64,1024]{1,0:T(8,128)S(1)}, u32[]{:S(2)}, u32[]{:S(2)}) collective-permute-start(f32[64,1024]{1,0:T(8,128)} %get-tuple-element.25), channel_id=1, source_target_pairs={{0,1},{1,0},{2,3},{3,2},{4,5},{5,4},{6,7},{7,6},{8,9},{9,8},{10,11... | collective-permute-start | bytes 786440 | tf_op jit(solution)/shard_map/ppermute | solution.py:630
  34.5 1.0 %copy-done.9 = f32[8,8,2048]{2,1,0:T(8,128)S(1)} copy-done((f32[8,8,2048]{2,1,0:T(8,128)S(1)}, f32[8,8,2048]{2,1,0:T(8,128)}, u32[]{:S(2)}) %copy-start.9) | copy-done | bytes 524312
  35.6 1.0 %copy-done.11 = f32[8,8,2048]{2,1,0:T(8,128)S(1)} copy-done((f32[8,8,2048]{2,1,0:T(8,128)S(1)}, f32[8,8,2048]{2,1,0:T(8,128)}, u32[]{:S(2)}) %copy-start.11) | copy-done | bytes 524312
  38.8 2.0 %collective-permute-start.6 = (f32[8,128]{1,0:T(8,128)S(1)}, f32[8,128]{1,0:T(8,128)S(1)}, u32[]{:S(2)}, u32[]{:S(2)}) collective-permute-start(f32[8,128]{1,0:T(8,128)S(1)} %get-tuple-element.41), channel_id=1, source_target_pairs={{0,2},{4,6},{2,0},{6,4},{1,3},{5,7},{3,1},{7,5},{8,10},{12,14},{10... | collective-permute-start | bytes 12296 | tf_op jit(solution)/shard_map/ppermute | solution.py:599
  40.8 1.2 %collective-permute-start.7 = (f32[8,128]{1,0:T(8,128)S(1)}, f32[8,128]{1,0:T(8,128)S(1)}, u32[]{:S(2)}, u32[]{:S(2)}) collective-permute-start(f32[8,128]{1,0:T(8,128)S(1)} %get-tuple-element.42), channel_id=1, source_target_pairs={{2,4},{6,0},{4,2},{0,6},{3,5},{7,1},{5,3},{1,7},{10,12},{14,8},{12... | collective-permute-start | bytes 12296 | tf_op jit(solution)/shard_map/ppermute | solution.py:599
  42.0 2.1 %collective-permute-done.7.x_b = f32[8,128]{1,0:T(8,128)S(1)} collective-permute-done((f32[8,128]{1,0:T(8,128)S(1)}, f32[8,128]{1,0:T(8,128)S(1)}, u32[]{:S(2)}, u32[]{:S(2)}) %collective-permute-start.7) | collective-permute-done | bytes 4128 | tf_op jit(solution)/shard_map/ppermute | solution.py:599
  44.1 2.2 %collective-permute-start.5 = (f32[8,2304]{1,0:T(8,128)S(1)}, f32[8,2304]{1,0:T(8,128)S(1)}, u32[]{:S(2)}, u32[]{:S(2)}) collective-permute-start(f32[8,2304]{1,0:T(8,128)S(1)} %get-tuple-element.40), channel_id=1, source_target_pairs={{8,16},{24,0},{16,8},{0,24},{9,17},{25,1},{17,9},{1,25},{10,18},{2... | collective-permute-start | bytes 221192 | tf_op jit(solution)/shard_map/ppermute | solution.py:599
  46.3 3.7 %collective-permute-done.5.far_b = f32[8,2304]{1,0:T(8,128)S(1)} collective-permute-done((f32[8,2304]{1,0:T(8,128)S(1)}, f32[8,2304]{1,0:T(8,128)S(1)}, u32[]{:S(2)}, u32[]{:S(2)}) %collective-permute-start.5) | collective-permute-done | bytes 73760 | tf_op jit(solution)/shard_map/ppermute | solution.py:599
  50.2 1.3 %collective-permute-start.9 = (f32[8,1152]{1,0:T(8,128)S(1)}, f32[8,1152]{1,0:T(8,128)S(1)}, u32[]{:S(2)}, u32[]{:S(2)}) collective-permute-start(f32[8,1152]{1,0:T(8,128)S(1)} %rim_pack.1), channel_id=1, source_target_pairs={{0,1},{1,0},{2,3},{3,2},{4,5},{5,4},{6,7},{7,6},{8,9},{9,8},{10,11... | collective-permute-start | bytes 110600 | tf_op jit(solution)/shard_map/ppermute | solution.py:628
  51.5 2.7 %copy-done.1 = f32[8,18,80,128]{3,2,1,0:T(8,128)S(1)} copy-done((f32[8,18,80,128]{3,2,1,0:T(8,128)S(1)}, f32[8,18,80,128]{3,2,1,0:T(8,128)}, u32[]{:S(2)}) %copy-start.1) | copy-done | bytes 5898264
  54.8 2.5 %copy-done.2 = f32[8,18,80,128]{3,2,1,0:T(8,128)} copy-done((f32[8,18,80,128]{3,2,1,0:T(8,128)}, f32[8,18,80,128]{3,2,1,0:T(8,128)S(1)}, u32[]{:S(2)}) %copy-start.2) | copy-done | bytes 5898264
  57.4 2.7 %copy-done.3 = f32[8,18,80,128]{3,2,1,0:T(8,128)S(1)} copy-done((f32[8,18,80,128]{3,2,1,0:T(8,128)S(1)}, f32[8,18,80,128]{3,2,1,0:T(8,128)}, u32[]{:S(2)}) %copy-start.3) | copy-done | bytes 5898264
  60.0 4.7 %own_half.1.before = f32[8,64,2048]{2,1,0:T(8,128)} custom-call(s32[1]{0:T(128)} %bitcast.1.group.group_ref, f32[8,18,80,128]{3,2,1,0:T(8,128)S(1)} %copy-done.3, f32[18,80,128]{2,1,0:T(8,128)S(1)} %get-tuple-element.44.depth, f32[64,2048]{1,0:T(8,128)S(1)} %collective-permute-done.8.far_layer, f32[8,1152]{1,0:T(8,128)S(1)} %collective-permute-done.9.rims, ...), custom_call_target="tpu_custom_call" | custom-call | tf_op jit(solution)/shard_map/own_half/pallas_call | solution.py:650
  64.7 4.7 %other_half.1 = (f32[8,64,2048]{2,1,0:T(8,128)}, f32[64,1024]{1,0:T(8,128)S(1)}, f32[3,64,1024]{2,1,0:T(8,128)S(1)}) custom-call(s32[1]{0:T(128)} %bitcast.1.group.group_ref, f32[8,64,2048]{2,1,0:T(8,128)} %own_half.1.before, f32[8,18,80,128]{3,2,1,0:T(8,128)S(1)} %copy-done.4, ...), custom_call_target="tpu_custom_call", output_to_operand_aliasing={{0}: (1, {})} | custom-call | tf_op jit(solution)/shard_map/other_half/pallas_call | solution.py:663
  69.4 1.0 %top.1 = f32[8,64,2048]{2,1,0:T(8,128)} custom-call(s32[1]{0:T(128)} %bitcast.1.group.group_ref, f32[8,64,2048]{2,1,0:T(8,128)} %get-tuple-element.48.before, f32[64,1024]{1,0:T(8,128)S(1)} %get-tuple-element.49.part, f32[3,64,1024]{2,1,0:T(8,128)S(1)} %get-tuple-element.50.coefficients, ...), custom_call_target="tpu_custom_call", output_to_operand_aliasing={{}: (1, {})} | custom-call | tf_op jit(solution)/shard_map/top/pallas_call | solution.py:681
  (42 shorter events, 6.4 us)
Async XLA Ops:
  0.6 19.8 %copy-start.6 = (f32[64,1024]{1,0:T(8,128)S(1)}, f32[64,1024]{1,0:T(8,128)}, u32[]{:S(2)}) copy-start(f32[64,1024]{1,0:T(8,128)} %e.3) | copy-start | bytes 786436
  0.6 19.8 %copy-start.7 = (f32[64,1024]{1,0:T(8,128)S(1)}, f32[64,1024]{1,0:T(8,128)}, u32[]{:S(2)}) copy-start(f32[64,1024]{1,0:T(8,128)} %p.3) | copy-start | bytes 786436
  0.7 26.7 %copy-start.5 = (s32[64,2048]{1,0:T(8,128)S(1)}, s32[64,2048]{1,0:T(8,128)}, u32[]{:S(2)}) copy-start(s32[64,2048]{1,0:T(8,128)} %s_right.1) | copy-start | bytes 1572868
  5.5 18.9 %copy-start.14 = (f32[8,64,128]{2,1,0:T(8,128)}, f32[8,64,128]{2,1,0:T(8,128)S(1)}, u32[]{:S(2)}) copy-start(f32[8,64,128]{2,1,0:T(8,128)S(1)} %get-tuple-element.38.v_right) | copy-start | bytes 786436
  5.5 51.8 %collective-permute-start.8 = (f32[64,2048]{1,0:T(8,128)}, f32[64,2048]{1,0:T(8,128)S(1)}, u32[]{:S(2)}, u32[]{:S(2)}) collective-permute-start(f32[64,2048]{1,0:T(8,128)} %get-tuple-element.45), channel_id=1, source_target_pairs={{0,1},{1,0},{2,3},{3,2},{4,5},{5,4},{6,7},{7,6},{8,9},{9,8},{10,11... | collective-permute-start | bytes 1572872 | tf_op jit(solution)/shard_map/ppermute | solution.py:541
  7.6 12.0 %collective-permute-start = (f32[8,128]{1,0:T(8,128)S(1)}, f32[8,128]{1,0:T(8,128)S(1)}, u32[]{:S(2)}, u32[]{:S(2)}) collective-permute-start(f32[8,128]{1,0:T(8,128)S(1)} %get-tuple-element.27), channel_id=1, source_target_pairs={{0,1},{1,0},{2,3},{3,2},{4,5},{5,4},{6,7},{7,6},{8,9},{9,8},{10,11... | collective-permute-start | bytes 12296 | tf_op jit(solution)/shard_map/ppermute | solution.py:540
  7.6 12.8 %collective-permute-start.1 = (f32[8,128]{1,0:T(8,128)S(1)}, f32[8,128]{1,0:T(8,128)S(1)}, u32[]{:S(2)}, u32[]{:S(2)}) collective-permute-start(f32[8,128]{1,0:T(8,128)S(1)} %get-tuple-element.28), channel_id=1, source_target_pairs={{1,2},{3,4},{5,6},{7,0},{2,1},{4,3},{6,5},{0,7},{9,10},{11,12},{13... | collective-permute-start | bytes 12296 | tf_op jit(solution)/shard_map/ppermute | solution.py:542
  20.5 3.9 %collective-permute-start.2 = (f32[8,1664]{1,0:T(8,128)S(1)}, f32[8,1664]{1,0:T(8,128)S(1)}, u32[]{:S(2)}, u32[]{:S(2)}) collective-permute-start(f32[8,1664]{1,0:T(8,128)S(1)} %get-tuple-element.29), channel_id=1, source_target_pairs={{0,8},{16,24},{8,0},{24,16},{1,9},{17,25},{9,1},{25,17},{2,10},{18... | collective-permute-start | bytes 159752 | tf_op jit(solution)/shard_map/ppermute | solution.py:599
  22.1 5.2 %collective-permute-start.3 = (f32[8,1664]{1,0:T(8,128)S(1)}, f32[8,1664]{1,0:T(8,128)S(1)}, u32[]{:S(2)}, u32[]{:S(2)}) collective-permute-start(f32[8,1664]{1,0:T(8,128)S(1)} %get-tuple-element.30), channel_id=1, source_target_pairs={{8,16},{24,0},{16,8},{0,24},{9,17},{25,1},{17,9},{1,25},{10,18},{2... | collective-permute-start | bytes 159752 | tf_op jit(solution)/shard_map/ppermute | solution.py:599
  30.5 2.5 %copy-start = (f32[8,18,80,128]{3,2,1,0:T(8,128)}, f32[8,18,80,128]{3,2,1,0:T(8,128)S(1)}, u32[]{:S(2)}) copy-start(f32[8,18,80,128]{3,2,1,0:T(8,128)S(1)} %get-tuple-element.33.old_volume) | copy-start | bytes 17694724
  33.1 31.7 %collective-permute-start.10 = (f32[64,1024]{1,0:T(8,128)}, f32[64,1024]{1,0:T(8,128)S(1)}, u32[]{:S(2)}, u32[]{:S(2)}) collective-permute-start(f32[64,1024]{1,0:T(8,128)} %get-tuple-element.24), channel_id=1, source_target_pairs={{0,1},{1,0},{2,3},{3,2},{4,5},{5,4},{6,7},{7,6},{8,9},{9,8},{10,11... | collective-permute-start | bytes 786440 | tf_op jit(solution)/shard_map/ppermute | solution.py:629
  33.1 36.3 %collective-permute-start.11 = (f32[64,1024]{1,0:T(8,128)}, f32[64,1024]{1,0:T(8,128)S(1)}, u32[]{:S(2)}, u32[]{:S(2)}) collective-permute-start(f32[64,1024]{1,0:T(8,128)} %get-tuple-element.25), channel_id=1, source_target_pairs={{0,1},{1,0},{2,3},{3,2},{4,5},{5,4},{6,7},{7,6},{8,9},{9,8},{10,11... | collective-permute-start | bytes 786440 | tf_op jit(solution)/shard_map/ppermute | solution.py:630
  34.5 1.0 %copy-start.9 = (f32[8,8,2048]{2,1,0:T(8,128)S(1)}, f32[8,8,2048]{2,1,0:T(8,128)}, u32[]{:S(2)}) copy-start(f32[8,8,2048]{2,1,0:T(8,128)} %copy-done.8) | copy-start | bytes 1572868
  35.6 1.0 %copy-start.11 = (f32[8,8,2048]{2,1,0:T(8,128)S(1)}, f32[8,8,2048]{2,1,0:T(8,128)}, u32[]{:S(2)}) copy-start(f32[8,8,2048]{2,1,0:T(8,128)} %copy-done.10) | copy-start | bytes 1572868
  36.6 0.9 %copy-start.13 = (f32[8,64,128]{2,1,0:T(8,128)S(1)}, f32[8,64,128]{2,1,0:T(8,128)}, u32[]{:S(2)}) copy-start(f32[8,64,128]{2,1,0:T(8,128)} %copy-done.12) | copy-start | bytes 786436
  38.8 3.2 %collective-permute-start.6 = (f32[8,128]{1,0:T(8,128)S(1)}, f32[8,128]{1,0:T(8,128)S(1)}, u32[]{:S(2)}, u32[]{:S(2)}) collective-permute-start(f32[8,128]{1,0:T(8,128)S(1)} %get-tuple-element.41), channel_id=1, source_target_pairs={{0,2},{4,6},{2,0},{6,4},{1,3},{5,7},{3,1},{7,5},{8,10},{12,14},{10... | collective-permute-start | bytes 12296 | tf_op jit(solution)/shard_map/ppermute | solution.py:599
  40.8 3.3 %collective-permute-start.7 = (f32[8,128]{1,0:T(8,128)S(1)}, f32[8,128]{1,0:T(8,128)S(1)}, u32[]{:S(2)}, u32[]{:S(2)}) collective-permute-start(f32[8,128]{1,0:T(8,128)S(1)} %get-tuple-element.42), channel_id=1, source_target_pairs={{2,4},{6,0},{4,2},{0,6},{3,5},{7,1},{5,3},{1,7},{10,12},{14,8},{12... | collective-permute-start | bytes 12296 | tf_op jit(solution)/shard_map/ppermute | solution.py:599
  42.0 4.3 %collective-permute-start.4 = (f32[8,2304]{1,0:T(8,128)S(1)}, f32[8,2304]{1,0:T(8,128)S(1)}, u32[]{:S(2)}, u32[]{:S(2)}) collective-permute-start(f32[8,2304]{1,0:T(8,128)S(1)} %get-tuple-element.39), channel_id=1, source_target_pairs={{0,8},{16,24},{8,0},{24,16},{1,9},{17,25},{9,1},{25,17},{2,10},{18... | collective-permute-start | bytes 221192 | tf_op jit(solution)/shard_map/ppermute | solution.py:599
  44.1 5.8 %collective-permute-start.5 = (f32[8,2304]{1,0:T(8,128)S(1)}, f32[8,2304]{1,0:T(8,128)S(1)}, u32[]{:S(2)}, u32[]{:S(2)}) collective-permute-start(f32[8,2304]{1,0:T(8,128)S(1)} %get-tuple-element.40), channel_id=1, source_target_pairs={{8,16},{24,0},{16,8},{0,24},{9,17},{25,1},{17,9},{1,25},{10,18},{2... | collective-permute-start | bytes 221192 | tf_op jit(solution)/shard_map/ppermute | solution.py:599
  50.2 7.2 %collective-permute-start.9 = (f32[8,1152]{1,0:T(8,128)S(1)}, f32[8,1152]{1,0:T(8,128)S(1)}, u32[]{:S(2)}, u32[]{:S(2)}) collective-permute-start(f32[8,1152]{1,0:T(8,128)S(1)} %rim_pack.1), channel_id=1, source_target_pairs={{0,1},{1,0},{2,3},{3,2},{4,5},{5,4},{6,7},{7,6},{8,9},{9,8},{10,11... | collective-permute-start | bytes 110600 | tf_op jit(solution)/shard_map/ppermute | solution.py:628
  51.4 2.7 %copy-start.1 = (f32[8,18,80,128]{3,2,1,0:T(8,128)S(1)}, f32[8,18,80,128]{3,2,1,0:T(8,128)}, u32[]{:S(2)}) copy-start(f32[8,18,80,128]{3,2,1,0:T(8,128)} %copy-done) | copy-start | bytes 17694724
  54.8 2.5 %copy-start.2 = (f32[8,18,80,128]{3,2,1,0:T(8,128)}, f32[8,18,80,128]{3,2,1,0:T(8,128)S(1)}, u32[]{:S(2)}) copy-start(f32[8,18,80,128]{3,2,1,0:T(8,128)S(1)} %get-tuple-element.43.volume) | copy-start | bytes 17694724
  57.3 2.7 %copy-start.3 = (f32[8,18,80,128]{3,2,1,0:T(8,128)S(1)}, f32[8,18,80,128]{3,2,1,0:T(8,128)}, u32[]{:S(2)}) copy-start(f32[8,18,80,128]{3,2,1,0:T(8,128)} %copy-done.2) | copy-start | bytes 17694724
  60.0 4.7 %copy-start.4 = (f32[8,18,80,128]{3,2,1,0:T(8,128)S(1)}, f32[8,18,80,128]{3,2,1,0:T(8,128)}, u32[]{:S(2)}) copy-start(f32[8,18,80,128]{3,2,1,0:T(8,128)} %copy-done.2) | copy-start | bytes 17694724
  (4 other events, 3.3 us)

commit v8 on v7

--- a/solution.py
+++ b/solution.py
@@ -25,7 +25,7 @@
     return jnp.concatenate([rest, tile] if at_end else [tile, rest], 0)
 
 
-def first_pack(group, e, p, v, seam, outer, layer, v_top, v_bottom, v_left, v_right, edges, sems):
+def first_pack(group, e, p, v, seam, outer, layer, edges, sems):
     rows, width = e.shape
     low = group[0] == 0
     source = jnp.where(low, v.shape[0] - 1, 0)
@@ -34,23 +34,9 @@
     for index, (field, start) in enumerate(((e, 0), (p, 0), (e, width - LANES), (p, width - LANES))):
         into = edges.at[index // 2, (index % 2) * rows : (index % 2 + 1) * rows, :]
         copies.append(pltpu.make_async_copy(field.at[:, start : start + LANES], into, sems.at[index]))
-    tile = v.shape[2]
-    ends = [
-        pltpu.make_async_copy(source, into, sems.at[5 + index])
-        for index, (source, into) in enumerate(
-            (
-                (v.at[:, :SUBS, :], v_top),
-                (v.at[:, rows - SUBS :, :], v_bottom),
-                (v.at[:, :, :LANES], v_left),
-                (v.at[:, :, tile - LANES :], v_right),
-            )
-        )
-    ]
     for copy in copies:
         copy.start()
     whole.start()
-    for copy in ends:
-        copy.start()
     for copy in copies:
         copy.wait()
     left = edges[0].T[:SUBS]
@@ -58,8 +44,6 @@
     seam[...] = jnp.where(low, right, left)
     outer[...] = jnp.where(low, left, right)
     whole.wait()
-    for copy in ends:
-        copy.wait()
 
 
 def by_parity(odd, fill, first, second):
@@ -520,14 +504,12 @@
     params = pltpu.CompilerParams(vmem_limit_bytes=24 * 1024 * 1024)
     vmem = pl.BlockSpec(memory_space=pltpu.VMEM)
     hbm = pl.BlockSpec(memory_space=pltpu.HBM)
-    seam, outer, layer, *ends = pl.pallas_call(
+    seam, outer, layer = pl.pallas_call(
         first_pack,
-        out_shape=(shape(SUBS, LANES), shape(SUBS, LANES), shape(rows, tile))
-        + (shape(layers, SUBS, tile),) * 2
-        + (shape(layers, rows, LANES),) * 2,
+        out_shape=(shape(SUBS, LANES), shape(SUBS, LANES), shape(rows, tile)),
         in_specs=[scalar, hbm, hbm, hbm],
-        out_specs=[vmem] * 7,
-        scratch_shapes=[pltpu.VMEM((2, LANES, LANES), f32), pltpu.SemaphoreType.DMA((9,))],
+        out_specs=[vmem] * 3,
+        scratch_shapes=[pltpu.VMEM((2, LANES, LANES), f32), pltpu.SemaphoreType.DMA((5,))],
         compiler_params=params,
         name="first_pack",
     )(group, *(pltpu.with_memory_space_constraint(x, pltpu.HBM) for x in (elevation, surface_potential, interior_potential)))
@@ -560,7 +542,10 @@
         in_specs=[
             scalar,
             scalar,
-            *[vmem] * 4,
+            block((layers, SUBS, tile), 0, 0, 0),
+            block((layers, SUBS, tile), 0, last_row, 0),
+            block((layers, rows, LANES), 0, 0, 0),
+            block((layers, rows, LANES), 0, 0, last_tile),
             block((SUBS, tile), 0, 0),
             block((SUBS, tile), last_row, 0),
             block((rows, LANES), 0, 0),
@@ -569,7 +554,7 @@
         out_specs=[whole(SUBS, tile + tile // SUBS)] * 2 + [whole(SUBS, LANES)] * 2,
         compiler_params=params,
         name="lazy_pack",
-    )(odd_x, odd_y, *ends, *(seabed,) * 4)
+    )(odd_x, odd_y, *(pltpu.with_memory_space_constraint(interior_potential, pltpu.HBM),) * 4, *(seabed,) * 4)
 
     wide = width + 2 * LANES
     packed = wide + pl.cdiv((2 * REACH - SUBS) * (wide // LANES), SUBS) * LANES

time: 71.7 us -> 60.1 us (0.84)
  the two profiles are of different devices: /device:TPU:1 before, /device:TPU:0 now
where the time goes in v8:
time: 60.1 us; the launch traced here: 59.9 us
  waiting for transfers between devices  21.3 us (35%)
  Pallas kernels  18.4 us (31%)
  starting transfers between devices  17 us (28%)
  local copies, waits for them, and re-layouts  2.55 us (4%)
  between operations  0.75 us (1%)
    ppermute x1, waiting for transfers between devices, shards(): seam = lax.ppermute(seam, flat, partner)  10.4 us
    ppermute x6, waiting for transfers between devices, shards(): sides[name] = lax.ppermute(value, axis, couples(axis, shifted))  9.1 us
    ppermute x6, starting transfers between devices, shards(): sides[name] = lax.ppermute(value, axis, couples(axis, shifted))  8.46 us
    pallas_call x1, Pallas kernels, shards(): pl.pallas_call(functools.partial(other_half, total_layers), out_shape=(sh...  4.69 us
    pallas_call x1, Pallas kernels, shards(): pl.pallas_call(functools.partial(own_half, total_layers), out_shape=shape...  4.69 us
    pallas_call x1, Pallas kernels, shards(): pl.pallas_call(surface, out_shape=(shape(rows, width),) * 2 + (shape(*pad...  3.15 us
    ppermute x1, starting transfers between devices, shards(): far_layer = lax.ppermute(layer, flat, partner)  3.06 us
    unnamed x12, local copies, waits for them, and re-layouts  2.55 us
  transfers between devices with their start and end apart: 12, of which 6 were waited for; matrix products, arithmetic and copies ran while one was open for 0% of the time, Pallas kernels for 26%

profile of v8, /device:TPU:0, one launch (start us, length us, event | category | flops | bytes accessed | tf_op | source)
XLA Modules:
  0.0 59.9 jit_solution(10748995717564401108)
XLA Ops:
  0.7 2.0 %first_pack.1 = (f32[8,128]{1,0:T(8,128)S(1)}, f32[8,128]{1,0:T(8,128)S(1)}, f32[64,2048]{1,0:T(8,128)}) custom-call(s32[1]{0:T(128)} %bitcast.1.group.group_ref, f32[64,1024]{1,0:T(8,128)} %e.3, f32[64,1024]{1,0:T(8,128)} %p.3, f32[8,64,2048]{2,1,0:T(8,128)} %v_right.1), custom_call_target="tpu_custom_call" | custom-call | tf_op jit(solution)/shard_map/first_pack/pallas_call | solution.py:507
  2.7 3.1 %collective-permute-start.8 = (f32[64,2048]{1,0:T(8,128)}, f32[64,2048]{1,0:T(8,128)S(1)}, u32[]{:S(2)}, u32[]{:S(2)}) collective-permute-start(f32[64,2048]{1,0:T(8,128)} %get-tuple-element.37), channel_id=1, source_target_pairs={{0,1},{1,0},{2,3},{3,2},{4,5},{5,4},{6,7},{7,6},{8,9},{9,8},{10,11... | collective-permute-start | bytes 1572872 | tf_op jit(solution)/shard_map/ppermute | solution.py:523
  5.9 1.8 %collective-permute-start.1 = (f32[8,128]{1,0:T(8,128)S(1)}, f32[8,128]{1,0:T(8,128)S(1)}, u32[]{:S(2)}, u32[]{:S(2)}) collective-permute-start(f32[8,128]{1,0:T(8,128)S(1)} %get-tuple-element.24), channel_id=1, source_target_pairs={{1,2},{3,4},{5,6},{7,0},{2,1},{4,3},{6,5},{0,7},{9,10},{11,12},{13... | collective-permute-start | bytes 12296 | tf_op jit(solution)/shard_map/ppermute | solution.py:524
  7.6 10.4 %collective-permute-done.seam = f32[8,128]{1,0:T(8,128)S(1)} collective-permute-done((f32[8,128]{1,0:T(8,128)S(1)}, f32[8,128]{1,0:T(8,128)S(1)}, u32[]{:S(2)}, u32[]{:S(2)}) %collective-permute-start) | collective-permute-done | bytes 4128 | tf_op jit(solution)/shard_map/ppermute | solution.py:522
  18.2 1.9 %collective-permute-start.2 = (f32[8,1664]{1,0:T(8,128)S(1)}, f32[8,1664]{1,0:T(8,128)S(1)}, u32[]{:S(2)}, u32[]{:S(2)}) collective-permute-start(f32[8,1664]{1,0:T(8,128)S(1)} %get-tuple-element.25), channel_id=1, source_target_pairs={{0,8},{16,24},{8,0},{24,16},{1,9},{17,25},{9,1},{25,17},{2,10},{18... | collective-permute-start | bytes 159752 | tf_op jit(solution)/shard_map/ppermute | solution.py:584
  20.1 2.5 %collective-permute-start.3 = (f32[8,1664]{1,0:T(8,128)S(1)}, f32[8,1664]{1,0:T(8,128)S(1)}, u32[]{:S(2)}, u32[]{:S(2)}) collective-permute-start(f32[8,1664]{1,0:T(8,128)S(1)} %get-tuple-element.26), channel_id=1, source_target_pairs={{8,16},{24,0},{16,8},{0,24},{9,17},{25,1},{17,9},{1,25},{10,18},{2... | collective-permute-start | bytes 159752 | tf_op jit(solution)/shard_map/ppermute | solution.py:584
  22.6 3.4 %collective-permute-done.3.row_b = f32[8,1664]{1,0:T(8,128)S(1)} collective-permute-done((f32[8,1664]{1,0:T(8,128)S(1)}, f32[8,1664]{1,0:T(8,128)S(1)}, u32[]{:S(2)}, u32[]{:S(2)}) %collective-permute-start.3) | collective-permute-done | bytes 53280 | tf_op jit(solution)/shard_map/ppermute | solution.py:584
  26.0 3.1 %surface.1 = (f32[64,1024]{1,0:T(8,128)}, f32[64,1024]{1,0:T(8,128)}, f32[10,88,128]{2,1,0:T(8,128)S(1)}, f32[10,88,128]{2,1,0:T(8,128)S(1)}, f32[8,18,80,128]{3...) custom-call(s32[1]{0:T(128)} %bitcast.odd_x, f32[64,1024]{1,0:T(8,128)S(1)} %copy-done.2, f32[64,1024]{1,0:T(8,128)S(1)} %copy-done.3, ...), custom_call_target="tpu_custom_call" | custom-call | tf_op jit(solution)/shard_map/surface/pallas_call | solution.py:592
  29.2 2.5 %copy-done = f32[8,18,80,128]{3,2,1,0:T(8,128)} copy-done((f32[8,18,80,128]{3,2,1,0:T(8,128)}, f32[8,18,80,128]{3,2,1,0:T(8,128)S(1)}, u32[]{:S(2)}) %copy-start) | copy-done | bytes 5898264
  31.7 1.6 %collective-permute-start.10 = (f32[64,1024]{1,0:T(8,128)}, f32[64,1024]{1,0:T(8,128)S(1)}, u32[]{:S(2)}, u32[]{:S(2)}) collective-permute-start(f32[64,1024]{1,0:T(8,128)} %get-tuple-element.20), channel_id=1, source_target_pairs={{0,1},{1,0},{2,3},{3,2},{4,5},{5,4},{6,7},{7,6},{8,9},{9,8},{10,11... | collective-permute-start | bytes 786440 | tf_op jit(solution)/shard_map/ppermute | solution.py:614
  33.2 0.5 collective-permute-start.11
  33.7 1.8 %lazy_pack.1 = (f32[8,2304]{1,0:T(8,128)S(1)}, f32[8,2304]{1,0:T(8,128)S(1)}, f32[8,128]{1,0:T(8,128)S(1)}, f32[8,128]{1,0:T(8,128)S(1)}) custom-call(s32[1]{0:T(128)} %bitcast.odd_x, s32[1]{0:T(128)} %bitcast.2.odd_y, f32[8,64,2048]{2,1,0:T(8,128)} %v_right.1, f32[8,64,2048]{2,1,0:T(8,128)} %v_right.1, f32[8,64,2048]{2,1,0:T(8,128)} %v_right.1, ...), custom_call_target="tpu_custom_call" | custom-call | tf_op jit(solution)/shard_map/lazy_pack/pallas_call | solution.py:538
  35.6 1.6 %collective-permute-start.7 = (f32[8,128]{1,0:T(8,128)S(1)}, f32[8,128]{1,0:T(8,128)S(1)}, u32[]{:S(2)}, u32[]{:S(2)}) collective-permute-start(f32[8,128]{1,0:T(8,128)S(1)} %get-tuple-element.34), channel_id=1, source_target_pairs={{2,4},{6,0},{4,2},{0,6},{3,5},{7,1},{5,3},{1,7},{10,12},{14,8},{12... | collective-permute-start | bytes 12296 | tf_op jit(solution)/shard_map/ppermute | solution.py:584
  37.2 1.5 %collective-permute-done.7.x_b = f32[8,128]{1,0:T(8,128)S(1)} collective-permute-done((f32[8,128]{1,0:T(8,128)S(1)}, f32[8,128]{1,0:T(8,128)S(1)}, u32[]{:S(2)}, u32[]{:S(2)}) %collective-permute-start.7) | collective-permute-done | bytes 4128 | tf_op jit(solution)/shard_map/ppermute | solution.py:584
  38.7 2.5 %collective-permute-start.5 = (f32[8,2304]{1,0:T(8,128)S(1)}, f32[8,2304]{1,0:T(8,128)S(1)}, u32[]{:S(2)}, u32[]{:S(2)}) collective-permute-start(f32[8,2304]{1,0:T(8,128)S(1)} %get-tuple-element.32), channel_id=1, source_target_pairs={{8,16},{24,0},{16,8},{0,24},{9,17},{25,1},{17,9},{1,25},{10,18},{2... | collective-permute-start | bytes 221192 | tf_op jit(solution)/shard_map/ppermute | solution.py:584
  41.1 0.4 collective-permute-done.4.far_a
  41.5 3.8 %collective-permute-done.5.far_b = f32[8,2304]{1,0:T(8,128)S(1)} collective-permute-done((f32[8,2304]{1,0:T(8,128)S(1)}, f32[8,2304]{1,0:T(8,128)S(1)}, u32[]{:S(2)}, u32[]{:S(2)}) %collective-permute-start.5) | collective-permute-done | bytes 73760 | tf_op jit(solution)/shard_map/ppermute | solution.py:584
  45.4 0.2 rim_pack.1
  45.5 1.6 %collective-permute-start.9 = (f32[8,1152]{1,0:T(8,128)S(1)}, f32[8,1152]{1,0:T(8,128)S(1)}, u32[]{:S(2)}, u32[]{:S(2)}) collective-permute-start(f32[8,1152]{1,0:T(8,128)S(1)} %rim_pack.1), channel_id=1, source_target_pairs={{0,1},{1,0},{2,3},{3,2},{4,5},{5,4},{6,7},{7,6},{8,9},{9,8},{10,11... | collective-permute-start | bytes 110600 | tf_op jit(solution)/shard_map/ppermute | solution.py:613
  47.1 0.7 %fill.1 = (f32[8,18,80,128]{3,2,1,0:T(8,128)S(1)}, f32[18,80,128]{2,1,0:T(8,128)S(1)}) custom-call(s32[1]{0:T(128)} %bitcast.odd_x, s32[1]{0:T(128)} %bitcast.2.odd_y, f32[8,18,80,128]{3,2,1,0:T(8,128)S(1)} %bitcast.4, f32[18,80,128]{2,1,0:T(8,128)S(1)} %get-tuple-element.30.old_depth, ...), custom_call_target="tpu_custom_call", output_to_operand_aliasing={{0}: (2, {}), {1}: (3, {})} | custom-call | tf_op jit(solution)/shard_map/fill/pallas_call | solution.py:616
  47.8 1.7 %collective-permute-done.9.rims = f32[8,1152]{1,0:T(8,128)S(1)} collective-permute-done((f32[8,1152]{1,0:T(8,128)S(1)}, f32[8,1152]{1,0:T(8,128)S(1)}, u32[]{:S(2)}, u32[]{:S(2)}) %collective-permute-start.9) | collective-permute-done | bytes 36896 | tf_op jit(solution)/shard_map/ppermute | solution.py:613
  49.5 4.7 %own_half.1.before = f32[8,64,2048]{2,1,0:T(8,128)} custom-call(s32[1]{0:T(128)} %bitcast.1.group.group_ref, f32[8,18,80,128]{3,2,1,0:T(8,128)S(1)} %get-tuple-element.35.volume, f32[18,80,128]{2,1,0:T(8,128)S(1)} %get-tuple-element.36.depth, f32[64,2048]{1,0:T(8,128)S(1)} %collective-permute-done.8.far_layer, f32[8,1152]{1,0:T(8,128)S(1)} %collective-permute-done.9.rims, ...), custom_call_target="tpu_custom_call" | custom-call | tf_op jit(solution)/shard_map/own_half/pallas_call | solution.py:635
  54.2 4.7 %other_half.1 = (f32[8,64,2048]{2,1,0:T(8,128)}, f32[64,1024]{1,0:T(8,128)S(1)}, f32[3,64,1024]{2,1,0:T(8,128)S(1)}) custom-call(s32[1]{0:T(128)} %bitcast.1.group.group_ref, f32[8,64,2048]{2,1,0:T(8,128)} %own_half.1.before, f32[8,18,80,128]{3,2,1,0:T(8,128)S(1)} %get-tuple-element.35.volume, ...), custom_call_target="tpu_custom_call", output_to_operand_aliasing={{0}: (1, {})} | custom-call | tf_op jit(solution)/shard_map/other_half/pallas_call | solution.py:648
  58.9 1.0 %top.1 = f32[8,64,2048]{2,1,0:T(8,128)} custom-call(s32[1]{0:T(128)} %bitcast.1.group.group_ref, f32[8,64,2048]{2,1,0:T(8,128)} %get-tuple-element.40.before, f32[64,1024]{1,0:T(8,128)S(1)} %get-tuple-element.41.part, f32[3,64,1024]{2,1,0:T(8,128)S(1)} %get-tuple-element.42.coefficients, ...), custom_call_target="tpu_custom_call", output_to_operand_aliasing={{}: (1, {})} | custom-call | tf_op jit(solution)/shard_map/top/pallas_call | solution.py:666
  (23 shorter events, 0.4 us)
Async XLA Ops:
  0.6 17.4 %copy-start.2 = (f32[64,1024]{1,0:T(8,128)S(1)}, f32[64,1024]{1,0:T(8,128)}, u32[]{:S(2)}) copy-start(f32[64,1024]{1,0:T(8,128)} %e.3) | copy-start | bytes 786436
  0.6 17.4 %copy-start.3 = (f32[64,1024]{1,0:T(8,128)S(1)}, f32[64,1024]{1,0:T(8,128)}, u32[]{:S(2)}) copy-start(f32[64,1024]{1,0:T(8,128)} %p.3) | copy-start | bytes 786436
  0.7 25.3 %copy-start.1 = (s32[64,2048]{1,0:T(8,128)S(1)}, s32[64,2048]{1,0:T(8,128)}, u32[]{:S(2)}) copy-start(s32[64,2048]{1,0:T(8,128)} %s_right.1) | copy-start | bytes 1572868
  2.7 46.8 %collective-permute-start.8 = (f32[64,2048]{1,0:T(8,128)}, f32[64,2048]{1,0:T(8,128)S(1)}, u32[]{:S(2)}, u32[]{:S(2)}) collective-permute-start(f32[64,2048]{1,0:T(8,128)} %get-tuple-element.37), channel_id=1, source_target_pairs={{0,1},{1,0},{2,3},{3,2},{4,5},{5,4},{6,7},{7,6},{8,9},{9,8},{10,11... | collective-permute-start | bytes 1572872 | tf_op jit(solution)/shard_map/ppermute | solution.py:523
  5.8 12.3 %collective-permute-start = (f32[8,128]{1,0:T(8,128)S(1)}, f32[8,128]{1,0:T(8,128)S(1)}, u32[]{:S(2)}, u32[]{:S(2)}) collective-permute-start(f32[8,128]{1,0:T(8,128)S(1)} %get-tuple-element.23), channel_id=1, source_target_pairs={{0,1},{1,0},{2,3},{3,2},{4,5},{5,4},{6,7},{7,6},{8,9},{9,8},{10,11... | collective-permute-start | bytes 12296 | tf_op jit(solution)/shard_map/ppermute | solution.py:522
  5.9 12.2 %collective-permute-start.1 = (f32[8,128]{1,0:T(8,128)S(1)}, f32[8,128]{1,0:T(8,128)S(1)}, u32[]{:S(2)}, u32[]{:S(2)}) collective-permute-start(f32[8,128]{1,0:T(8,128)S(1)} %get-tuple-element.24), channel_id=1, source_target_pairs={{1,2},{3,4},{5,6},{7,0},{2,1},{4,3},{6,5},{0,7},{9,10},{11,12},{13... | collective-permute-start | bytes 12296 | tf_op jit(solution)/shard_map/ppermute | solution.py:524
  18.2 4.4 %collective-permute-start.2 = (f32[8,1664]{1,0:T(8,128)S(1)}, f32[8,1664]{1,0:T(8,128)S(1)}, u32[]{:S(2)}, u32[]{:S(2)}) collective-permute-start(f32[8,1664]{1,0:T(8,128)S(1)} %get-tuple-element.25), channel_id=1, source_target_pairs={{0,8},{16,24},{8,0},{24,16},{1,9},{17,25},{9,1},{25,17},{2,10},{18... | collective-permute-start | bytes 159752 | tf_op jit(solution)/shard_map/ppermute | solution.py:584
  20.1 5.9 %collective-permute-start.3 = (f32[8,1664]{1,0:T(8,128)S(1)}, f32[8,1664]{1,0:T(8,128)S(1)}, u32[]{:S(2)}, u32[]{:S(2)}) collective-permute-start(f32[8,1664]{1,0:T(8,128)S(1)} %get-tuple-element.26), channel_id=1, source_target_pairs={{8,16},{24,0},{16,8},{0,24},{9,17},{25,1},{17,9},{1,25},{10,18},{2... | collective-permute-start | bytes 159752 | tf_op jit(solution)/shard_map/ppermute | solution.py:584
  29.1 2.5 %copy-start = (f32[8,18,80,128]{3,2,1,0:T(8,128)}, f32[8,18,80,128]{3,2,1,0:T(8,128)S(1)}, u32[]{:S(2)}) copy-start(f32[8,18,80,128]{3,2,1,0:T(8,128)S(1)} %get-tuple-element.29.old_volume) | copy-start | bytes 17694724
  31.7 22.5 %collective-permute-start.10 = (f32[64,1024]{1,0:T(8,128)}, f32[64,1024]{1,0:T(8,128)S(1)}, u32[]{:S(2)}, u32[]{:S(2)}) collective-permute-start(f32[64,1024]{1,0:T(8,128)} %get-tuple-element.20), channel_id=1, source_target_pairs={{0,1},{1,0},{2,3},{3,2},{4,5},{5,4},{6,7},{7,6},{8,9},{9,8},{10,11... | collective-permute-start | bytes 786440 | tf_op jit(solution)/shard_map/ppermute | solution.py:614
  33.2 25.7 %collective-permute-start.11 = (f32[64,1024]{1,0:T(8,128)}, f32[64,1024]{1,0:T(8,128)S(1)}, u32[]{:S(2)}, u32[]{:S(2)}) collective-permute-start(f32[64,1024]{1,0:T(8,128)} %get-tuple-element.21), channel_id=1, source_target_pairs={{0,1},{1,0},{2,3},{3,2},{4,5},{5,4},{6,7},{7,6},{8,9},{9,8},{10,11... | collective-permute-start | bytes 786440 | tf_op jit(solution)/shard_map/ppermute | solution.py:615
  33.7 13.4 %slice-start = ((s8[5898240]{0:T(1024)(128)(4,1)}), s8[4194304]{0:T(1024)(128)(4,1)S(1)}, s32[]{:S(2)}) async-start(s8[5898240]{0:T(1024)(128)(4,1)} %bitcast.3), calls=%async_computation | async-start | bytes 8388608
  33.7 13.4 %slice-start.1 = ((s8[5898240]{0:T(1024)(128)(4,1)}), s8[1703936]{0:T(1024)(128)(4,1)S(1)}, s32[]{:S(2)}) async-start(s8[5898240]{0:T(1024)(128)(4,1)} %bitcast.3), calls=%async_computation.1 | async-start | bytes 3407872
  35.5 1.7 %collective-permute-start.6 = (f32[8,128]{1,0:T(8,128)S(1)}, f32[8,128]{1,0:T(8,128)S(1)}, u32[]{:S(2)}, u32[]{:S(2)}) collective-permute-start(f32[8,128]{1,0:T(8,128)S(1)} %get-tuple-element.33), channel_id=1, source_target_pairs={{0,2},{4,6},{2,0},{6,4},{1,3},{5,7},{3,1},{7,5},{8,10},{12,14},{10... | collective-permute-start | bytes 12296 | tf_op jit(solution)/shard_map/ppermute | solution.py:584
  35.6 3.1 %collective-permute-start.7 = (f32[8,128]{1,0:T(8,128)S(1)}, f32[8,128]{1,0:T(8,128)S(1)}, u32[]{:S(2)}, u32[]{:S(2)}) collective-permute-start(f32[8,128]{1,0:T(8,128)S(1)} %get-tuple-element.34), channel_id=1, source_target_pairs={{2,4},{6,0},{4,2},{0,6},{3,5},{7,1},{5,3},{1,7},{10,12},{14,8},{12... | collective-permute-start | bytes 12296 | tf_op jit(solution)/shard_map/ppermute | solution.py:584
  37.2 4.4 %collective-permute-start.4 = (f32[8,2304]{1,0:T(8,128)S(1)}, f32[8,2304]{1,0:T(8,128)S(1)}, u32[]{:S(2)}, u32[]{:S(2)}) collective-permute-start(f32[8,2304]{1,0:T(8,128)S(1)} %get-tuple-element.31), channel_id=1, source_target_pairs={{0,8},{16,24},{8,0},{24,16},{1,9},{17,25},{9,1},{25,17},{2,10},{18... | collective-permute-start | bytes 221192 | tf_op jit(solution)/shard_map/ppermute | solution.py:584
  38.7 6.7 %collective-permute-start.5 = (f32[8,2304]{1,0:T(8,128)S(1)}, f32[8,2304]{1,0:T(8,128)S(1)}, u32[]{:S(2)}, u32[]{:S(2)}) collective-permute-start(f32[8,2304]{1,0:T(8,128)S(1)} %get-tuple-element.32), channel_id=1, source_target_pairs={{8,16},{24,0},{16,8},{0,24},{9,17},{25,1},{17,9},{1,25},{10,18},{2... | collective-permute-start | bytes 221192 | tf_op jit(solution)/shard_map/ppermute | solution.py:584
  45.5 4.0 %collective-permute-start.9 = (f32[8,1152]{1,0:T(8,128)S(1)}, f32[8,1152]{1,0:T(8,128)S(1)}, u32[]{:S(2)}, u32[]{:S(2)}) collective-permute-start(f32[8,1152]{1,0:T(8,128)S(1)} %rim_pack.1), channel_id=1, source_target_pairs={{0,1},{1,0},{2,3},{3,2},{4,5},{5,4},{6,7},{7,6},{8,9},{9,8},{10,11... | collective-permute-start | bytes 110600 | tf_op jit(solution)/shard_map/ppermute | solution.py:613
